TPU v7x, 256 devices: a whole 4x4x8 slice. The times are simulated.
256 devices in a mesh: dp: 16 (over z_lo, x, core), section: 16 (over y, z_hi).
Axes of the slice: x: 4, y: 4, z: 8 (z_hi: 4, z_lo: 2; z = z_hi * 2 + z_lo), core: 2. Of those that a mesh axis runs over, the one named last changes fastest.
Arguments:
- frames: bfloat16 [16, 64, 40, 1024], P('section', 'dp'), may hold values from -240 to 240
- frame_lens: int32 [16, 16, 4], P('section', 'dp'), may hold values from 1 to 40, 128 in all within a row
- tgt_lens: int32 [16, 64], P(None, 'dp'), may hold values from 1 to 8
- enc_gain_in: float32 [1024], replicated, may hold values from 0.25 to 1.75
- w_in: bfloat16 [1024, 2048], P('dp'), may hold values from -0.1875 to 0.1875
- depthwise: bfloat16 [31, 1024], replicated, may hold values from -1 to 1
- enc_gain_mid: float32 [1024], replicated, may hold values from 0.25 to 1.75
- w_out: bfloat16 [1024, 1024], P('dp'), may hold values from -0.1875 to 0.1875
- dec_gain: float32 [16, 1024], P('section'), may hold values from 0.25 to 1.75
- w_query: bfloat16 [16, 1024, 1024], P('section'), may hold values from -1 to 1
- w_key: bfloat16 [16, 1024, 1024], P('section'), may hold values from -1 to 1
- w_value: bfloat16 [16, 1024, 1024], P('section'), may hold values from -0.1875 to 0.1875
- w_output: bfloat16 [16, 1024, 1024], P('section'), may hold values from -0.1875 to 0.1875
- hidden: bfloat16 [16, 16, 64, 8, 1024], P('section', None, 'dp'), may hold values from -6 to 6
Outputs:
- decoded: bfloat16 [16, 16, 64, 8, 1024], P('section', None, 'dp')
Inputs may be any that keep to these rules, and one draw needn't show every extreme that they name: `frame_lens`: the 4 utterances at [m, g] have 128 frames together, and the longest of them exactly 40.
All inputs are finite; a program needn't handle non-finite values.
Results may differ from a plain program's by a relative error of at most 0.019.
Values may be sent and summed in bfloat16 or wider, within the bound.
No kernel may reach another device: no remote copies, remote signals or barrier semaphores. Data moves between devices by JAX's collectives and lax.ppermute only.
A program may use at most 128 MiB of HBM per device.

v0:
```python
import functools

import jax
import jax.numpy as jnp
from jax import lax
from jax.experimental import pallas as pl
from jax.experimental.pallas import tpu as pltpu
from jax.sharding import PartitionSpec as P

HEADS = 16
D = 1024
HEAD = 64
FR = 40
TGT = 8
UTT = 4
TOT = 128
TAPS = 31
HALF = 15
GROUP = 4
EXTRA = 16
BF = jnp.bfloat16
F32 = jnp.float32
HBM = pl.BlockSpec(memory_space=pltpu.HBM)
VM = pl.BlockSpec(memory_space=pltpu.VMEM)
SM = pl.BlockSpec(memory_space=pltpu.SMEM)


def norm_rows(values, gain):
    average = jnp.mean(values, -1, keepdims=True)
    centered = values - average
    spread = jnp.mean(centered * centered, -1, keepdims=True)
    return centered * lax.rsqrt(spread + 1e-05) * gain


def params(limit):
    return pltpu.CompilerParams(vmem_limit_bytes=limit << 20)


def cost(flops, moved):
    return pl.CostEstimate(flops=flops, bytes_accessed=moved, transcendentals=0)


def one_hot(flags):
    return jnp.where(flags, 1.0, 0.0).astype(BF)


def slot_place(slot, lens_ref):
    utt = jnp.zeros_like(slot)
    start = jnp.zeros_like(slot)
    end = jnp.int32(0)
    for u in range(UTT - 1):
        end = end + lens_ref[u]
        later = slot >= end
        utt = jnp.where(later, u + 1, utt)
        start = jnp.where(later, end, start)
    return utt, slot - start


def prepare_kernel(lens_ref, frames_hbm, w_in_hbm, w_out_hbm, own_ref, out_ref, frames_ref, sems):
    loads = [
        pltpu.make_async_copy(w_in_hbm, own_ref.at[:, pl.ds(0, 2 * D)], sems.at[0]),
        pltpu.make_async_copy(w_out_hbm, own_ref.at[:, pl.ds(2 * D, D)], sems.at[1]),
        pltpu.make_async_copy(frames_hbm, frames_ref, sems.at[2]),
    ]
    for load in loads:
        load.start()
    slot = lax.broadcasted_iota(jnp.int32, (TOT, UTT * FR), 0)
    lane = lax.broadcasted_iota(jnp.int32, (TOT, UTT * FR), 1)
    utt, frame = slot_place(slot, lens_ref)
    pick = one_hot(utt * FR + frame == lane)
    utt, frame = slot_place(lax.broadcasted_iota(jnp.int32, (EXTRA, TOT), 1), lens_ref)
    kind = lax.broadcasted_iota(jnp.int32, (EXTRA, TOT), 0)
    out_ref[TOT:, :TOT] = jnp.where(kind == 0, frame, utt).astype(F32).astype(BF)
    out_ref[TOT:, TOT:] = jnp.zeros((EXTRA, D - TOT), BF)
    loads[2].wait()
    for j in range(D // 256):
        cols = slice(j * 256, (j + 1) * 256)
        out_ref[:TOT, cols] = jnp.dot(
            pick, frames_ref[:, cols], preferred_element_type=F32
        ).astype(BF)
    loads[0].wait()
    loads[1].wait()


def prepare(lens, frames, w_in, w_out):
    depth = w_in.shape[0]
    return pl.pallas_call(
        prepare_kernel,
        out_shape=(
            jax.ShapeDtypeStruct((depth, 3 * D), BF),
            jax.ShapeDtypeStruct((TOT + EXTRA, D), BF),
        ),
        in_specs=[SM, HBM, HBM, HBM],
        out_specs=(VM, VM),
        scratch_shapes=[pltpu.VMEM((UTT * FR, D), BF), pltpu.SemaphoreType.DMA((3,))],
        compiler_params=params(60),
        cost_estimate=cost(50_000_000, 1_400_000),
        name="prepare",
    )(lens, frames, w_in, w_out)


def query_kernel(hidden_ref, gain_ref, w_ref, out_ref, normed):
    @pl.loop(0, hidden_ref.shape[0] // 64)
    def _(i):
        for r in range(0, 64, 16):
            rows = pl.ds(pl.multiple_of(i * 64 + r, 16), 16)
            normed[rows, :] = norm_rows(hidden_ref[rows, :].astype(F32), gain_ref[...]).astype(BF)

    for j in range(D // 256):
        cols = slice(j * 256, (j + 1) * 256)
        q = jnp.dot(normed[...], w_ref[:, cols], preferred_element_type=F32)
        out_ref[:, cols] = (q * (HEAD**-0.5)).astype(BF)


def project_query(hidden, gain, w):
    rows = hidden.shape[0]
    return pl.pallas_call(
        query_kernel,
        out_shape=jax.ShapeDtypeStruct((rows, D), BF),
        in_specs=[VM, VM, VM],
        out_specs=VM,
        scratch_shapes=[pltpu.VMEM((rows, D), BF)],
        compiler_params=params(8),
        cost_estimate=cost(2 * rows * D * D, 4 << 20),
        name="project_query",
    )(hidden, gain, w)


def order_columns(dst, src, where_ref):
    odd = jnp.broadcast_to(where_ref[0] % 2 == 1, (src.shape[0], 128))
    for i in range(D // 128):
        at = pl.multiple_of(where_ref[i] // 2 * 128, 128)
        block = src[:, pl.ds(at, 128)].astype(F32)
        block = jnp.where(odd, pltpu.roll(block, HEAD, 1), block)
        dst[:, i * 128 : (i + 1) * 128] = block.astype(BF)


def shard_rows(w_refs, k, cols):
    own, other = w_refs
    picks = [own[2 * k], other[2 * k], own[2 * k + 1], other[2 * k + 1]]
    return jnp.concatenate([ref[row : row + 64, cols] for ref, row in picks], axis=0)


def dot_shards(lhs, w_refs, cols):
    total = None
    for k in range(D // 256):
        term = jnp.dot(
            lhs[:, k * 256 : (k + 1) * 256],
            shard_rows(w_refs, k, cols),
            preferred_element_type=F32,
        )
        total = term if total is None else total + term
    return total


def encode_kernel(n_w, where_ref, *refs):
    x_refs = refs[:2]
    gain_in_ref, dw_ref, gain_mid_ref = refs[2:5]
    blocks = []
    for ref in refs[5 : 5 + n_w]:
        blocks += [(ref, row) for row in range(0, ref.shape[0], 64)]
    w_refs = blocks[: len(blocks) // 2], blocks[len(blocks) // 2 :]
    out_ref, plain, normed, spread, conv, taps, act = refs[5 + n_w :]
    step = 16
    for i, x in enumerate(x_refs):
        for r in range(0, TOT, step):
            plain[i * TOT + r : i * TOT + r + step, :] = norm_rows(
                x[r : r + step, :].astype(F32), gain_in_ref[...]
            ).astype(BF)
    order_columns(normed, plain, where_ref)
    taps[...] = dw_ref[...].astype(F32)
    rows = normed.shape[0]
    frame_rows = conv.shape[0]
    lanes = 2 * UTT
    target = []
    for i, x in enumerate(x_refs):
        places = x[TOT : TOT + EXTRA, :TOT].astype(F32)
        target.append(places[0:1] * lanes + places[1:2] + i * UTT)
    target = jnp.concatenate(target, axis=1)
    spot = lax.broadcasted_iota(jnp.int32, (frame_rows, rows), 0)
    expand = one_hot(target.astype(jnp.int32) == spot)
    column = jnp.broadcast_to(target, (8, rows)).T[:, 0:1].astype(jnp.int32)
    shrink = one_hot(column == lax.broadcasted_iota(jnp.int32, (rows, frame_rows), 1))
    for j in range(D // 256):
        value = dot_shards(normed, w_refs, slice(j * 256, (j + 1) * 256))
        gate = dot_shards(normed, w_refs, slice(D + j * 256, D + (j + 1) * 256))
        gated = (value * jax.nn.sigmoid(gate)).astype(BF)
        spread[:, j * 256 : (j + 1) * 256] = jnp.dot(expand, gated, preferred_element_type=F32)
    block = 8

    @pl.loop(0, D // 128)
    def _(c):
        cols = pl.ds(pl.multiple_of(c * 128, 128), 128)
        weights = [jnp.broadcast_to(taps[k : k + 1, cols], (lanes, 128)) for k in range(TAPS)]
        for first in range(0, FR, block):
            sums = [None] * block
            for f in range(max(0, first - HALF), min(FR, first + block + HALF)):
                here = spread[f * lanes : (f + 1) * lanes, cols]
                for b in range(block):
                    k = f - (first + b) + HALF
                    if 0 <= k < TAPS:
                        term = here * weights[k]
                        sums[b] = term if sums[b] is None else sums[b] + term
            for b in range(block):
                at = (first + b) * lanes
                conv[at : at + lanes, cols] = sums[b]

    for r in range(0, frame_rows, step):
        v = norm_rows(conv[r : r + step, :], gain_mid_ref[...])
        act[r : r + step, :] = (v * jax.nn.sigmoid(v)).astype(BF)
    for j in range(D // 256):
        cols = slice(j * 256, (j + 1) * 256)
        plain[:, cols] = jnp.dot(shrink, act[:, cols], preferred_element_type=F32).astype(BF)
    order_columns(normed, plain, where_ref)
    for j in range(D // 256):
        cols = slice(j * 256, (j + 1) * 256)
        low = dot_shards(normed, w_refs, slice(2 * D + j * 256, 2 * D + (j + 1) * 256))
        for i, x in enumerate(x_refs):
            at = slice(i * TOT, (i + 1) * TOT)
            out_ref[at, cols] = (x[:TOT, cols].astype(F32) + low[at]).astype(BF)
    utts = [x[TOT : TOT + EXTRA, :TOT].astype(F32)[1:2] for x in x_refs]
    kind = lax.broadcasted_iota(jnp.int32, (EXTRA, TOT), 0)
    out_ref[rows:, :TOT] = jnp.where(kind == 0, utts[0], utts[1]).astype(BF)
    out_ref[rows:, TOT:] = jnp.zeros((EXTRA, D - TOT), BF)


def encode(where, xs, gain_in, dw, gain_mid, shards):
    rows = 2 * TOT
    frame_rows = 2 * UTT * FR
    return pl.pallas_call(
        functools.partial(encode_kernel, len(shards)),
        out_shape=jax.ShapeDtypeStruct((rows + EXTRA, D), BF),
        in_specs=[SM] + [VM] * (5 + len(shards)),
        out_specs=VM,
        scratch_shapes=[
            pltpu.VMEM((rows, D), BF),
            pltpu.VMEM((rows, D), BF),
            pltpu.VMEM((frame_rows, D), F32),
            pltpu.VMEM((frame_rows, D), F32),
            pltpu.VMEM((TAPS, D), F32),
            pltpu.VMEM((frame_rows, D), BF),
        ],
        compiler_params=params(9),
        cost_estimate=cost(8_000_000_000, 8 << 20),
        name="encode",
    )(where, *xs, gain_in, dw, gain_mid, *shards)


def decode_kernel(n_mem, aliased, micro_ref, tgt_ref, *refs):
    mem_refs = refs[:n_mem]
    q_ref, hidden_ref, wk, wv, wo = refs[n_mem : n_mem + 5]
    rest = refs[n_mem + 5 + (1 if aliased else 0) :]
    out_hbm, keys, values, ctx, res, seg, out_sems = rest
    slots = UTT * TGT
    micros = 2 * n_mem
    for w, out in ((wk, keys), (wv, values)):
        for p, mem in enumerate(mem_refs):
            for j in range(D // 256):
                cols = slice(j * 256, (j + 1) * 256)
                out[p * 2 * TOT : (p + 1) * 2 * TOT, cols] = jnp.dot(
                    mem[: 2 * TOT, :], w[:, cols], preferred_element_type=F32
                ).astype(BF)
    width = GROUP * HEAD
    tall = GROUP * slots
    row = lax.broadcasted_iota(jnp.int32, (tall, width), 0)
    lane = lax.broadcasted_iota(jnp.int32, (tall, width), 1)
    own = (row // slots) == (lane // HEAD)
    own_bf = one_hot(own)
    utt_of_row = (lax.broadcasted_iota(jnp.int32, (tall, TOT), 0) // TGT) % UTT
    groups = HEADS // GROUP
    for i in range(micros):
        utts = mem_refs[i // 2][2 * TOT : 2 * TOT + EXTRA, :TOT].astype(F32)
        seg[i * 8 : i * 8 + 8, :] = jnp.broadcast_to(utts[i % 2 : i % 2 + 1], (8, TOT))

    def attend(i):
        line = seg[pl.ds(pl.multiple_of(i * 8, 8), 8), :]
        allowed = utt_of_row == line[0:1].astype(jnp.int32)
        at = pl.ds(pl.multiple_of(i * TOT, TOT), TOT)
        mine = pl.ds(pl.multiple_of(i * slots, slots), slots)
        from_rows = pl.ds(pl.multiple_of(micro_ref[i] * slots, slots), slots)
        cuts = [slice(j * width, (j + 1) * width) for j in range(groups)]
        scores = []
        for cols in cuts:
            q = q_ref[from_rows, cols]
            q = jnp.concatenate([q] * GROUP, axis=0) * own_bf
            scores.append(
                lax.dot_general(
                    q, keys[at, cols], (((1,), (1,)), ((), ())), preferred_element_type=F32
                )
            )
        probs = []
        for s in scores:
            s = jnp.where(allowed, s, -1e30)
            expo = jnp.exp(s - jnp.max(s, -1, keepdims=True))
            probs.append((expo * (1.0 / jnp.sum(expo, -1, keepdims=True))).astype(BF))
        for prob, cols in zip(probs, cuts):
            mixed = jnp.dot(prob, values[at, cols], preferred_element_type=F32)
            mixed = jnp.where(own, mixed, 0.0)
            total = mixed[:slots]
            for g in range(1, GROUP):
                total = total + mixed[g * slots : (g + 1) * slots]
            ctx[mine, cols] = total.astype(BF)

    @pl.loop(0, micros // 2)
    def _(p):
        attend(2 * p)
        attend(2 * p + 1)

    pos = lax.broadcasted_iota(jnp.int32, (slots, 256), 0)

    @pl.loop(0, D // 512)
    def _(h):
      for half in range(2):
        cols = pl.ds(pl.multiple_of(h * 512 + half * 256, 256), 256)
        proj = jnp.dot(ctx[...], wo[:, cols], preferred_element_type=F32)
        for i in range(micros):
            mine = slice(i * slots, (i + 1) * slots)
            from_rows = pl.ds(pl.multiple_of(micro_ref[i] * slots, slots), slots)
            base = micro_ref[i] * UTT
            limit = jnp.full((slots, 256), tgt_ref[base], jnp.int32)
            for u in range(1, UTT):
                limit = jnp.where(pos // TGT == u, tgt_ref[base + u], limit)
            both = hidden_ref[from_rows, cols].astype(F32) + proj[mine]
            res[mine, cols] = jnp.where(pos % TGT < limit, both, 0.0).astype(BF)

    outs = []
    for i in range(micros):
        at = pl.ds(pl.multiple_of(micro_ref[i] * slots, slots), slots)
        here = pl.ds(i * slots, slots)
        copy = pltpu.make_async_copy(res.at[here, :], out_hbm.at[at, :], out_sems.at[i])
        copy.start()
        outs.append(copy)
    for copy in outs:
        copy.wait()


def decode(micro, tgt, mems, q, hidden, wk, wv, wo, prev):
    rows = hidden.shape[0]
    micros = 2 * len(mems)
    total = micros * TOT
    slots = UTT * TGT
    aliased = prev is not None
    args = [micro, tgt, *mems, q, hidden, wk, wv, wo] + ([prev] if aliased else [])
    return pl.pallas_call(
        functools.partial(decode_kernel, len(mems), aliased),
        out_shape=jax.ShapeDtypeStruct((rows, D), BF),
        in_specs=[SM, SM] + [VM] * (len(mems) + 5) + [HBM] * aliased,
        out_specs=HBM,
        scratch_shapes=[
            pltpu.VMEM((total, D), BF),
            pltpu.VMEM((total, D), BF),
            pltpu.VMEM((micros * slots, D), BF),
            pltpu.VMEM((micros * slots, D), BF),
            pltpu.VMEM((micros * 8, TOT), F32),
            pltpu.SemaphoreType.DMA((micros,)),
        ],
        input_output_aliases={len(args) - 1: 0} if aliased else {},
        compiler_params=params(7),
        cost_estimate=cost(16 * total * D * D, 8 << 20),
        name="decode",
    )(*args)


def dp_perm(move):
    pairs = []
    for z in range(2):
        for x in range(4):
            for c in range(2):
                nz, nx, nc = move(z, x, c)
                pairs.append(((z * 4 + x) * 2 + c, (nz * 4 + nx % 4) * 2 + nc))
    return pairs


def section_perm(dy, dz):
    return [(y * 4 + z, (y + dy) % 4 * 4 + (z + dz) % 4) for y in range(4) for z in range(4)]


TO_PAIR = dp_perm(lambda z, x, c: (1 - z, x, c))
TO_RIGHT = dp_perm(lambda z, x, c: (z, x + 1, c))
TO_LEFT = dp_perm(lambda z, x, c: (z, x + 3, c))
TO_CORE = dp_perm(lambda z, x, c: (z, x, 1 - c))


def pass_kernel(value_ref, *refs):
    refs[-1][...] = value_ref[...]


def pass_after(value, *others):
    return pl.pallas_call(
        pass_kernel,
        out_shape=jax.ShapeDtypeStruct(value.shape, value.dtype),
        in_specs=[VM] + [HBM] * len(others),
        out_specs=VM,
        compiler_params=params(2),
        cost_estimate=cost(0, 600_000),
        name="pass_after",
    )(value, *others)


def shard_table():
    places = [(0, 0), (1, 0), (0, 3), (0, 1), (1, 3), (1, 1), (0, 2), (1, 2)]
    table = []
    for index in range(16):
        z, x, c = index // 8, index // 2 % 4, index % 2
        table.append(
            [
                ((z + a) % 2 * 4 + (x + b) % 4) * 2 + (c + s) % 2
                for s in (0, 1)
                for a, b in places
            ]
        )
    return table


REL = (0, -1, 1, 2)


def micro_table():
    return [
        [(y + dy) % 4 * 4 + (z + dz) % 4 for dy in REL for dz in REL]
        for y in range(4)
        for z in range(4)
    ]


def body(
    frames,
    frame_lens,
    tgt_lens,
    enc_gain_in,
    w_in,
    depthwise,
    enc_gain_mid,
    w_out,
    dec_gain,
    w_query,
    w_key,
    w_value,
    w_output,
    hidden,
):
    across = lambda v, perm: lax.ppermute(v, "dp", perm)
    along = lambda v, dy, dz: lax.ppermute(v, "section", section_perm(dy, dz))
    where = jnp.array(shard_table(), jnp.int32)[lax.axis_index("dp")]
    micros = jnp.array(micro_table(), jnp.int32)[lax.axis_index("section")].reshape(4, 4)

    own, packed = prepare(
        frame_lens.reshape(UTT), frames.reshape(UTT * FR, D), w_in, w_out
    )
    pair = across(own, TO_PAIR)
    own_r, own_l = across(own, TO_LEFT), across(own, TO_RIGHT)
    source = hidden.reshape(-1, D)
    query = project_query(source, dec_gain, w_query[0])
    pair_l, pair_r = across(pair, TO_RIGHT), across(pair, TO_LEFT)
    own_2, pair_2 = across(own_l, TO_RIGHT), across(pair_r, TO_LEFT)
    ready = pass_after(packed, pair, query)
    from_b = along(ready, 0, 1)
    shards = [own, pair, own_l, own_r, pair_l, pair_r, own_2, pair_2]
    turn = [pass_after(own, pair, query, from_b)] + shards[1:]
    shards += [across(v, TO_CORE) for v in turn]

    from_a, from_2 = along(ready, 0, -1), along(ready, 0, 2)

    def encode_pair(first, second):
        return encode(
            where,
            [first, second],
            enc_gain_in.reshape(1, D),
            depthwise,
            enc_gain_mid.reshape(1, D),
            shards,
        )

    mem_a = encode_pair(packed, from_b)
    mem_b = encode_pair(from_a, from_2)

    a_from_l, a_from_r = along(mem_a, 1, 0), along(mem_a, -1, 0)
    b_from_l, b_from_r = along(mem_b, 1, 0), along(mem_b, -1, 0)

    tgt = tgt_lens.reshape(-1)

    def attend(parts, mems, prev):
        micro = jnp.concatenate([micros[y, z : z + 2] for y, z in parts])
        return decode(micro, tgt, mems, query, source, w_key[0], w_value[0], w_output[0], prev)

    a_far, b_far = along(a_from_l, 1, 0), along(b_from_r, -1, 0)
    out = attend([(0, 0), (0, 2)], [mem_a, mem_b], None)
    out = attend([(1, 0), (2, 0)], [a_from_l, a_from_r], out)
    out = attend([(1, 2), (2, 2)], [b_from_l, b_from_r], out)
    out = attend([(3, 0), (3, 2)], [a_far, b_far], out)
    return out.reshape(hidden.shape)


def solution(mesh):
    return jax.shard_map(
        body,
        mesh=mesh,
        in_specs=(
            P("section", "dp", None, None),
            P("section", "dp", None),
            P(None, "dp"),
            P(),
            P("dp", None),
            P(),
            P(),
            P("dp", None),
            P("section", None),
            P("section", None, None),
            P("section", None, None),
            P("section", None, None),
            P("section", None, None),
            P("section", None, "dp", None, None),
        ),
        out_specs=P("section", None, "dp", None, None),
        check_vma=False,
    )
```

profile of v0, /device:TPU:70, one launch (start us, length us, event | category | flops | bytes accessed | tf_op | source)
XLA Modules:
  0.0 133.2 jit_solution(8747192663157042963)
XLA Ops:
  0.0 2.9 %prepare.1 = (bf16[64,3072]{1,0:T(8,128)(2,1)}, bf16[144,1024]{1,0:T(8,128)(2,1)}) custom-call(s32[4]{0:T(128)} %bitcast.51, bf16[160,1024]{1,0:T(8,128)(2,1)} %bitcast.50, bf16[64,2048]{1,0:T(8,128)(2,1)} %w_in_hbm.1, bf16[64,1024]{1,0:T(8,128)(2,1)} %w_out_hbm.1), custom_call_target="tpu_custom_call" | custom-call | flops 50000000 | bytes 1400000 | tf_op jit(solution)/shard_map/prepare/pallas_call | solution.py:87
  2.9 2.0 %collective-permute-start = (bf16[64,3072]{1,0:T(8,128)(2,1)}, bf16[64,3072]{1,0:T(8,128)(2,1)S(1)}, u32[]{:S(2)}, u32[]{:S(2)}) collective-permute-start(bf16[64,3072]{1,0:T(8,128)(2,1)} %get-tuple-element.8.value_ref.refs_5_), channel_id=1, source_target_pairs={{0,128},{16,144},{32,160},{48,176},{64,192},{80,208},{96,224},{112... | collective-permute-start | bytes 1179656 | tf_op jit(solution)/shard_map/ppermute | solution.py:442
  4.9 0.5 collective-permute-start.2
  5.4 1.5 %collective-permute-start.3 = (bf16[64,3072]{1,0:T(8,128)(2,1)}, bf16[64,3072]{1,0:T(8,128)(2,1)S(1)}, u32[]{:S(2)}, u32[]{:S(2)}) collective-permute-start(bf16[64,3072]{1,0:T(8,128)(2,1)} %get-tuple-element.8.value_ref.refs_5_), channel_id=1, source_target_pairs={{0,96},{16,112},{32,0},{48,16},{64,32},{80,48},{96,64},{112,80},{1... | collective-permute-start | bytes 1179656 | tf_op jit(solution)/shard_map/ppermute | solution.py:442
  6.9 7.3 %collective-permute-done.refs_0_.refs_6_ = bf16[64,3072]{1,0:T(8,128)(2,1)S(1)} collective-permute-done((bf16[64,3072]{1,0:T(8,128)(2,1)}, bf16[64,3072]{1,0:T(8,128)(2,1)S(1)}, u32[]{:S(2)}, u32[]{:S(2)}) %collective-permute-start) | collective-permute-done | bytes 393248 | tf_op jit(solution)/shard_map/ppermute | solution.py:442
  14.2 0.8 collective-permute-start.5
  15.0 2.4 %collective-permute-start.4 = (bf16[64,3072]{1,0:T(8,128)(2,1)S(1)}, bf16[64,3072]{1,0:T(8,128)(2,1)S(1)}, u32[]{:S(2)}, u32[]{:S(2)}) collective-permute-start(bf16[64,3072]{1,0:T(8,128)(2,1)S(1)} %collective-permute-done.refs_0_.refs_6_), channel_id=1, source_target_pairs={{0,32},{16,48},{32,64},{48,80},{64,96},{80,112},{96,0},{112,16},{1... | collective-permute-start | bytes 1179656 | tf_op jit(solution)/shard_map/ppermute | solution.py:442
  17.5 1.6 %copy-done = bf16[1,1024,1024]{2,1,0:T(8,128)(2,1)S(1)} copy-done((bf16[1,1024,1024]{2,1,0:T(8,128)(2,1)S(1)}, bf16[1,1024,1024]{2,1,0:T(8,128)(2,1)}, u32[]{:S(2)}) %copy-start) | copy-done | bytes 2097176
  19.0 1.2 copy-done.1
  20.3 0.7 copy-done.5
  21.0 2.9 %project_query.1.refs_1_.refs_2_ = bf16[512,1024]{1,0:T(8,128)(2,1)S(1)} custom-call(bf16[512,1024]{1,0:T(8,128)(2,1)S(1)} %bitcast.29, f32[1,1024]{1,0:T(1,128)S(1)} %copy-done.5, bf16[1024,1024]{1,0:T(8,128)(2,1)S(1)} %bitcast.28), custom_call_target="tpu_custom_call" | custom-call | flops 1073741824 | bytes 4194304 | tf_op jit(solution)/shard_map/project_query/pallas_call | solution.py:117
  24.0 4.4 %collective-permute-start.1 = (bf16[144,1024]{1,0:T(8,128)(2,1)S(1)}, bf16[144,1024]{1,0:T(8,128)(2,1)S(1)}, u32[]{:S(2)}, u32[]{:S(2)}) collective-permute-start(bf16[144,1024]{1,0:T(8,128)(2,1)S(1)} %pass_after.2), channel_id=1, source_target_pairs={{0,1},{1,2},{2,3},{3,0},{4,5},{5,6},{6,7},{7,4},{8,9},{9,10},{10,1... | collective-permute-start | bytes 884744 | tf_op jit(solution)/shard_map/ppermute | solution.py:443
  28.4 0.1 collective-permute-start.6
  28.5 11.0 %collective-permute-done.1.refs_2_.refs_1_ = bf16[144,1024]{1,0:T(8,128)(2,1)S(1)} collective-permute-done((bf16[144,1024]{1,0:T(8,128)(2,1)S(1)}, bf16[144,1024]{1,0:T(8,128)(2,1)S(1)}, u32[]{:S(2)}, u32[]{:S(2)}) %collective-permute-start.1) | collective-permute-done | bytes 294944 | tf_op jit(solution)/shard_map/ppermute | solution.py:443
  39.4 0.5 collective-permute-start.11
  39.9 0.8 copy-done.9
  40.7 0.7 dynamic-slice_reduce_fusion
  41.4 0.1 reshape_squeeze.3
  41.5 0.1 copy.21
  41.6 0.1 reshape.23.tgt_ref
  41.7 0.0 copy-start.11
  41.7 0.7 dynamic-slice_bitcast_fusion.where_ref
  42.4 0.1 slice_bitcast_fusion.1
  42.6 0.1 collective-permute-start.8
  42.7 0.5 collective-permute-start.13
  43.2 0.1 collective-permute-start.12
  43.3 0.4 collective-permute-start.14
  43.7 9.6 %collective-permute-done.7.refs_12_ = bf16[64,3072]{1,0:T(8,128)(2,1)} collective-permute-done((bf16[64,3072]{1,0:T(8,128)(2,1)}, bf16[64,3072]{1,0:T(8,128)(2,1)}, u32[]{:S(2)}, u32[]{:S(2)}) %collective-permute-start.7) | collective-permute-done | bytes 393248 | tf_op jit(solution)/shard_map/ppermute | solution.py:442
  53.3 0.1 pad_add_fusion.3.micro_ref
  53.3 0.1 pad_add_fusion.2.micro_ref
  53.4 0.1 pad_add_fusion.1.micro_ref
  53.5 0.1 pad_add_fusion.micro_ref
  53.6 0.2 collective-permute-start.18
  53.8 6.9 %collective-permute-start.19 = (bf16[144,1024]{1,0:T(8,128)(2,1)S(1)}, bf16[144,1024]{1,0:T(8,128)(2,1)S(1)}, u32[]{:S(2)}, u32[]{:S(2)}) collective-permute-start(bf16[144,1024]{1,0:T(8,128)(2,1)S(1)} %pass_after.2), channel_id=1, source_target_pairs={{0,2},{1,3},{2,0},{3,1},{4,6},{5,7},{6,4},{7,5},{8,10},{9,11},{10,... | collective-permute-start | bytes 884744 | tf_op jit(solution)/shard_map/ppermute | solution.py:443
  60.8 8.5 %encode.2.refs_0_ = bf16[272,1024]{1,0:T(8,128)(2,1)S(1)} custom-call(s32[16]{0:T(128)S(1)} %dynamic-slice_bitcast_fusion.where_ref, bf16[144,1024]{1,0:T(8,128)(2,1)S(1)} %copy-done.4, bf16[144,1024]{1,0:T(8,128)(2,1)S(1)} %collective-permute-done.1.refs_2_.refs_1_, f32[1,1024]{1,0:T(1,128)S(1)} %bitcast.46, bf16[31,1024]{1,0:T(8,128)(2,1)S(1)} %copy-done.11, ...), custom_call_target="tpu_custom_call" | custom-call | flops 8000000000 | bytes 8388608 | tf_op jit(solution)/shard_map/encode/pallas_call | solution.py:230
  69.3 0.0 copy-start.7
  69.3 1.6 %collective-permute-start.16 = (bf16[272,1024]{1,0:T(8,128)(2,1)S(1)}, bf16[272,1024]{1,0:T(8,128)(2,1)S(1)}, u32[]{:S(2)}, u32[]{:S(2)}) collective-permute-start(bf16[272,1024]{1,0:T(8,128)(2,1)S(1)} %encode.2.refs_0_), channel_id=1, source_target_pairs={{0,4},{1,5},{2,6},{3,7},{4,8},{5,9},{6,10},{7,11},{8,12},{9,13},{1... | collective-permute-start | bytes 1671176 | tf_op jit(solution)/shard_map/ppermute | solution.py:443
  70.9 1.7 %collective-permute-start.23 = (bf16[272,1024]{1,0:T(8,128)(2,1)S(1)}, bf16[272,1024]{1,0:T(8,128)(2,1)S(1)}, u32[]{:S(2)}, u32[]{:S(2)}) collective-permute-start(bf16[272,1024]{1,0:T(8,128)(2,1)S(1)} %encode.2.refs_0_), channel_id=1, source_target_pairs={{0,12},{1,13},{2,14},{3,15},{4,0},{5,1},{6,2},{7,3},{8,4},{9,5},{1... | collective-permute-start | bytes 1671176 | tf_op jit(solution)/shard_map/ppermute | solution.py:443
  72.6 12.0 %collective-permute-done.18.refs_0_ = bf16[144,1024]{1,0:T(8,128)(2,1)S(1)} collective-permute-done((bf16[144,1024]{1,0:T(8,128)(2,1)S(1)}, bf16[144,1024]{1,0:T(8,128)(2,1)S(1)}, u32[]{:S(2)}, u32[]{:S(2)}) %collective-permute-start.18) | collective-permute-done | bytes 294944 | tf_op jit(solution)/shard_map/ppermute | solution.py:443
  84.6 8.5 %encode.3.refs_1_ = bf16[272,1024]{1,0:T(8,128)(2,1)S(1)} custom-call(s32[16]{0:T(128)S(1)} %dynamic-slice_bitcast_fusion.where_ref, bf16[144,1024]{1,0:T(8,128)(2,1)S(1)} %collective-permute-done.18.refs_0_, bf16[144,1024]{1,0:T(8,128)(2,1)S(1)} %collective-permute-done.19.refs_1_, f32[1,1024]{1,0:T(1,128)S(1)} %bitcast.47, ...), custom_call_target="tpu_custom_call" | custom-call | flops 8000000000 | bytes 8388608 | tf_op jit(solution)/shard_map/encode/pallas_call | solution.py:230
  93.1 3.1 %collective-permute-start.20 = (bf16[272,1024]{1,0:T(8,128)(2,1)S(1)}, bf16[272,1024]{1,0:T(8,128)(2,1)S(1)}, u32[]{:S(2)}, u32[]{:S(2)}) collective-permute-start(bf16[272,1024]{1,0:T(8,128)(2,1)S(1)} %encode.3.refs_1_), channel_id=1, source_target_pairs={{0,12},{1,13},{2,14},{3,15},{4,0},{5,1},{6,2},{7,3},{8,4},{9,5},{1... | collective-permute-start | bytes 1671176 | tf_op jit(solution)/shard_map/ppermute | solution.py:443
  96.2 6.1 %decode.4.refs_7_ = bf16[512,1024]{1,0:T(8,128)(2,1)} custom-call(s32[4]{0:T(128)S(1)} %pad_add_fusion.3.micro_ref, s32[64]{0:T(128)S(1)} %reshape.23.tgt_ref, bf16[272,1024]{1,0:T(8,128)(2,1)S(1)} %encode.2.refs_0_, bf16[272,1024]{1,0:T(8,128)(2,1)S(1)} %encode.3.refs_1_, bf16[512,1024]{1,0:T(8,128)(2,1)S(1)} %project_query.1.refs_1_.refs_2_, ...), custom_call_target="tpu_custom_call" | custom-call | flops 8589934592 | bytes 8388608 | tf_op jit(solution)/shard_map/decode/pallas_call | solution.py:344
  102.4 6.0 %collective-permute-done.20.refs_1_ = bf16[272,1024]{1,0:T(8,128)(2,1)S(1)} collective-permute-done((bf16[272,1024]{1,0:T(8,128)(2,1)S(1)}, bf16[272,1024]{1,0:T(8,128)(2,1)S(1)}, u32[]{:S(2)}, u32[]{:S(2)}) %collective-permute-start.20) | collective-permute-done | bytes 557088 | tf_op jit(solution)/shard_map/ppermute | solution.py:443
  108.3 3.7 %collective-permute-start.21 = (bf16[272,1024]{1,0:T(8,128)(2,1)S(1)}, bf16[272,1024]{1,0:T(8,128)(2,1)S(1)}, u32[]{:S(2)}, u32[]{:S(2)}) collective-permute-start(bf16[272,1024]{1,0:T(8,128)(2,1)S(1)} %collective-permute-done.20.refs_1_), channel_id=1, source_target_pairs={{0,12},{1,13},{2,14},{3,15},{4,0},{5,1},{6,2},{7,3},{8,4},{9,5},{1... | collective-permute-start | bytes 1671176 | tf_op jit(solution)/shard_map/ppermute | solution.py:443
  112.0 6.2 %decode.5.refs_7_ = bf16[512,1024]{1,0:T(8,128)(2,1)} custom-call(s32[4]{0:T(128)S(1)} %pad_add_fusion.2.micro_ref, s32[64]{0:T(128)S(1)} %reshape.23.tgt_ref, bf16[272,1024]{1,0:T(8,128)(2,1)S(1)} %collective-permute-done.16.refs_0_, bf16[272,1024]{1,0:T(8,128)(2,1)S(1)} %collective-permute-done.23.refs_1_, ...), custom_call_target="tpu_custom_call", output_to_operand_aliasing={{}: (9, {})} | custom-call | flops 8589934592 | bytes 8388608 | tf_op jit(solution)/shard_map/decode/pallas_call | solution.py:344
  118.3 6.2 %decode.6.refs_7_ = bf16[512,1024]{1,0:T(8,128)(2,1)} custom-call(s32[4]{0:T(128)S(1)} %pad_add_fusion.1.micro_ref, s32[64]{0:T(128)S(1)} %reshape.23.tgt_ref, bf16[272,1024]{1,0:T(8,128)(2,1)S(1)} %collective-permute-done.22.refs_0_, bf16[272,1024]{1,0:T(8,128)(2,1)S(1)} %collective-permute-done.20.refs_1_, ...), custom_call_target="tpu_custom_call", output_to_operand_aliasing={{}: (9, {})} | custom-call | flops 8589934592 | bytes 8388608 | tf_op jit(solution)/shard_map/decode/pallas_call | solution.py:344
  124.5 2.3 %collective-permute-done.17.refs_0_ = bf16[272,1024]{1,0:T(8,128)(2,1)S(1)} collective-permute-done((bf16[272,1024]{1,0:T(8,128)(2,1)S(1)}, bf16[272,1024]{1,0:T(8,128)(2,1)S(1)}, u32[]{:S(2)}, u32[]{:S(2)}) %collective-permute-start.17) | collective-permute-done | bytes 557088 | tf_op jit(solution)/shard_map/ppermute | solution.py:443
  126.8 6.2 %decode.7 = bf16[512,1024]{1,0:T(8,128)(2,1)} custom-call(s32[4]{0:T(128)S(1)} %pad_add_fusion.micro_ref, s32[64]{0:T(128)S(1)} %reshape.23.tgt_ref, bf16[272,1024]{1,0:T(8,128)(2,1)S(1)} %collective-permute-done.17.refs_0_, bf16[272,1024]{1,0:T(8,128)(2,1)S(1)} %collective-permute-done.21.refs_1_, ...), custom_call_target="tpu_custom_call", output_to_operand_aliasing={{}: (9, {})} | custom-call | flops 8589934592 | bytes 8388608 | tf_op jit(solution)/shard_map/decode/pallas_call | solution.py:344
  (50 shorter events, 0.2 us)
Async XLA Ops:
  2.9 11.3 %collective-permute-start = (bf16[64,3072]{1,0:T(8,128)(2,1)}, bf16[64,3072]{1,0:T(8,128)(2,1)S(1)}, u32[]{:S(2)}, u32[]{:S(2)}) collective-permute-start(bf16[64,3072]{1,0:T(8,128)(2,1)} %get-tuple-element.8.value_ref.refs_5_), channel_id=1, source_target_pairs={{0,128},{16,144},{32,160},{48,176},{64,192},{80,208},{96,224},{112... | collective-permute-start | bytes 1179656 | tf_op jit(solution)/shard_map/ppermute | solution.py:442
  4.9 23.5 %collective-permute-start.2 = (bf16[64,3072]{1,0:T(8,128)(2,1)}, bf16[64,3072]{1,0:T(8,128)(2,1)S(1)}, u32[]{:S(2)}, u32[]{:S(2)}) collective-permute-start(bf16[64,3072]{1,0:T(8,128)(2,1)} %get-tuple-element.8.value_ref.refs_5_), channel_id=1, source_target_pairs={{0,32},{16,48},{32,64},{48,80},{64,96},{80,112},{96,0},{112,16},{1... | collective-permute-start | bytes 1179656 | tf_op jit(solution)/shard_map/ppermute | solution.py:442
  5.4 23.0 %collective-permute-start.3 = (bf16[64,3072]{1,0:T(8,128)(2,1)}, bf16[64,3072]{1,0:T(8,128)(2,1)S(1)}, u32[]{:S(2)}, u32[]{:S(2)}) collective-permute-start(bf16[64,3072]{1,0:T(8,128)(2,1)} %get-tuple-element.8.value_ref.refs_5_), channel_id=1, source_target_pairs={{0,96},{16,112},{32,0},{48,16},{64,32},{80,48},{96,64},{112,80},{1... | collective-permute-start | bytes 1179656 | tf_op jit(solution)/shard_map/ppermute | solution.py:442
  14.2 25.2 %collective-permute-start.5 = (bf16[64,3072]{1,0:T(8,128)(2,1)S(1)}, bf16[64,3072]{1,0:T(8,128)(2,1)}, u32[]{:S(2)}, u32[]{:S(2)}) collective-permute-start(bf16[64,3072]{1,0:T(8,128)(2,1)S(1)} %collective-permute-done.refs_0_.refs_6_), channel_id=1, source_target_pairs={{0,96},{16,112},{32,0},{48,16},{64,32},{80,48},{96,64},{112,80},{1... | collective-permute-start | bytes 1179656 | tf_op jit(solution)/shard_map/ppermute | solution.py:442
  15.0 24.9 %collective-permute-start.4 = (bf16[64,3072]{1,0:T(8,128)(2,1)S(1)}, bf16[64,3072]{1,0:T(8,128)(2,1)S(1)}, u32[]{:S(2)}, u32[]{:S(2)}) collective-permute-start(bf16[64,3072]{1,0:T(8,128)(2,1)S(1)} %collective-permute-done.refs_0_.refs_6_), channel_id=1, source_target_pairs={{0,32},{16,48},{32,64},{48,80},{64,96},{80,112},{96,0},{112,16},{1... | collective-permute-start | bytes 1179656 | tf_op jit(solution)/shard_map/ppermute | solution.py:442
  17.5 1.6 %copy-start = (bf16[1,1024,1024]{2,1,0:T(8,128)(2,1)S(1)}, bf16[1,1024,1024]{2,1,0:T(8,128)(2,1)}, u32[]{:S(2)}) copy-start(bf16[1,1024,1024]{2,1,0:T(8,128)(2,1)} %param.25) | copy-start | bytes 6291460
  19.0 1.2 copy-start.1
  20.3 0.7 copy-start.5
  21.0 3.0 %copy-start.4 = (bf16[144,1024]{1,0:T(8,128)(2,1)S(1)}, bf16[144,1024]{1,0:T(8,128)(2,1)}, u32[]{:S(2)}) copy-start(bf16[144,1024]{1,0:T(8,128)(2,1)} %get-tuple-element.7.value_ref.refs_0_) | copy-start | bytes 884740
  21.0 20.5 %copy-start.14 = (s32[16,4]{0,1:T(4,128)S(1)}, s32[16,4]{0,1:T(4,128)}, u32[]{:S(2)}) copy-start(s32[16,4]{0,1:T(4,128)} %param.18) | copy-start | bytes 772
  21.0 21.6 %copy-start.3 = (bf16[64,3072]{1,0:T(8,128)(2,1)S(1)}, bf16[64,3072]{1,0:T(8,128)(2,1)}, u32[]{:S(2)}) copy-start(bf16[64,3072]{1,0:T(8,128)(2,1)} %get-tuple-element.8.value_ref.refs_5_) | copy-start | bytes 1179652
  23.9 36.8 %copy-start.12 = (f32[1024]{0:T(1024)S(1)}, f32[1024]{0:T(1024)}, u32[]{:S(2)}) copy-start(f32[1024]{0:T(1024)} %param.19) | copy-start | bytes 12292
  23.9 36.8 %copy-start.13 = (f32[1024]{0:T(1024)S(1)}, f32[1024]{0:T(1024)}, u32[]{:S(2)}) copy-start(f32[1024]{0:T(1024)} %param.22) | copy-start | bytes 12292
  24.0 15.4 %collective-permute-start.1 = (bf16[144,1024]{1,0:T(8,128)(2,1)S(1)}, bf16[144,1024]{1,0:T(8,128)(2,1)S(1)}, u32[]{:S(2)}, u32[]{:S(2)}) collective-permute-start(bf16[144,1024]{1,0:T(8,128)(2,1)S(1)} %pass_after.2), channel_id=1, source_target_pairs={{0,1},{1,2},{2,3},{3,0},{4,5},{5,6},{6,7},{7,4},{8,9},{9,10},{10,1... | collective-permute-start | bytes 884744 | tf_op jit(solution)/shard_map/ppermute | solution.py:443
  28.4 14.2 %collective-permute-start.9 = (bf16[64,3072]{1,0:T(8,128)(2,1)S(1)}, bf16[64,3072]{1,0:T(8,128)(2,1)}, u32[]{:S(2)}, u32[]{:S(2)}) collective-permute-start(bf16[64,3072]{1,0:T(8,128)(2,1)S(1)} %collective-permute-done.refs_0_.refs_6_), channel_id=1, source_target_pairs={{0,16},{16,0},{32,48},{48,32},{64,80},{80,64},{96,112},{112,96},{1... | collective-permute-start | bytes 1179656 | tf_op jit(solution)/shard_map/ppermute | solution.py:442
  28.4 14.3 %collective-permute-start.6 = (bf16[64,3072]{1,0:T(8,128)(2,1)S(1)}, bf16[64,3072]{1,0:T(8,128)(2,1)}, u32[]{:S(2)}, u32[]{:S(2)}) collective-permute-start(bf16[64,3072]{1,0:T(8,128)(2,1)S(1)} %collective-permute-done.2.refs_7_), channel_id=1, source_target_pairs={{0,32},{16,48},{32,64},{48,80},{64,96},{80,112},{96,0},{112,16},{1... | collective-permute-start | bytes 1179656 | tf_op jit(solution)/shard_map/ppermute | solution.py:442
  39.4 3.7 %collective-permute-start.10 = (bf16[64,3072]{1,0:T(8,128)(2,1)S(1)}, bf16[64,3072]{1,0:T(8,128)(2,1)}, u32[]{:S(2)}, u32[]{:S(2)}) collective-permute-start(bf16[64,3072]{1,0:T(8,128)(2,1)S(1)} %collective-permute-done.2.refs_7_), channel_id=1, source_target_pairs={{0,16},{16,0},{32,48},{48,32},{64,80},{80,64},{96,112},{112,96},{1... | collective-permute-start | bytes 1179656 | tf_op jit(solution)/shard_map/ppermute | solution.py:442
  39.4 3.9 %collective-permute-start.11 = (bf16[64,3072]{1,0:T(8,128)(2,1)S(1)}, bf16[64,3072]{1,0:T(8,128)(2,1)}, u32[]{:S(2)}, u32[]{:S(2)}) collective-permute-start(bf16[64,3072]{1,0:T(8,128)(2,1)S(1)} %collective-permute-done.3.refs_8_), channel_id=1, source_target_pairs={{0,16},{16,0},{32,48},{48,32},{64,80},{80,64},{96,112},{112,96},{1... | collective-permute-start | bytes 1179656 | tf_op jit(solution)/shard_map/ppermute | solution.py:442
  39.9 0.8 copy-start.9
  40.7 12.6 %collective-permute-start.7 = (bf16[64,3072]{1,0:T(8,128)(2,1)}, bf16[64,3072]{1,0:T(8,128)(2,1)}, u32[]{:S(2)}, u32[]{:S(2)}) collective-permute-start(bf16[64,3072]{1,0:T(8,128)(2,1)} %collective-permute-done.5.refs_10_), channel_id=1, source_target_pairs={{0,96},{16,112},{32,0},{48,16},{64,32},{80,48},{96,64},{112,80},{1... | collective-permute-start | bytes 1179656 | tf_op jit(solution)/shard_map/ppermute | solution.py:442
  41.7 1.5 %copy-start.10 = (bf16[64,3072]{1,0:T(8,128)(2,1)S(1)}, bf16[64,3072]{1,0:T(8,128)(2,1)}, u32[]{:S(2)}) copy-start(bf16[64,3072]{1,0:T(8,128)(2,1)} %copy-done.9) | copy-start | bytes 1179652
  41.7 19.1 %copy-start.11 = (bf16[31,1024]{1,0:T(8,128)(2,1)S(1)}, bf16[31,1024]{1,0:T(8,128)(2,1)}, u32[]{:S(2)}) copy-start(bf16[31,1024]{1,0:T(8,128)(2,1)} %refs_3_.3) | copy-start | bytes 190468
  42.6 11.0 %collective-permute-start.8 = (bf16[64,3072]{1,0:T(8,128)(2,1)S(1)}, bf16[64,3072]{1,0:T(8,128)(2,1)S(1)}, u32[]{:S(2)}, u32[]{:S(2)}) collective-permute-start(bf16[64,3072]{1,0:T(8,128)(2,1)S(1)} %pass_after.3), channel_id=1, source_target_pairs={{0,16},{16,0},{32,48},{48,32},{64,80},{80,64},{96,112},{112,96},{1... | collective-permute-start | bytes 1179656 | tf_op jit(solution)/shard_map/ppermute | solution.py:442
  42.7 11.1 %collective-permute-start.13 = (bf16[64,3072]{1,0:T(8,128)(2,1)}, bf16[64,3072]{1,0:T(8,128)(2,1)S(1)}, u32[]{:S(2)}, u32[]{:S(2)}) collective-permute-start(bf16[64,3072]{1,0:T(8,128)(2,1)} %collective-permute-done.5.refs_10_), channel_id=1, source_target_pairs={{0,16},{16,0},{32,48},{48,32},{64,80},{80,64},{96,112},{112,96},{1... | collective-permute-start | bytes 1179656 | tf_op jit(solution)/shard_map/ppermute | solution.py:442
  43.2 17.5 %collective-permute-start.12 = (bf16[64,3072]{1,0:T(8,128)(2,1)S(1)}, bf16[64,3072]{1,0:T(8,128)(2,1)S(1)}, u32[]{:S(2)}, u32[]{:S(2)}) collective-permute-start(bf16[64,3072]{1,0:T(8,128)(2,1)S(1)} %copy-done.10), channel_id=1, source_target_pairs={{0,16},{16,0},{32,48},{48,32},{64,80},{80,64},{96,112},{112,96},{1... | collective-permute-start | bytes 1179656 | tf_op jit(solution)/shard_map/ppermute | solution.py:442
  43.3 17.4 %collective-permute-start.14 = (bf16[64,3072]{1,0:T(8,128)(2,1)}, bf16[64,3072]{1,0:T(8,128)(2,1)S(1)}, u32[]{:S(2)}, u32[]{:S(2)}) collective-permute-start(bf16[64,3072]{1,0:T(8,128)(2,1)} %collective-permute-done.6.refs_11_), channel_id=1, source_target_pairs={{0,16},{16,0},{32,48},{48,32},{64,80},{80,64},{96,112},{112,96},{1... | collective-permute-start | bytes 1179656 | tf_op jit(solution)/shard_map/ppermute | solution.py:442
  53.3 7.5 %collective-permute-start.15 = (bf16[64,3072]{1,0:T(8,128)(2,1)}, bf16[64,3072]{1,0:T(8,128)(2,1)S(1)}, u32[]{:S(2)}, u32[]{:S(2)}) collective-permute-start(bf16[64,3072]{1,0:T(8,128)(2,1)} %collective-permute-done.7.refs_12_), channel_id=1, source_target_pairs={{0,16},{16,0},{32,48},{48,32},{64,80},{80,64},{96,112},{112,96},{1... | collective-permute-start | bytes 1179656 | tf_op jit(solution)/shard_map/ppermute | solution.py:442
  53.6 31.1 %collective-permute-start.18 = (bf16[144,1024]{1,0:T(8,128)(2,1)S(1)}, bf16[144,1024]{1,0:T(8,128)(2,1)S(1)}, u32[]{:S(2)}, u32[]{:S(2)}) collective-permute-start(bf16[144,1024]{1,0:T(8,128)(2,1)S(1)} %pass_after.2), channel_id=1, source_target_pairs={{0,3},{1,0},{2,1},{3,2},{4,7},{5,4},{6,5},{7,6},{8,11},{9,8},{10,9... | collective-permute-start | bytes 884744 | tf_op jit(solution)/shard_map/ppermute | solution.py:443
  53.8 30.9 %collective-permute-start.19 = (bf16[144,1024]{1,0:T(8,128)(2,1)S(1)}, bf16[144,1024]{1,0:T(8,128)(2,1)S(1)}, u32[]{:S(2)}, u32[]{:S(2)}) collective-permute-start(bf16[144,1024]{1,0:T(8,128)(2,1)S(1)} %pass_after.2), channel_id=1, source_target_pairs={{0,2},{1,3},{2,0},{3,1},{4,6},{5,7},{6,4},{7,5},{8,10},{9,11},{10,... | collective-permute-start | bytes 884744 | tf_op jit(solution)/shard_map/ppermute | solution.py:443
  69.3 26.9 %copy-start.2 = (bf16[1,16,4,8,1024]{4,3,2,1,0:T(8,128)(2,1)S(1)}, bf16[1,16,4,8,1024]{4,3,2,1,0:T(8,128)(2,1)}, u32[]{:S(2)}) copy-start(bf16[1,16,4,8,1024]{4,3,2,1,0:T(8,128)(2,1)} %param.29) | copy-start | bytes 3145732
  69.3 26.9 %copy-start.6 = (bf16[1,1024,1024]{2,1,0:T(8,128)(2,1)S(1)}, bf16[1,1024,1024]{2,1,0:T(8,128)(2,1)}, u32[]{:S(2)}) copy-start(bf16[1,1024,1024]{2,1,0:T(8,128)(2,1)} %param.26) | copy-start | bytes 6291460
  69.3 26.9 %copy-start.7 = (bf16[1,1024,1024]{2,1,0:T(8,128)(2,1)S(1)}, bf16[1,1024,1024]{2,1,0:T(8,128)(2,1)}, u32[]{:S(2)}) copy-start(bf16[1,1024,1024]{2,1,0:T(8,128)(2,1)} %param.27) | copy-start | bytes 6291460
  69.3 26.9 %copy-start.8 = (bf16[1,1024,1024]{2,1,0:T(8,128)(2,1)S(1)}, bf16[1,1024,1024]{2,1,0:T(8,128)(2,1)}, u32[]{:S(2)}) copy-start(bf16[1,1024,1024]{2,1,0:T(8,128)(2,1)} %param.28) | copy-start | bytes 6291460
  69.3 42.7 %collective-permute-start.16 = (bf16[272,1024]{1,0:T(8,128)(2,1)S(1)}, bf16[272,1024]{1,0:T(8,128)(2,1)S(1)}, u32[]{:S(2)}, u32[]{:S(2)}) collective-permute-start(bf16[272,1024]{1,0:T(8,128)(2,1)S(1)} %encode.2.refs_0_), channel_id=1, source_target_pairs={{0,4},{1,5},{2,6},{3,7},{4,8},{5,9},{6,10},{7,11},{8,12},{9,13},{1... | collective-permute-start | bytes 1671176 | tf_op jit(solution)/shard_map/ppermute | solution.py:443
  70.9 41.1 %collective-permute-start.23 = (bf16[272,1024]{1,0:T(8,128)(2,1)S(1)}, bf16[272,1024]{1,0:T(8,128)(2,1)S(1)}, u32[]{:S(2)}, u32[]{:S(2)}) collective-permute-start(bf16[272,1024]{1,0:T(8,128)(2,1)S(1)} %encode.2.refs_0_), channel_id=1, source_target_pairs={{0,12},{1,13},{2,14},{3,15},{4,0},{5,1},{6,2},{7,3},{8,4},{9,5},{1... | collective-permute-start | bytes 1671176 | tf_op jit(solution)/shard_map/ppermute | solution.py:443
  93.1 15.2 %collective-permute-start.20 = (bf16[272,1024]{1,0:T(8,128)(2,1)S(1)}, bf16[272,1024]{1,0:T(8,128)(2,1)S(1)}, u32[]{:S(2)}, u32[]{:S(2)}) collective-permute-start(bf16[272,1024]{1,0:T(8,128)(2,1)S(1)} %encode.3.refs_1_), channel_id=1, source_target_pairs={{0,12},{1,13},{2,14},{3,15},{4,0},{5,1},{6,2},{7,3},{8,4},{9,5},{1... | collective-permute-start | bytes 1671176 | tf_op jit(solution)/shard_map/ppermute | solution.py:443
  96.2 22.1 %collective-permute-start.22 = (bf16[272,1024]{1,0:T(8,128)(2,1)S(1)}, bf16[272,1024]{1,0:T(8,128)(2,1)S(1)}, u32[]{:S(2)}, u32[]{:S(2)}) collective-permute-start(bf16[272,1024]{1,0:T(8,128)(2,1)S(1)} %encode.3.refs_1_), channel_id=1, source_target_pairs={{0,4},{1,5},{2,6},{3,7},{4,8},{5,9},{6,10},{7,11},{8,12},{9,13},{1... | collective-permute-start | bytes 1671176 | tf_op jit(solution)/shard_map/ppermute | solution.py:443
  108.3 16.2 %collective-permute-start.21 = (bf16[272,1024]{1,0:T(8,128)(2,1)S(1)}, bf16[272,1024]{1,0:T(8,128)(2,1)S(1)}, u32[]{:S(2)}, u32[]{:S(2)}) collective-permute-start(bf16[272,1024]{1,0:T(8,128)(2,1)S(1)} %collective-permute-done.20.refs_1_), channel_id=1, source_target_pairs={{0,12},{1,13},{2,14},{3,15},{4,0},{5,1},{6,2},{7,3},{8,4},{9,5},{1... | collective-permute-start | bytes 1671176 | tf_op jit(solution)/shard_map/ppermute | solution.py:443
  112.0 14.7 %collective-permute-start.17 = (bf16[272,1024]{1,0:T(8,128)(2,1)S(1)}, bf16[272,1024]{1,0:T(8,128)(2,1)S(1)}, u32[]{:S(2)}, u32[]{:S(2)}) collective-permute-start(bf16[272,1024]{1,0:T(8,128)(2,1)S(1)} %collective-permute-done.16.refs_0_), channel_id=1, source_target_pairs={{0,4},{1,5},{2,6},{3,7},{4,8},{5,9},{6,10},{7,11},{8,12},{9,13},{1... | collective-permute-start | bytes 1671176 | tf_op jit(solution)/shard_map/ppermute | solution.py:443
where the time goes:
time: 133 us
  waiting for transfers between devices  48.1 us (36%)
  Pallas kernels  47.6 us (36%)
  starting transfers between devices  30.6 us (23%)
  local copies, waits for them, and re-layouts  6.11 us (5%)
    ppermute x9, waiting for transfers between devices, body(): along = lambda v, dy, dz: lax.ppermute(v, 'section', section_perm(dy, dz))  31.2 us
    pallas_call x4, Pallas kernels, decode(): pl.pallas_call(functools.partial(decode_kernel, len(mems), aliased), out_...  24.8 us
    ppermute x9, starting transfers between devices, body(): along = lambda v, dy, dz: lax.ppermute(v, 'section', section_perm(dy, dz))  21.6 us
    pallas_call x2, Pallas kernels, encode(): pl.pallas_call(functools.partial(encode_kernel, len(shards)), out_shape=j...  17 us
    ppermute x15, waiting for transfers between devices, body(): across = lambda v, perm: lax.ppermute(v, 'dp', perm)  16.9 us
    ppermute x15, starting transfers between devices, body(): across = lambda v, perm: lax.ppermute(v, 'dp', perm)  8.97 us
    unnamed x31, local copies, waits for them, and re-layouts  4.41 us
    pallas_call x1, Pallas kernels, project_query(): pl.pallas_call(query_kernel, out_shape=jax.ShapeDtypeStruct((rows, D), BF...  2.95 us
  transfers between devices with their start and end apart: 24, of which 6 were waited for; matrix products, arithmetic and copies ran while one was open for 2% of the time, Pallas kernels for 29%

commit v1 on v0

--- a/solution.py
+++ b/solution.py
@@ -453,13 +453,12 @@
     query = project_query(source, dec_gain, w_query[0])
     pair_l, pair_r = across(pair, TO_RIGHT), across(pair, TO_LEFT)
     own_2, pair_2 = across(own_l, TO_RIGHT), across(pair_r, TO_LEFT)
-    ready = pass_after(packed, pair, query)
-    from_b = along(ready, 0, 1)
+    ready = pass_after(packed, pair)
+    from_b, from_a = along(ready, 0, 1), along(ready, 0, -1)
     shards = [own, pair, own_l, own_r, pair_l, pair_r, own_2, pair_2]
-    turn = [pass_after(own, pair, query, from_b)] + shards[1:]
+    turn = [pass_after(own, query, from_b, from_a)] + shards[1:]
     shards += [across(v, TO_CORE) for v in turn]
-
-    from_a, from_2 = along(ready, 0, -1), along(ready, 0, 2)
+    from_2 = along(pass_after(packed, from_a), 0, 2)
 
     def encode_pair(first, second):
         return encode(

time: 133 us -> 120 us (0.902)
  the two profiles are of different devices: /device:TPU:70 before, /device:TPU:6 now
where the time goes in v1:
time: 120 us; the launch traced here: 119 us
  Pallas kernels  45.6 us (38%)
  waiting for transfers between devices  40.3 us (34%)
  starting transfers between devices  25.7 us (21%)
  local copies, waits for them, and re-layouts  6.96 us (6%)
    ppermute x9, waiting for transfers between devices, body(): along = lambda v, dy, dz: lax.ppermute(v, 'section', section_perm(dy, dz))  27.9 us
    pallas_call x4, Pallas kernels, decode(): pl.pallas_call(functools.partial(decode_kernel, len(mems), aliased), out_...  24.8 us
    ppermute x9, starting transfers between devices, body(): along = lambda v, dy, dz: lax.ppermute(v, 'section', section_perm(dy, dz))  16.5 us
    pallas_call x2, Pallas kernels, encode(): pl.pallas_call(functools.partial(encode_kernel, len(shards)), out_shape=j...  14.9 us
    ppermute x15, waiting for transfers between devices, body(): across = lambda v, perm: lax.ppermute(v, 'dp', perm)  12.3 us
    ppermute x15, starting transfers between devices, body(): across = lambda v, perm: lax.ppermute(v, 'dp', perm)  9.26 us
    unnamed x27, local copies, waits for them, and re-layouts  5.27 us
    pallas_call x1, Pallas kernels, project_query(): pl.pallas_call(query_kernel, out_shape=jax.ShapeDtypeStruct((rows, D), BF...  2.95 us
  transfers between devices with their start and end apart: 24, of which 8 were waited for; matrix products, arithmetic and copies ran while one was open for 2% of the time, Pallas kernels for 31%

profile of v1, /device:TPU:6, one launch (start us, length us, event | category | flops | bytes accessed | tf_op | source)
XLA Modules:
  0.0 119.3 jit_solution(11934170660121316714)
XLA Ops:
  0.0 2.9 %prepare.1 = (bf16[64,3072]{1,0:T(8,128)(2,1)}, bf16[144,1024]{1,0:T(8,128)(2,1)}) custom-call(s32[4]{0:T(128)} %bitcast.51, bf16[160,1024]{1,0:T(8,128)(2,1)} %bitcast.50, bf16[64,2048]{1,0:T(8,128)(2,1)} %w_in_hbm.1, bf16[64,1024]{1,0:T(8,128)(2,1)} %w_out_hbm.1), custom_call_target="tpu_custom_call" | custom-call | flops 50000000 | bytes 1400000 | tf_op jit(solution)/shard_map/prepare/pallas_call | solution.py:87
  2.9 2.0 %collective-permute-start = (bf16[64,3072]{1,0:T(8,128)(2,1)}, bf16[64,3072]{1,0:T(8,128)(2,1)S(1)}, u32[]{:S(2)}, u32[]{:S(2)}) collective-permute-start(bf16[64,3072]{1,0:T(8,128)(2,1)} %get-tuple-element.8.value_ref.refs_5_), channel_id=1, source_target_pairs={{0,128},{16,144},{32,160},{48,176},{64,192},{80,208},{96,224},{112... | collective-permute-start | bytes 1179656 | tf_op jit(solution)/shard_map/ppermute | solution.py:442
  4.9 0.5 collective-permute-start.2
  5.4 1.5 %collective-permute-start.3 = (bf16[64,3072]{1,0:T(8,128)(2,1)}, bf16[64,3072]{1,0:T(8,128)(2,1)S(1)}, u32[]{:S(2)}, u32[]{:S(2)}) collective-permute-start(bf16[64,3072]{1,0:T(8,128)(2,1)} %get-tuple-element.8.value_ref.refs_5_), channel_id=1, source_target_pairs={{0,96},{16,112},{32,0},{48,16},{64,32},{80,48},{96,64},{112,80},{1... | collective-permute-start | bytes 1179656 | tf_op jit(solution)/shard_map/ppermute | solution.py:442
  6.9 7.3 %collective-permute-done.refs_0_.refs_6_ = bf16[64,3072]{1,0:T(8,128)(2,1)S(1)} collective-permute-done((bf16[64,3072]{1,0:T(8,128)(2,1)}, bf16[64,3072]{1,0:T(8,128)(2,1)S(1)}, u32[]{:S(2)}, u32[]{:S(2)}) %collective-permute-start) | collective-permute-done | bytes 393248 | tf_op jit(solution)/shard_map/ppermute | solution.py:442
  14.2 0.8 collective-permute-start.5
  15.0 2.4 %collective-permute-start.4 = (bf16[64,3072]{1,0:T(8,128)(2,1)S(1)}, bf16[64,3072]{1,0:T(8,128)(2,1)S(1)}, u32[]{:S(2)}, u32[]{:S(2)}) collective-permute-start(bf16[64,3072]{1,0:T(8,128)(2,1)S(1)} %collective-permute-done.refs_0_.refs_6_), channel_id=1, source_target_pairs={{0,32},{16,48},{32,64},{48,80},{64,96},{80,112},{96,0},{112,16},{1... | collective-permute-start | bytes 1179656 | tf_op jit(solution)/shard_map/ppermute | solution.py:442
  17.5 1.0 copy-done.1
  18.4 6.2 %collective-permute-start.8 = (bf16[144,1024]{1,0:T(8,128)(2,1)S(1)}, bf16[144,1024]{1,0:T(8,128)(2,1)S(1)}, u32[]{:S(2)}, u32[]{:S(2)}) collective-permute-start(bf16[144,1024]{1,0:T(8,128)(2,1)S(1)} %pass_after.3), channel_id=1, source_target_pairs={{0,3},{1,0},{2,1},{3,2},{4,7},{5,4},{6,5},{7,6},{8,11},{9,8},{10,9... | collective-permute-start | bytes 884744 | tf_op jit(solution)/shard_map/ppermute | solution.py:443
  24.6 0.7 dynamic-slice_reduce_fusion
  25.4 0.1 reshape_squeeze.3
  25.4 0.8 copy.21
  26.2 0.1 reshape.23.tgt_ref
  26.3 0.1 collective-permute-start.10
  26.4 9.4 %collective-permute-done.8.refs_2_.refs_0_ = bf16[144,1024]{1,0:T(8,128)(2,1)S(1)} collective-permute-done((bf16[144,1024]{1,0:T(8,128)(2,1)S(1)}, bf16[144,1024]{1,0:T(8,128)(2,1)S(1)}, u32[]{:S(2)}, u32[]{:S(2)}) %collective-permute-start.8) | collective-permute-done | bytes 294944 | tf_op jit(solution)/shard_map/ppermute | solution.py:443
  35.8 0.3 collective-permute-start.6
  36.1 3.5 %collective-permute-done.1.refs_1_ = bf16[144,1024]{1,0:T(8,128)(2,1)S(1)} collective-permute-done((bf16[144,1024]{1,0:T(8,128)(2,1)S(1)}, bf16[144,1024]{1,0:T(8,128)(2,1)S(1)}, u32[]{:S(2)}, u32[]{:S(2)}) %collective-permute-start.1) | collective-permute-done | bytes 294944 | tf_op jit(solution)/shard_map/ppermute | solution.py:443
  39.7 0.5 collective-permute-start.12
  40.2 1.6 %copy-done = bf16[1,1024,1024]{2,1,0:T(8,128)(2,1)S(1)} copy-done((bf16[1,1024,1024]{2,1,0:T(8,128)(2,1)S(1)}, bf16[1,1024,1024]{2,1,0:T(8,128)(2,1)}, u32[]{:S(2)}) %copy-start) | copy-done | bytes 2097176
  41.8 1.2 %copy-done.3 = bf16[1,16,4,8,1024]{4,3,2,1,0:T(8,128)(2,1)S(1)} copy-done((bf16[1,16,4,8,1024]{4,3,2,1,0:T(8,128)(2,1)S(1)}, bf16[1,16,4,8,1024]{4,3,2,1,0:T(8,128)(2,1)}, u32[]{:S(2)}) %copy-start.3) | copy-done | bytes 1048600
  43.0 0.7 copy-done.6
  43.7 2.9 %project_query.1.refs_0_.refs_2_ = bf16[512,1024]{1,0:T(8,128)(2,1)S(1)} custom-call(bf16[512,1024]{1,0:T(8,128)(2,1)S(1)} %bitcast.29, f32[1,1024]{1,0:T(1,128)S(1)} %copy-done.6, bf16[1024,1024]{1,0:T(8,128)(2,1)S(1)} %bitcast.28), custom_call_target="tpu_custom_call" | custom-call | flops 1073741824 | bytes 4194304 | tf_op jit(solution)/shard_map/project_query/pallas_call | solution.py:117
  46.7 0.7 dynamic-slice_bitcast_fusion.where_ref
  47.4 0.1 slice_bitcast_fusion.1
  47.5 0.2 collective-permute-start.9
  47.7 0.4 collective-permute-start.14
  48.1 0.1 collective-permute-start.13
  48.3 0.4 collective-permute-start.15
  48.7 3.8 %collective-permute-done.7.refs_12_ = bf16[64,3072]{1,0:T(8,128)(2,1)S(1)} collective-permute-done((bf16[64,3072]{1,0:T(8,128)(2,1)S(1)}, bf16[64,3072]{1,0:T(8,128)(2,1)S(1)}, u32[]{:S(2)}, u32[]{:S(2)}) %collective-permute-start.7) | collective-permute-done | bytes 393248 | tf_op jit(solution)/shard_map/ppermute | solution.py:442
  52.5 0.1 pad_add_fusion.3.micro_ref
  52.6 0.1 pad_add_fusion.2.micro_ref
  52.6 0.1 pad_add_fusion.1.micro_ref
  52.7 0.1 pad_add_fusion.micro_ref
  52.8 0.2 collective-permute-start.19
  53.0 1.2 collective-permute-done.16.refs_20_
  54.2 7.5 %encode.2.refs_0_ = bf16[272,1024]{1,0:T(8,128)(2,1)S(1)} custom-call(s32[16]{0:T(128)S(1)} %dynamic-slice_bitcast_fusion.where_ref, bf16[144,1024]{1,0:T(8,128)(2,1)S(1)} %copy-done.2, bf16[144,1024]{1,0:T(8,128)(2,1)S(1)} %collective-permute-done.1.refs_1_, f32[1,1024]{1,0:T(1,128)S(1)} %bitcast.46, bf16[31,1024]{1,0:T(8,128)(2,1)S(1)} %copy-done.10, ...), custom_call_target="tpu_custom_call" | custom-call | flops 8000000000 | bytes 8388608 | tf_op jit(solution)/shard_map/encode/pallas_call | solution.py:230
  61.7 1.7 %collective-permute-start.17 = (bf16[272,1024]{1,0:T(8,128)(2,1)S(1)}, bf16[272,1024]{1,0:T(8,128)(2,1)S(1)}, u32[]{:S(2)}, u32[]{:S(2)}) collective-permute-start(bf16[272,1024]{1,0:T(8,128)(2,1)S(1)} %encode.2.refs_0_), channel_id=1, source_target_pairs={{0,4},{1,5},{2,6},{3,7},{4,8},{5,9},{6,10},{7,11},{8,12},{9,13},{1... | collective-permute-start | bytes 1671176 | tf_op jit(solution)/shard_map/ppermute | solution.py:443
  63.4 1.7 %collective-permute-start.23 = (bf16[272,1024]{1,0:T(8,128)(2,1)S(1)}, bf16[272,1024]{1,0:T(8,128)(2,1)S(1)}, u32[]{:S(2)}, u32[]{:S(2)}) collective-permute-start(bf16[272,1024]{1,0:T(8,128)(2,1)S(1)} %encode.2.refs_0_), channel_id=1, source_target_pairs={{0,12},{1,13},{2,14},{3,15},{4,0},{5,1},{6,2},{7,3},{8,4},{9,5},{1... | collective-permute-start | bytes 1671176 | tf_op jit(solution)/shard_map/ppermute | solution.py:443
  65.1 7.5 %collective-permute-done.19.refs_1_ = bf16[144,1024]{1,0:T(8,128)(2,1)S(1)} collective-permute-done((bf16[144,1024]{1,0:T(8,128)(2,1)S(1)}, bf16[144,1024]{1,0:T(8,128)(2,1)S(1)}, u32[]{:S(2)}, u32[]{:S(2)}) %collective-permute-start.19) | collective-permute-done | bytes 294944 | tf_op jit(solution)/shard_map/ppermute | solution.py:443
  72.6 7.5 %encode.3.refs_1_ = bf16[272,1024]{1,0:T(8,128)(2,1)S(1)} custom-call(s32[16]{0:T(128)S(1)} %dynamic-slice_bitcast_fusion.where_ref, bf16[144,1024]{1,0:T(8,128)(2,1)S(1)} %collective-permute-done.8.refs_2_.refs_0_, bf16[144,1024]{1,0:T(8,128)(2,1)S(1)} %collective-permute-done.19.refs_1_, f32[1,1024]{1,0:T(1,128)S(1)} %bitcast.47, ...), custom_call_target="tpu_custom_call" | custom-call | flops 8000000000 | bytes 8388608 | tf_op jit(solution)/shard_map/encode/pallas_call | solution.py:230
  80.0 3.1 %collective-permute-start.20 = (bf16[272,1024]{1,0:T(8,128)(2,1)S(1)}, bf16[272,1024]{1,0:T(8,128)(2,1)S(1)}, u32[]{:S(2)}, u32[]{:S(2)}) collective-permute-start(bf16[272,1024]{1,0:T(8,128)(2,1)S(1)} %encode.3.refs_1_), channel_id=1, source_target_pairs={{0,12},{1,13},{2,14},{3,15},{4,0},{5,1},{6,2},{7,3},{8,4},{9,5},{1... | collective-permute-start | bytes 1671176 | tf_op jit(solution)/shard_map/ppermute | solution.py:443
  83.1 6.2 %decode.4.refs_7_ = bf16[512,1024]{1,0:T(8,128)(2,1)} custom-call(s32[4]{0:T(128)S(1)} %pad_add_fusion.3.micro_ref, s32[64]{0:T(128)S(1)} %reshape.23.tgt_ref, bf16[272,1024]{1,0:T(8,128)(2,1)S(1)} %encode.2.refs_0_, bf16[272,1024]{1,0:T(8,128)(2,1)S(1)} %encode.3.refs_1_, bf16[512,1024]{1,0:T(8,128)(2,1)S(1)} %project_query.1.refs_0_.refs_2_, ...), custom_call_target="tpu_custom_call" | custom-call | flops 8589934592 | bytes 8388608 | tf_op jit(solution)/shard_map/decode/pallas_call | solution.py:344
  89.3 5.6 %collective-permute-done.20.refs_1_ = bf16[272,1024]{1,0:T(8,128)(2,1)S(1)} collective-permute-done((bf16[272,1024]{1,0:T(8,128)(2,1)S(1)}, bf16[272,1024]{1,0:T(8,128)(2,1)S(1)}, u32[]{:S(2)}, u32[]{:S(2)}) %collective-permute-start.20) | collective-permute-done | bytes 557088 | tf_op jit(solution)/shard_map/ppermute | solution.py:443
  94.9 3.7 %collective-permute-start.21 = (bf16[272,1024]{1,0:T(8,128)(2,1)S(1)}, bf16[272,1024]{1,0:T(8,128)(2,1)S(1)}, u32[]{:S(2)}, u32[]{:S(2)}) collective-permute-start(bf16[272,1024]{1,0:T(8,128)(2,1)S(1)} %collective-permute-done.20.refs_1_), channel_id=1, source_target_pairs={{0,12},{1,13},{2,14},{3,15},{4,0},{5,1},{6,2},{7,3},{8,4},{9,5},{1... | collective-permute-start | bytes 1671176 | tf_op jit(solution)/shard_map/ppermute | solution.py:443
  98.6 6.2 %decode.5.refs_7_ = bf16[512,1024]{1,0:T(8,128)(2,1)} custom-call(s32[4]{0:T(128)S(1)} %pad_add_fusion.2.micro_ref, s32[64]{0:T(128)S(1)} %reshape.23.tgt_ref, bf16[272,1024]{1,0:T(8,128)(2,1)S(1)} %collective-permute-done.17.refs_0_, bf16[272,1024]{1,0:T(8,128)(2,1)S(1)} %collective-permute-done.23.refs_1_, ...), custom_call_target="tpu_custom_call", output_to_operand_aliasing={{}: (9, {})} | custom-call | flops 8589934592 | bytes 8388608 | tf_op jit(solution)/shard_map/decode/pallas_call | solution.py:344
  104.8 6.2 %decode.6.refs_7_ = bf16[512,1024]{1,0:T(8,128)(2,1)} custom-call(s32[4]{0:T(128)S(1)} %pad_add_fusion.1.micro_ref, s32[64]{0:T(128)S(1)} %reshape.23.tgt_ref, bf16[272,1024]{1,0:T(8,128)(2,1)S(1)} %collective-permute-done.22.refs_0_, bf16[272,1024]{1,0:T(8,128)(2,1)S(1)} %collective-permute-done.20.refs_1_, ...), custom_call_target="tpu_custom_call", output_to_operand_aliasing={{}: (9, {})} | custom-call | flops 8589934592 | bytes 8388608 | tf_op jit(solution)/shard_map/decode/pallas_call | solution.py:344
  111.0 1.9 %collective-permute-done.18.refs_0_ = bf16[272,1024]{1,0:T(8,128)(2,1)S(1)} collective-permute-done((bf16[272,1024]{1,0:T(8,128)(2,1)S(1)}, bf16[272,1024]{1,0:T(8,128)(2,1)S(1)}, u32[]{:S(2)}, u32[]{:S(2)}) %collective-permute-start.18) | collective-permute-done | bytes 557088 | tf_op jit(solution)/shard_map/ppermute | solution.py:443
  112.9 6.2 %decode.7 = bf16[512,1024]{1,0:T(8,128)(2,1)} custom-call(s32[4]{0:T(128)S(1)} %pad_add_fusion.micro_ref, s32[64]{0:T(128)S(1)} %reshape.23.tgt_ref, bf16[272,1024]{1,0:T(8,128)(2,1)S(1)} %collective-permute-done.18.refs_0_, bf16[272,1024]{1,0:T(8,128)(2,1)S(1)} %collective-permute-done.21.refs_1_, ...), custom_call_target="tpu_custom_call", output_to_operand_aliasing={{}: (9, {})} | custom-call | flops 8589934592 | bytes 8388608 | tf_op jit(solution)/shard_map/decode/pallas_call | solution.py:344
  (47 shorter events, 0.2 us)
Async XLA Ops:
  2.9 11.3 %collective-permute-start = (bf16[64,3072]{1,0:T(8,128)(2,1)}, bf16[64,3072]{1,0:T(8,128)(2,1)S(1)}, u32[]{:S(2)}, u32[]{:S(2)}) collective-permute-start(bf16[64,3072]{1,0:T(8,128)(2,1)} %get-tuple-element.8.value_ref.refs_5_), channel_id=1, source_target_pairs={{0,128},{16,144},{32,160},{48,176},{64,192},{80,208},{96,224},{112... | collective-permute-start | bytes 1179656 | tf_op jit(solution)/shard_map/ppermute | solution.py:442
  4.9 19.8 %collective-permute-start.2 = (bf16[64,3072]{1,0:T(8,128)(2,1)}, bf16[64,3072]{1,0:T(8,128)(2,1)S(1)}, u32[]{:S(2)}, u32[]{:S(2)}) collective-permute-start(bf16[64,3072]{1,0:T(8,128)(2,1)} %get-tuple-element.8.value_ref.refs_5_), channel_id=1, source_target_pairs={{0,32},{16,48},{32,64},{48,80},{64,96},{80,112},{96,0},{112,16},{1... | collective-permute-start | bytes 1179656 | tf_op jit(solution)/shard_map/ppermute | solution.py:442
  5.4 20.9 %collective-permute-start.3 = (bf16[64,3072]{1,0:T(8,128)(2,1)}, bf16[64,3072]{1,0:T(8,128)(2,1)S(1)}, u32[]{:S(2)}, u32[]{:S(2)}) collective-permute-start(bf16[64,3072]{1,0:T(8,128)(2,1)} %get-tuple-element.8.value_ref.refs_5_), channel_id=1, source_target_pairs={{0,96},{16,112},{32,0},{48,16},{64,32},{80,48},{96,64},{112,80},{1... | collective-permute-start | bytes 1179656 | tf_op jit(solution)/shard_map/ppermute | solution.py:442
  14.2 25.4 %collective-permute-start.5 = (bf16[64,3072]{1,0:T(8,128)(2,1)S(1)}, bf16[64,3072]{1,0:T(8,128)(2,1)S(1)}, u32[]{:S(2)}, u32[]{:S(2)}) collective-permute-start(bf16[64,3072]{1,0:T(8,128)(2,1)S(1)} %collective-permute-done.refs_0_.refs_6_), channel_id=1, source_target_pairs={{0,96},{16,112},{32,0},{48,16},{64,32},{80,48},{96,64},{112,80},{1... | collective-permute-start | bytes 1179656 | tf_op jit(solution)/shard_map/ppermute | solution.py:442
  15.0 25.1 %collective-permute-start.4 = (bf16[64,3072]{1,0:T(8,128)(2,1)S(1)}, bf16[64,3072]{1,0:T(8,128)(2,1)S(1)}, u32[]{:S(2)}, u32[]{:S(2)}) collective-permute-start(bf16[64,3072]{1,0:T(8,128)(2,1)S(1)} %collective-permute-done.refs_0_.refs_6_), channel_id=1, source_target_pairs={{0,32},{16,48},{32,64},{48,80},{64,96},{80,112},{96,0},{112,16},{1... | collective-permute-start | bytes 1179656 | tf_op jit(solution)/shard_map/ppermute | solution.py:442
  17.5 1.0 copy-start.1
  18.4 17.4 %collective-permute-start.8 = (bf16[144,1024]{1,0:T(8,128)(2,1)S(1)}, bf16[144,1024]{1,0:T(8,128)(2,1)S(1)}, u32[]{:S(2)}, u32[]{:S(2)}) collective-permute-start(bf16[144,1024]{1,0:T(8,128)(2,1)S(1)} %pass_after.3), channel_id=1, source_target_pairs={{0,3},{1,0},{2,1},{3,2},{4,7},{5,4},{6,5},{7,6},{8,11},{9,8},{10,9... | collective-permute-start | bytes 884744 | tf_op jit(solution)/shard_map/ppermute | solution.py:443
  24.6 15.0 %collective-permute-start.1 = (bf16[144,1024]{1,0:T(8,128)(2,1)S(1)}, bf16[144,1024]{1,0:T(8,128)(2,1)S(1)}, u32[]{:S(2)}, u32[]{:S(2)}) collective-permute-start(bf16[144,1024]{1,0:T(8,128)(2,1)S(1)} %pass_after.3), channel_id=1, source_target_pairs={{0,1},{1,2},{2,3},{3,0},{4,5},{5,6},{6,7},{7,4},{8,9},{9,10},{10,1... | collective-permute-start | bytes 884744 | tf_op jit(solution)/shard_map/ppermute | solution.py:443
  26.3 21.4 %collective-permute-start.10 = (bf16[64,3072]{1,0:T(8,128)(2,1)S(1)}, bf16[64,3072]{1,0:T(8,128)(2,1)S(1)}, u32[]{:S(2)}, u32[]{:S(2)}) collective-permute-start(bf16[64,3072]{1,0:T(8,128)(2,1)S(1)} %collective-permute-done.refs_0_.refs_6_), channel_id=1, source_target_pairs={{0,16},{16,0},{32,48},{48,32},{64,80},{80,64},{96,112},{112,96},{1... | collective-permute-start | bytes 1179656 | tf_op jit(solution)/shard_map/ppermute | solution.py:442
  35.8 11.7 %collective-permute-start.6 = (bf16[64,3072]{1,0:T(8,128)(2,1)S(1)}, bf16[64,3072]{1,0:T(8,128)(2,1)S(1)}, u32[]{:S(2)}, u32[]{:S(2)}) collective-permute-start(bf16[64,3072]{1,0:T(8,128)(2,1)S(1)} %collective-permute-done.2.refs_7_), channel_id=1, source_target_pairs={{0,32},{16,48},{32,64},{48,80},{64,96},{80,112},{96,0},{112,16},{1... | collective-permute-start | bytes 1179656 | tf_op jit(solution)/shard_map/ppermute | solution.py:442
  39.7 8.5 %collective-permute-start.11 = (bf16[64,3072]{1,0:T(8,128)(2,1)S(1)}, bf16[64,3072]{1,0:T(8,128)(2,1)S(1)}, u32[]{:S(2)}, u32[]{:S(2)}) collective-permute-start(bf16[64,3072]{1,0:T(8,128)(2,1)S(1)} %collective-permute-done.2.refs_7_), channel_id=1, source_target_pairs={{0,16},{16,0},{32,48},{48,32},{64,80},{80,64},{96,112},{112,96},{1... | collective-permute-start | bytes 1179656 | tf_op jit(solution)/shard_map/ppermute | solution.py:442
  39.7 8.6 %collective-permute-start.12 = (bf16[64,3072]{1,0:T(8,128)(2,1)S(1)}, bf16[64,3072]{1,0:T(8,128)(2,1)S(1)}, u32[]{:S(2)}, u32[]{:S(2)}) collective-permute-start(bf16[64,3072]{1,0:T(8,128)(2,1)S(1)} %collective-permute-done.3.refs_8_), channel_id=1, source_target_pairs={{0,16},{16,0},{32,48},{48,32},{64,80},{80,64},{96,112},{112,96},{1... | collective-permute-start | bytes 1179656 | tf_op jit(solution)/shard_map/ppermute | solution.py:442
  40.2 12.3 %collective-permute-start.7 = (bf16[64,3072]{1,0:T(8,128)(2,1)S(1)}, bf16[64,3072]{1,0:T(8,128)(2,1)S(1)}, u32[]{:S(2)}, u32[]{:S(2)}) collective-permute-start(bf16[64,3072]{1,0:T(8,128)(2,1)S(1)} %collective-permute-done.5.refs_10_), channel_id=1, source_target_pairs={{0,96},{16,112},{32,0},{48,16},{64,32},{80,48},{96,64},{112,80},{1... | collective-permute-start | bytes 1179656 | tf_op jit(solution)/shard_map/ppermute | solution.py:442
  40.2 1.6 %copy-start = (bf16[1,1024,1024]{2,1,0:T(8,128)(2,1)S(1)}, bf16[1,1024,1024]{2,1,0:T(8,128)(2,1)}, u32[]{:S(2)}) copy-start(bf16[1,1024,1024]{2,1,0:T(8,128)(2,1)} %param.25) | copy-start | bytes 6291460
  41.8 1.2 %copy-start.3 = (bf16[1,16,4,8,1024]{4,3,2,1,0:T(8,128)(2,1)S(1)}, bf16[1,16,4,8,1024]{4,3,2,1,0:T(8,128)(2,1)}, u32[]{:S(2)}) copy-start(bf16[1,16,4,8,1024]{4,3,2,1,0:T(8,128)(2,1)} %param.29) | copy-start | bytes 3145732
  43.0 0.7 copy-start.6
  43.7 3.8 %copy-start.5 = (bf16[64,3072]{1,0:T(8,128)(2,1)S(1)}, bf16[64,3072]{1,0:T(8,128)(2,1)}, u32[]{:S(2)}) copy-start(bf16[64,3072]{1,0:T(8,128)(2,1)} %get-tuple-element.8.value_ref.refs_5_) | copy-start | bytes 1179652
  46.6 6.2 %copy-start.2 = (bf16[144,1024]{1,0:T(8,128)(2,1)S(1)}, bf16[144,1024]{1,0:T(8,128)(2,1)}, u32[]{:S(2)}) copy-start(bf16[144,1024]{1,0:T(8,128)(2,1)} %get-tuple-element.7.value_ref.refs_0_) | copy-start | bytes 884740
  46.7 7.6 %copy-start.10 = (bf16[31,1024]{1,0:T(8,128)(2,1)S(1)}, bf16[31,1024]{1,0:T(8,128)(2,1)}, u32[]{:S(2)}) copy-start(bf16[31,1024]{1,0:T(8,128)(2,1)} %refs_3_.3) | copy-start | bytes 190468
  46.7 7.6 %copy-start.11 = (f32[1024]{0:T(1024)S(1)}, f32[1024]{0:T(1024)}, u32[]{:S(2)}) copy-start(f32[1024]{0:T(1024)} %param.19) | copy-start | bytes 12292
  46.7 7.5 %copy-start.12 = (f32[1024]{0:T(1024)S(1)}, f32[1024]{0:T(1024)}, u32[]{:S(2)}) copy-start(f32[1024]{0:T(1024)} %param.22) | copy-start | bytes 12292
  47.5 5.3 %collective-permute-start.9 = (bf16[64,3072]{1,0:T(8,128)(2,1)S(1)}, bf16[64,3072]{1,0:T(8,128)(2,1)S(1)}, u32[]{:S(2)}, u32[]{:S(2)}) collective-permute-start(bf16[64,3072]{1,0:T(8,128)(2,1)S(1)} %pass_after.4), channel_id=1, source_target_pairs={{0,16},{16,0},{32,48},{48,32},{64,80},{80,64},{96,112},{112,96},{1... | collective-permute-start | bytes 1179656 | tf_op jit(solution)/shard_map/ppermute | solution.py:442
  47.7 5.3 %collective-permute-start.14 = (bf16[64,3072]{1,0:T(8,128)(2,1)S(1)}, bf16[64,3072]{1,0:T(8,128)(2,1)S(1)}, u32[]{:S(2)}, u32[]{:S(2)}) collective-permute-start(bf16[64,3072]{1,0:T(8,128)(2,1)S(1)} %collective-permute-done.5.refs_10_), channel_id=1, source_target_pairs={{0,16},{16,0},{32,48},{48,32},{64,80},{80,64},{96,112},{112,96},{1... | collective-permute-start | bytes 1179656 | tf_op jit(solution)/shard_map/ppermute | solution.py:442
  48.1 4.9 %collective-permute-start.13 = (bf16[64,3072]{1,0:T(8,128)(2,1)S(1)}, bf16[64,3072]{1,0:T(8,128)(2,1)S(1)}, u32[]{:S(2)}, u32[]{:S(2)}) collective-permute-start(bf16[64,3072]{1,0:T(8,128)(2,1)S(1)} %collective-permute-done.4.refs_9_), channel_id=1, source_target_pairs={{0,16},{16,0},{32,48},{48,32},{64,80},{80,64},{96,112},{112,96},{1... | collective-permute-start | bytes 1179656 | tf_op jit(solution)/shard_map/ppermute | solution.py:442
  48.3 4.8 %collective-permute-start.15 = (bf16[64,3072]{1,0:T(8,128)(2,1)S(1)}, bf16[64,3072]{1,0:T(8,128)(2,1)S(1)}, u32[]{:S(2)}, u32[]{:S(2)}) collective-permute-start(bf16[64,3072]{1,0:T(8,128)(2,1)S(1)} %collective-permute-done.6.refs_11_), channel_id=1, source_target_pairs={{0,16},{16,0},{32,48},{48,32},{64,80},{80,64},{96,112},{112,96},{1... | collective-permute-start | bytes 1179656 | tf_op jit(solution)/shard_map/ppermute | solution.py:442
  52.5 1.7 %collective-permute-start.16 = (bf16[64,3072]{1,0:T(8,128)(2,1)S(1)}, bf16[64,3072]{1,0:T(8,128)(2,1)S(1)}, u32[]{:S(2)}, u32[]{:S(2)}) collective-permute-start(bf16[64,3072]{1,0:T(8,128)(2,1)S(1)} %collective-permute-done.7.refs_12_), channel_id=1, source_target_pairs={{0,16},{16,0},{32,48},{48,32},{64,80},{80,64},{96,112},{112,96},{1... | collective-permute-start | bytes 1179656 | tf_op jit(solution)/shard_map/ppermute | solution.py:442
  52.8 19.7 %collective-permute-start.19 = (bf16[144,1024]{1,0:T(8,128)(2,1)S(1)}, bf16[144,1024]{1,0:T(8,128)(2,1)S(1)}, u32[]{:S(2)}, u32[]{:S(2)}) collective-permute-start(bf16[144,1024]{1,0:T(8,128)(2,1)S(1)} %pass_after.5), channel_id=1, source_target_pairs={{0,2},{1,3},{2,0},{3,1},{4,6},{5,7},{6,4},{7,5},{8,10},{9,11},{10,... | collective-permute-start | bytes 884744 | tf_op jit(solution)/shard_map/ppermute | solution.py:443
  61.7 21.4 %copy-start.4 = (bf16[1,16,4,8,1024]{4,3,2,1,0:T(8,128)(2,1)S(1)}, bf16[1,16,4,8,1024]{4,3,2,1,0:T(8,128)(2,1)}, u32[]{:S(2)}) copy-start(bf16[1,16,4,8,1024]{4,3,2,1,0:T(8,128)(2,1)} %param.29) | copy-start | bytes 3145732
  61.7 21.4 %copy-start.7 = (bf16[1,1024,1024]{2,1,0:T(8,128)(2,1)S(1)}, bf16[1,1024,1024]{2,1,0:T(8,128)(2,1)}, u32[]{:S(2)}) copy-start(bf16[1,1024,1024]{2,1,0:T(8,128)(2,1)} %param.26) | copy-start | bytes 6291460
  61.7 21.4 %copy-start.8 = (bf16[1,1024,1024]{2,1,0:T(8,128)(2,1)S(1)}, bf16[1,1024,1024]{2,1,0:T(8,128)(2,1)}, u32[]{:S(2)}) copy-start(bf16[1,1024,1024]{2,1,0:T(8,128)(2,1)} %param.27) | copy-start | bytes 6291460
  61.7 21.4 %copy-start.9 = (bf16[1,1024,1024]{2,1,0:T(8,128)(2,1)S(1)}, bf16[1,1024,1024]{2,1,0:T(8,128)(2,1)}, u32[]{:S(2)}) copy-start(bf16[1,1024,1024]{2,1,0:T(8,128)(2,1)} %param.28) | copy-start | bytes 6291460
  61.7 36.8 %collective-permute-start.17 = (bf16[272,1024]{1,0:T(8,128)(2,1)S(1)}, bf16[272,1024]{1,0:T(8,128)(2,1)S(1)}, u32[]{:S(2)}, u32[]{:S(2)}) collective-permute-start(bf16[272,1024]{1,0:T(8,128)(2,1)S(1)} %encode.2.refs_0_), channel_id=1, source_target_pairs={{0,4},{1,5},{2,6},{3,7},{4,8},{5,9},{6,10},{7,11},{8,12},{9,13},{1... | collective-permute-start | bytes 1671176 | tf_op jit(solution)/shard_map/ppermute | solution.py:443
  63.4 35.2 %collective-permute-start.23 = (bf16[272,1024]{1,0:T(8,128)(2,1)S(1)}, bf16[272,1024]{1,0:T(8,128)(2,1)S(1)}, u32[]{:S(2)}, u32[]{:S(2)}) collective-permute-start(bf16[272,1024]{1,0:T(8,128)(2,1)S(1)} %encode.2.refs_0_), channel_id=1, source_target_pairs={{0,12},{1,13},{2,14},{3,15},{4,0},{5,1},{6,2},{7,3},{8,4},{9,5},{1... | collective-permute-start | bytes 1671176 | tf_op jit(solution)/shard_map/ppermute | solution.py:443
  80.0 14.9 %collective-permute-start.20 = (bf16[272,1024]{1,0:T(8,128)(2,1)S(1)}, bf16[272,1024]{1,0:T(8,128)(2,1)S(1)}, u32[]{:S(2)}, u32[]{:S(2)}) collective-permute-start(bf16[272,1024]{1,0:T(8,128)(2,1)S(1)} %encode.3.refs_1_), channel_id=1, source_target_pairs={{0,12},{1,13},{2,14},{3,15},{4,0},{5,1},{6,2},{7,3},{8,4},{9,5},{1... | collective-permute-start | bytes 1671176 | tf_op jit(solution)/shard_map/ppermute | solution.py:443
  83.1 21.7 %collective-permute-start.22 = (bf16[272,1024]{1,0:T(8,128)(2,1)S(1)}, bf16[272,1024]{1,0:T(8,128)(2,1)S(1)}, u32[]{:S(2)}, u32[]{:S(2)}) collective-permute-start(bf16[272,1024]{1,0:T(8,128)(2,1)S(1)} %encode.3.refs_1_), channel_id=1, source_target_pairs={{0,4},{1,5},{2,6},{3,7},{4,8},{5,9},{6,10},{7,11},{8,12},{9,13},{1... | collective-permute-start | bytes 1671176 | tf_op jit(solution)/shard_map/ppermute | solution.py:443
  94.9 16.1 %collective-permute-start.21 = (bf16[272,1024]{1,0:T(8,128)(2,1)S(1)}, bf16[272,1024]{1,0:T(8,128)(2,1)S(1)}, u32[]{:S(2)}, u32[]{:S(2)}) collective-permute-start(bf16[272,1024]{1,0:T(8,128)(2,1)S(1)} %collective-permute-done.20.refs_1_), channel_id=1, source_target_pairs={{0,12},{1,13},{2,14},{3,15},{4,0},{5,1},{6,2},{7,3},{8,4},{9,5},{1... | collective-permute-start | bytes 1671176 | tf_op jit(solution)/shard_map/ppermute | solution.py:443
  98.6 14.3 %collective-permute-start.18 = (bf16[272,1024]{1,0:T(8,128)(2,1)S(1)}, bf16[272,1024]{1,0:T(8,128)(2,1)S(1)}, u32[]{:S(2)}, u32[]{:S(2)}) collective-permute-start(bf16[272,1024]{1,0:T(8,128)(2,1)S(1)} %collective-permute-done.17.refs_0_), channel_id=1, source_target_pairs={{0,4},{1,5},{2,6},{3,7},{4,8},{5,9},{6,10},{7,11},{8,12},{9,13},{1... | collective-permute-start | bytes 1671176 | tf_op jit(solution)/shard_map/ppermute | solution.py:443

commit v2 on v1

--- a/solution.py
+++ b/solution.py
@@ -56,14 +56,31 @@
     return utt, slot - start
 
 
-def prepare_kernel(lens_ref, frames_hbm, w_in_hbm, w_out_hbm, own_ref, out_ref, frames_ref, sems):
+def join_kernel(w_in_hbm, w_out_hbm, own_ref, sems):
     loads = [
         pltpu.make_async_copy(w_in_hbm, own_ref.at[:, pl.ds(0, 2 * D)], sems.at[0]),
         pltpu.make_async_copy(w_out_hbm, own_ref.at[:, pl.ds(2 * D, D)], sems.at[1]),
-        pltpu.make_async_copy(frames_hbm, frames_ref, sems.at[2]),
     ]
     for load in loads:
         load.start()
+    for load in loads:
+        load.wait()
+
+
+def join_shards(w_in, w_out):
+    return pl.pallas_call(
+        join_kernel,
+        out_shape=jax.ShapeDtypeStruct((w_in.shape[0], 3 * D), BF),
+        in_specs=[HBM, HBM],
+        out_specs=VM,
+        scratch_shapes=[pltpu.SemaphoreType.DMA((2,))],
+        compiler_params=params(60),
+        cost_estimate=cost(0, 800_000),
+        name="join_shards",
+    )(w_in, w_out)
+
+
+def pack_kernel(lens_ref, frames_ref, own_hbm, out_ref):
     slot = lax.broadcasted_iota(jnp.int32, (TOT, UTT * FR), 0)
     lane = lax.broadcasted_iota(jnp.int32, (TOT, UTT * FR), 1)
     utt, frame = slot_place(slot, lens_ref)
@@ -72,34 +89,26 @@
     kind = lax.broadcasted_iota(jnp.int32, (EXTRA, TOT), 0)
     out_ref[TOT:, :TOT] = jnp.where(kind == 0, frame, utt).astype(F32).astype(BF)
     out_ref[TOT:, TOT:] = jnp.zeros((EXTRA, D - TOT), BF)
-    loads[2].wait()
     for j in range(D // 256):
         cols = slice(j * 256, (j + 1) * 256)
         out_ref[:TOT, cols] = jnp.dot(
             pick, frames_ref[:, cols], preferred_element_type=F32
         ).astype(BF)
-    loads[0].wait()
-    loads[1].wait()
-
-
-def prepare(lens, frames, w_in, w_out):
-    depth = w_in.shape[0]
+
+
+def pack_frames(lens, frames, after):
     return pl.pallas_call(
-        prepare_kernel,
-        out_shape=(
-            jax.ShapeDtypeStruct((depth, 3 * D), BF),
-            jax.ShapeDtypeStruct((TOT + EXTRA, D), BF),
-        ),
-        in_specs=[SM, HBM, HBM, HBM],
-        out_specs=(VM, VM),
-        scratch_shapes=[pltpu.VMEM((UTT * FR, D), BF), pltpu.SemaphoreType.DMA((3,))],
-        compiler_params=params(60),
-        cost_estimate=cost(50_000_000, 1_400_000),
-        name="prepare",
-    )(lens, frames, w_in, w_out)
-
-
-def query_kernel(hidden_ref, gain_ref, w_ref, out_ref, normed):
+        pack_kernel,
+        out_shape=jax.ShapeDtypeStruct((TOT + EXTRA, D), BF),
+        in_specs=[SM, VM, HBM],
+        out_specs=VM,
+        compiler_params=params(4),
+        cost_estimate=cost(50_000_000, 600_000),
+        name="pack_frames",
+    )(lens, frames, after)
+
+
+def query_kernel(hidden_ref, gain_ref, w_ref, after_hbm, out_ref, normed):
     @pl.loop(0, hidden_ref.shape[0] // 64)
     def _(i):
         for r in range(0, 64, 16):
@@ -112,18 +121,18 @@
         out_ref[:, cols] = (q * (HEAD**-0.5)).astype(BF)
 
 
-def project_query(hidden, gain, w):
+def project_query(hidden, gain, w, after):
     rows = hidden.shape[0]
     return pl.pallas_call(
         query_kernel,
         out_shape=jax.ShapeDtypeStruct((rows, D), BF),
-        in_specs=[VM, VM, VM],
+        in_specs=[VM, VM, VM, HBM],
         out_specs=VM,
         scratch_shapes=[pltpu.VMEM((rows, D), BF)],
         compiler_params=params(8),
         cost_estimate=cost(2 * rows * D * D, 4 << 20),
         name="project_query",
-    )(hidden, gain, w)
+    )(hidden, gain, w, after)
 
 
 def order_columns(dst, src, where_ref):
@@ -444,21 +453,20 @@
     where = jnp.array(shard_table(), jnp.int32)[lax.axis_index("dp")]
     micros = jnp.array(micro_table(), jnp.int32)[lax.axis_index("section")].reshape(4, 4)
 
-    own, packed = prepare(
-        frame_lens.reshape(UTT), frames.reshape(UTT * FR, D), w_in, w_out
-    )
+    own = join_shards(w_in, w_out)
     pair = across(own, TO_PAIR)
-    own_r, own_l = across(own, TO_LEFT), across(own, TO_RIGHT)
-    source = hidden.reshape(-1, D)
-    query = project_query(source, dec_gain, w_query[0])
+    own_l, own_r = across(own, TO_RIGHT), across(own, TO_LEFT)
     pair_l, pair_r = across(pair, TO_RIGHT), across(pair, TO_LEFT)
     own_2, pair_2 = across(own_l, TO_RIGHT), across(pair_r, TO_LEFT)
-    ready = pass_after(packed, pair)
-    from_b, from_a = along(ready, 0, 1), along(ready, 0, -1)
     shards = [own, pair, own_l, own_r, pair_l, pair_r, own_2, pair_2]
-    turn = [pass_after(own, query, from_b, from_a)] + shards[1:]
+
+    packed = pack_frames(frame_lens.reshape(UTT), frames.reshape(UTT * FR, D), pair)
+    from_b, from_a = along(packed, 0, 1), along(packed, 0, -1)
+    source = hidden.reshape(-1, D)
+    turn = list(shards)
+    turn[1] = pass_after(turn[1], from_b, from_a)
+    from_2 = along(pass_after(packed, from_a), 0, 2)
     shards += [across(v, TO_CORE) for v in turn]
-    from_2 = along(pass_after(packed, from_a), 0, 2)
 
     def encode_pair(first, second):
         return encode(
@@ -471,6 +479,7 @@
         )
 
     mem_a = encode_pair(packed, from_b)
+    query = project_query(source, dec_gain, w_query[0], mem_a)
     mem_b = encode_pair(from_a, from_2)
 
     a_from_l, a_from_r = along(mem_a, 1, 0), along(mem_a, -1, 0)

time: 120 us -> 119 us (level)
  local copies, waits for them, and re-layouts: 6.96 us -> 4.09 us
  Pallas kernels: 45.6 us -> 47 us
    ppermute x15, waiting for transfers between devices: 12.3 us -> 17.3 us  [body(): across = lambda v, perm: lax.ppermute(v, 'dp', perm)]
    ppermute x9, waiting for transfers between devices: 27.9 us -> 23.9 us  [body(): along = lambda v, dy, dz: lax.ppermute(v, 'section', section_perm(dy, dz))]
    unnamed x27 -> x25, local copies, waits for them, and re-layouts: 5.27 us -> 2.44 us
    pallas_call x2, Pallas kernels: 14.9 us -> 16.8 us  [encode(): pl.pallas_call(functools.partial(encode_kernel, len(shards)), out_shape=j...]
    pallas_call x1 -> x2, Pallas kernels: 2.89 us -> 2.54 us  [the longest x1 1.78 us: join_shards(): pl.pallas_call(join_kernel, out_shape=jax.ShapeDtypeStruct((w_in.shape[0]...]
  transfers between devices with their start and end apart: 24 -> 24, of which waited for: 8 -> 8; matrix products, arithmetic and copies ran while one was open for 2% -> 2% of each run, Pallas kernels for 31% -> 33%
where the time goes in v2:
time: 119 us
  Pallas kernels  47 us (39%)
  waiting for transfers between devices  41.2 us (35%)
  starting transfers between devices  25.7 us (22%)
  local copies, waits for them, and re-layouts  4.09 us (3%)
    pallas_call x4, Pallas kernels, decode(): pl.pallas_call(functools.partial(decode_kernel, len(mems), aliased), out_...  24.7 us
    ppermute x9, waiting for transfers between devices, body(): along = lambda v, dy, dz: lax.ppermute(v, 'section', section_perm(dy, dz))  23.9 us
    ppermute x15, waiting for transfers between devices, body(): across = lambda v, perm: lax.ppermute(v, 'dp', perm)  17.3 us
    pallas_call x2, Pallas kernels, encode(): pl.pallas_call(functools.partial(encode_kernel, len(shards)), out_shape=j...  16.8 us
    ppermute x9, starting transfers between devices, body(): along = lambda v, dy, dz: lax.ppermute(v, 'section', section_perm(dy, dz))  16.6 us
    ppermute x15, starting transfers between devices, body(): across = lambda v, perm: lax.ppermute(v, 'dp', perm)  9.1 us
    pallas_call x1, Pallas kernels, project_query(): pl.pallas_call(query_kernel, out_shape=jax.ShapeDtypeStruct((rows, D), BF...  2.94 us
    unnamed x25, local copies, waits for them, and re-layouts  2.44 us
  transfers between devices with their start and end apart: 24, of which 8 were waited for; matrix products, arithmetic and copies ran while one was open for 2% of the time, Pallas kernels for 33%

profile of v2, /device:TPU:6, one launch (start us, length us, event | category | flops | bytes accessed | tf_op | source)
XLA Modules:
  0.0 118.7 jit_solution(8981774706413469018)
XLA Ops:
  0.0 1.8 %join_shards.1.refs_5_ = bf16[64,3072]{1,0:T(8,128)(2,1)} custom-call(bf16[64,2048]{1,0:T(8,128)(2,1)} %w_in_hbm.1, bf16[64,1024]{1,0:T(8,128)(2,1)} %w_out_hbm.1), custom_call_target="tpu_custom_call" | custom-call | bytes 800000 | tf_op jit(solution)/shard_map/join_shards/pallas_call | solution.py:71
  1.8 0.0 copy-start.2
  1.8 2.0 %collective-permute-start = (bf16[64,3072]{1,0:T(8,128)(2,1)}, bf16[64,3072]{1,0:T(8,128)(2,1)S(1)}, u32[]{:S(2)}, u32[]{:S(2)}) collective-permute-start(bf16[64,3072]{1,0:T(8,128)(2,1)} %join_shards.1.refs_5_), channel_id=1, source_target_pairs={{0,128},{16,144},{32,160},{48,176},{64,192},{80,208},{96,224},{112... | collective-permute-start | bytes 1179656 | tf_op jit(solution)/shard_map/ppermute | solution.py:451
  3.8 0.5 collective-permute-start.2
  4.3 1.5 %collective-permute-start.3 = (bf16[64,3072]{1,0:T(8,128)(2,1)}, bf16[64,3072]{1,0:T(8,128)(2,1)S(1)}, u32[]{:S(2)}, u32[]{:S(2)}) collective-permute-start(bf16[64,3072]{1,0:T(8,128)(2,1)} %join_shards.1.refs_5_), channel_id=1, source_target_pairs={{0,96},{16,112},{32,0},{48,16},{64,32},{80,48},{96,64},{112,80},{1... | collective-permute-start | bytes 1179656 | tf_op jit(solution)/shard_map/ppermute | solution.py:451
  5.8 7.3 %collective-permute-done.own_hbm.value_ref.refs_6_ = bf16[64,3072]{1,0:T(8,128)(2,1)S(1)} collective-permute-done((bf16[64,3072]{1,0:T(8,128)(2,1)}, bf16[64,3072]{1,0:T(8,128)(2,1)S(1)}, u32[]{:S(2)}, u32[]{:S(2)}) %collective-permute-start) | collective-permute-done | bytes 393248 | tf_op jit(solution)/shard_map/ppermute | solution.py:451
  13.1 0.8 collective-permute-start.5
  14.0 1.0 copy-done.3
  14.9 0.7 copy-done.5
  15.6 0.8 pack_frames.1.refs_0_.value_ref
  16.4 6.2 %collective-permute-start.9 = (bf16[144,1024]{1,0:T(8,128)(2,1)S(1)}, bf16[144,1024]{1,0:T(8,128)(2,1)S(1)}, u32[]{:S(2)}, u32[]{:S(2)}) collective-permute-start(bf16[144,1024]{1,0:T(8,128)(2,1)S(1)} %pack_frames.1.refs_0_.value_ref), channel_id=1, source_target_pairs={{0,3},{1,0},{2,1},{3,2},{4,7},{5,4},{6,5},{7,6},{8,11},{9,8},{10,9... | collective-permute-start | bytes 884744 | tf_op jit(solution)/shard_map/ppermute | solution.py:452
  22.6 2.5 %collective-permute-start.4 = (bf16[64,3072]{1,0:T(8,128)(2,1)S(1)}, bf16[64,3072]{1,0:T(8,128)(2,1)}, u32[]{:S(2)}, u32[]{:S(2)}) collective-permute-start(bf16[64,3072]{1,0:T(8,128)(2,1)S(1)} %collective-permute-done.own_hbm.value_ref.refs_6_), channel_id=1, source_target_pairs={{0,32},{16,48},{32,64},{48,80},{64,96},{80,112},{96,0},{112,16},{1... | collective-permute-start | bytes 1179656 | tf_op jit(solution)/shard_map/ppermute | solution.py:451
  25.1 0.1 collective-permute-start.6
  25.2 8.9 %collective-permute-done.9.refs_1_.refs_0_ = bf16[144,1024]{1,0:T(8,128)(2,1)S(1)} collective-permute-done((bf16[144,1024]{1,0:T(8,128)(2,1)S(1)}, bf16[144,1024]{1,0:T(8,128)(2,1)S(1)}, u32[]{:S(2)}, u32[]{:S(2)}) %collective-permute-start.9) | collective-permute-done | bytes 294944 | tf_op jit(solution)/shard_map/ppermute | solution.py:452
  34.0 3.8 %collective-permute-done.1.refs_0_.refs_1_ = bf16[144,1024]{1,0:T(8,128)(2,1)S(1)} collective-permute-done((bf16[144,1024]{1,0:T(8,128)(2,1)S(1)}, bf16[144,1024]{1,0:T(8,128)(2,1)S(1)}, u32[]{:S(2)}, u32[]{:S(2)}) %collective-permute-start.1) | collective-permute-done | bytes 294944 | tf_op jit(solution)/shard_map/ppermute | solution.py:452
  37.9 0.5 collective-permute-start.7
  38.4 0.7 dynamic-slice_reduce_fusion
  39.1 0.1 reshape_squeeze.3
  39.2 0.8 copy.21
  40.0 0.1 reshape.23.tgt_ref
  40.1 0.7 dynamic-slice_bitcast_fusion.where_ref
  40.8 0.1 slice_bitcast_fusion.1
  40.9 0.3 collective-permute-start.10
  41.2 0.3 collective-permute-start.14
  41.5 0.2 collective-permute-start.13
  41.7 0.3 collective-permute-start.15
  42.0 8.7 %collective-permute-done.7.refs_12_ = bf16[64,3072]{1,0:T(8,128)(2,1)} collective-permute-done((bf16[64,3072]{1,0:T(8,128)(2,1)S(1)}, bf16[64,3072]{1,0:T(8,128)(2,1)}, u32[]{:S(2)}, u32[]{:S(2)}) %collective-permute-start.7) | collective-permute-done | bytes 393248 | tf_op jit(solution)/shard_map/ppermute | solution.py:451
  50.7 0.1 pad_add_fusion.3.micro_ref
  50.8 0.1 pad_add_fusion.2.micro_ref
  50.9 0.1 pad_add_fusion.1.micro_ref
  50.9 0.1 pad_add_fusion.micro_ref
  51.1 0.3 collective-permute-start.19
  51.4 1.3 %collective-permute-done.16.refs_20_ = bf16[64,3072]{1,0:T(8,128)(2,1)S(1)} collective-permute-done((bf16[64,3072]{1,0:T(8,128)(2,1)}, bf16[64,3072]{1,0:T(8,128)(2,1)S(1)}, u32[]{:S(2)}, u32[]{:S(2)}) %collective-permute-start.16) | collective-permute-done | bytes 393248 | tf_op jit(solution)/shard_map/ppermute | solution.py:451
  52.7 8.3 %encode.2.after_hbm.refs_0_ = bf16[272,1024]{1,0:T(8,128)(2,1)S(1)} custom-call(s32[16]{0:T(128)S(1)} %dynamic-slice_bitcast_fusion.where_ref, bf16[144,1024]{1,0:T(8,128)(2,1)S(1)} %pack_frames.1.refs_0_.value_ref, bf16[144,1024]{1,0:T(8,128)(2,1)S(1)} %collective-permute-done.1.refs_0_.refs_1_, f32[1,1024]{1,0:T(1,128)S(1)} %bitcast.48, ...), custom_call_target="tpu_custom_call" | custom-call | flops 8000000000 | bytes 8388608 | tf_op jit(solution)/shard_map/encode/pallas_call | solution.py:239
  61.0 0.0 copy-start.4
  61.0 1.7 %collective-permute-start.17 = (bf16[272,1024]{1,0:T(8,128)(2,1)S(1)}, bf16[272,1024]{1,0:T(8,128)(2,1)S(1)}, u32[]{:S(2)}, u32[]{:S(2)}) collective-permute-start(bf16[272,1024]{1,0:T(8,128)(2,1)S(1)} %encode.2.after_hbm.refs_0_), channel_id=1, source_target_pairs={{0,4},{1,5},{2,6},{3,7},{4,8},{5,9},{6,10},{7,11},{8,12},{9,13},{1... | collective-permute-start | bytes 1671176 | tf_op jit(solution)/shard_map/ppermute | solution.py:452
  62.7 1.7 %collective-permute-start.23 = (bf16[272,1024]{1,0:T(8,128)(2,1)S(1)}, bf16[272,1024]{1,0:T(8,128)(2,1)S(1)}, u32[]{:S(2)}, u32[]{:S(2)}) collective-permute-start(bf16[272,1024]{1,0:T(8,128)(2,1)S(1)} %encode.2.after_hbm.refs_0_), channel_id=1, source_target_pairs={{0,12},{1,13},{2,14},{3,15},{4,0},{5,1},{6,2},{7,3},{8,4},{9,5},{1... | collective-permute-start | bytes 1671176 | tf_op jit(solution)/shard_map/ppermute | solution.py:452
  64.4 6.6 %collective-permute-done.19.refs_1_ = bf16[144,1024]{1,0:T(8,128)(2,1)S(1)} collective-permute-done((bf16[144,1024]{1,0:T(8,128)(2,1)S(1)}, bf16[144,1024]{1,0:T(8,128)(2,1)S(1)}, u32[]{:S(2)}, u32[]{:S(2)}) %collective-permute-start.19) | collective-permute-done | bytes 294944 | tf_op jit(solution)/shard_map/ppermute | solution.py:452
  71.0 8.5 %encode.3.refs_1_ = bf16[272,1024]{1,0:T(8,128)(2,1)S(1)} custom-call(s32[16]{0:T(128)S(1)} %dynamic-slice_bitcast_fusion.where_ref, bf16[144,1024]{1,0:T(8,128)(2,1)S(1)} %collective-permute-done.9.refs_1_.refs_0_, bf16[144,1024]{1,0:T(8,128)(2,1)S(1)} %collective-permute-done.19.refs_1_, f32[1,1024]{1,0:T(1,128)S(1)} %bitcast.49, ...), custom_call_target="tpu_custom_call" | custom-call | flops 8000000000 | bytes 8388608 | tf_op jit(solution)/shard_map/encode/pallas_call | solution.py:239
  79.5 3.1 %collective-permute-start.20 = (bf16[272,1024]{1,0:T(8,128)(2,1)S(1)}, bf16[272,1024]{1,0:T(8,128)(2,1)S(1)}, u32[]{:S(2)}, u32[]{:S(2)}) collective-permute-start(bf16[272,1024]{1,0:T(8,128)(2,1)S(1)} %encode.3.refs_1_), channel_id=1, source_target_pairs={{0,12},{1,13},{2,14},{3,15},{4,0},{5,1},{6,2},{7,3},{8,4},{9,5},{1... | collective-permute-start | bytes 1671176 | tf_op jit(solution)/shard_map/ppermute | solution.py:452
  82.6 2.9 %project_query.1.refs_2_ = bf16[512,1024]{1,0:T(8,128)(2,1)S(1)} custom-call(bf16[512,1024]{1,0:T(8,128)(2,1)S(1)} %bitcast.29, f32[1,1024]{1,0:T(1,128)S(1)} %copy-done.4, bf16[1024,1024]{1,0:T(8,128)(2,1)S(1)} %bitcast.28, bf16[272,1024]{1,0:T(8,128)(2,1)S(1)} %encode.2.after_hbm.refs_0_), custom_call_target="tpu_custom_call" | custom-call | flops 1073741824 | bytes 4194304 | tf_op jit(solution)/shard_map/project_query/pallas_call | solution.py:126
  85.6 6.2 %decode.4.refs_7_ = bf16[512,1024]{1,0:T(8,128)(2,1)} custom-call(s32[4]{0:T(128)S(1)} %pad_add_fusion.3.micro_ref, s32[64]{0:T(128)S(1)} %reshape.23.tgt_ref, bf16[272,1024]{1,0:T(8,128)(2,1)S(1)} %encode.2.after_hbm.refs_0_, bf16[272,1024]{1,0:T(8,128)(2,1)S(1)} %encode.3.refs_1_, bf16[512,1024]{1,0:T(8,128)(2,1)S(1)} %project_query.1.refs_2_, ...), custom_call_target="tpu_custom_call" | custom-call | flops 8589934592 | bytes 8388608 | tf_op jit(solution)/shard_map/decode/pallas_call | solution.py:353
  91.8 2.6 %collective-permute-done.20.refs_1_ = bf16[272,1024]{1,0:T(8,128)(2,1)S(1)} collective-permute-done((bf16[272,1024]{1,0:T(8,128)(2,1)S(1)}, bf16[272,1024]{1,0:T(8,128)(2,1)S(1)}, u32[]{:S(2)}, u32[]{:S(2)}) %collective-permute-start.20) | collective-permute-done | bytes 557088 | tf_op jit(solution)/shard_map/ppermute | solution.py:452
  94.3 3.7 %collective-permute-start.21 = (bf16[272,1024]{1,0:T(8,128)(2,1)S(1)}, bf16[272,1024]{1,0:T(8,128)(2,1)S(1)}, u32[]{:S(2)}, u32[]{:S(2)}) collective-permute-start(bf16[272,1024]{1,0:T(8,128)(2,1)S(1)} %collective-permute-done.20.refs_1_), channel_id=1, source_target_pairs={{0,12},{1,13},{2,14},{3,15},{4,0},{5,1},{6,2},{7,3},{8,4},{9,5},{1... | collective-permute-start | bytes 1671176 | tf_op jit(solution)/shard_map/ppermute | solution.py:452
  98.0 6.1 %decode.5.refs_7_ = bf16[512,1024]{1,0:T(8,128)(2,1)} custom-call(s32[4]{0:T(128)S(1)} %pad_add_fusion.2.micro_ref, s32[64]{0:T(128)S(1)} %reshape.23.tgt_ref, bf16[272,1024]{1,0:T(8,128)(2,1)S(1)} %collective-permute-done.17.refs_0_, bf16[272,1024]{1,0:T(8,128)(2,1)S(1)} %collective-permute-done.23.refs_1_, ...), custom_call_target="tpu_custom_call", output_to_operand_aliasing={{}: (9, {})} | custom-call | flops 8589934592 | bytes 8388608 | tf_op jit(solution)/shard_map/decode/pallas_call | solution.py:353
  104.2 6.2 %decode.6.refs_7_ = bf16[512,1024]{1,0:T(8,128)(2,1)} custom-call(s32[4]{0:T(128)S(1)} %pad_add_fusion.1.micro_ref, s32[64]{0:T(128)S(1)} %reshape.23.tgt_ref, bf16[272,1024]{1,0:T(8,128)(2,1)S(1)} %collective-permute-done.22.refs_0_, bf16[272,1024]{1,0:T(8,128)(2,1)S(1)} %collective-permute-done.20.refs_1_, ...), custom_call_target="tpu_custom_call", output_to_operand_aliasing={{}: (9, {})} | custom-call | flops 8589934592 | bytes 8388608 | tf_op jit(solution)/shard_map/decode/pallas_call | solution.py:353
  110.4 2.0 %collective-permute-done.18.refs_0_ = bf16[272,1024]{1,0:T(8,128)(2,1)S(1)} collective-permute-done((bf16[272,1024]{1,0:T(8,128)(2,1)S(1)}, bf16[272,1024]{1,0:T(8,128)(2,1)S(1)}, u32[]{:S(2)}, u32[]{:S(2)}) %collective-permute-start.18) | collective-permute-done | bytes 557088 | tf_op jit(solution)/shard_map/ppermute | solution.py:452
  112.4 6.2 %decode.7 = bf16[512,1024]{1,0:T(8,128)(2,1)} custom-call(s32[4]{0:T(128)S(1)} %pad_add_fusion.micro_ref, s32[64]{0:T(128)S(1)} %reshape.23.tgt_ref, bf16[272,1024]{1,0:T(8,128)(2,1)S(1)} %collective-permute-done.18.refs_0_, bf16[272,1024]{1,0:T(8,128)(2,1)S(1)} %collective-permute-done.21.refs_1_, ...), custom_call_target="tpu_custom_call", output_to_operand_aliasing={{}: (9, {})} | custom-call | flops 8589934592 | bytes 8388608 | tf_op jit(solution)/shard_map/decode/pallas_call | solution.py:353
  (45 shorter events, 0.2 us)
Async XLA Ops:
  0.0 52.7 %copy-start.10 = (f32[1024]{0:T(1024)S(1)}, f32[1024]{0:T(1024)}, u32[]{:S(2)}) copy-start(f32[1024]{0:T(1024)} %param.19) | copy-start | bytes 12292
  0.0 52.7 %copy-start.11 = (f32[1024]{0:T(1024)S(1)}, f32[1024]{0:T(1024)}, u32[]{:S(2)}) copy-start(f32[1024]{0:T(1024)} %param.22) | copy-start | bytes 12292
  0.0 52.7 %copy-start.9 = (bf16[31,1024]{1,0:T(8,128)(2,1)S(1)}, bf16[31,1024]{1,0:T(8,128)(2,1)}, u32[]{:S(2)}) copy-start(bf16[31,1024]{1,0:T(8,128)(2,1)} %refs_3_.3) | copy-start | bytes 190468
  1.8 50.9 %copy-start.2 = (bf16[64,3072]{1,0:T(8,128)(2,1)S(1)}, bf16[64,3072]{1,0:T(8,128)(2,1)}, u32[]{:S(2)}) copy-start(bf16[64,3072]{1,0:T(8,128)(2,1)} %join_shards.1.refs_5_) | copy-start | bytes 1179652
  1.8 11.3 %collective-permute-start = (bf16[64,3072]{1,0:T(8,128)(2,1)}, bf16[64,3072]{1,0:T(8,128)(2,1)S(1)}, u32[]{:S(2)}, u32[]{:S(2)}) collective-permute-start(bf16[64,3072]{1,0:T(8,128)(2,1)} %join_shards.1.refs_5_), channel_id=1, source_target_pairs={{0,128},{16,144},{32,160},{48,176},{64,192},{80,208},{96,224},{112... | collective-permute-start | bytes 1179656 | tf_op jit(solution)/shard_map/ppermute | solution.py:451
  3.8 18.8 %collective-permute-start.2 = (bf16[64,3072]{1,0:T(8,128)(2,1)}, bf16[64,3072]{1,0:T(8,128)(2,1)S(1)}, u32[]{:S(2)}, u32[]{:S(2)}) collective-permute-start(bf16[64,3072]{1,0:T(8,128)(2,1)} %join_shards.1.refs_5_), channel_id=1, source_target_pairs={{0,32},{16,48},{32,64},{48,80},{64,96},{80,112},{96,0},{112,16},{1... | collective-permute-start | bytes 1179656 | tf_op jit(solution)/shard_map/ppermute | solution.py:451
  4.3 18.3 %collective-permute-start.3 = (bf16[64,3072]{1,0:T(8,128)(2,1)}, bf16[64,3072]{1,0:T(8,128)(2,1)S(1)}, u32[]{:S(2)}, u32[]{:S(2)}) collective-permute-start(bf16[64,3072]{1,0:T(8,128)(2,1)} %join_shards.1.refs_5_), channel_id=1, source_target_pairs={{0,96},{16,112},{32,0},{48,16},{64,32},{80,48},{96,64},{112,80},{1... | collective-permute-start | bytes 1179656 | tf_op jit(solution)/shard_map/ppermute | solution.py:451
  5.8 19.2 %collective-permute-start.8 = (bf16[64,3072]{1,0:T(8,128)(2,1)}, bf16[64,3072]{1,0:T(8,128)(2,1)S(1)}, u32[]{:S(2)}, u32[]{:S(2)}) collective-permute-start(bf16[64,3072]{1,0:T(8,128)(2,1)} %join_shards.1.refs_5_), channel_id=1, source_target_pairs={{0,16},{16,0},{32,48},{48,32},{64,80},{80,64},{96,112},{112,96},{1... | collective-permute-start | bytes 1179656 | tf_op jit(solution)/shard_map/ppermute | solution.py:451
  13.1 24.7 %collective-permute-start.5 = (bf16[64,3072]{1,0:T(8,128)(2,1)S(1)}, bf16[64,3072]{1,0:T(8,128)(2,1)S(1)}, u32[]{:S(2)}, u32[]{:S(2)}) collective-permute-start(bf16[64,3072]{1,0:T(8,128)(2,1)S(1)} %collective-permute-done.own_hbm.value_ref.refs_6_), channel_id=1, source_target_pairs={{0,96},{16,112},{32,0},{48,16},{64,32},{80,48},{96,64},{112,80},{1... | collective-permute-start | bytes 1179656 | tf_op jit(solution)/shard_map/ppermute | solution.py:451
  14.0 1.0 copy-start.3
  14.9 0.7 copy-start.5
  16.4 17.7 %collective-permute-start.9 = (bf16[144,1024]{1,0:T(8,128)(2,1)S(1)}, bf16[144,1024]{1,0:T(8,128)(2,1)S(1)}, u32[]{:S(2)}, u32[]{:S(2)}) collective-permute-start(bf16[144,1024]{1,0:T(8,128)(2,1)S(1)} %pack_frames.1.refs_0_.value_ref), channel_id=1, source_target_pairs={{0,3},{1,0},{2,1},{3,2},{4,7},{5,4},{6,5},{7,6},{8,11},{9,8},{10,9... | collective-permute-start | bytes 884744 | tf_op jit(solution)/shard_map/ppermute | solution.py:452
  22.6 15.3 %collective-permute-start.1 = (bf16[144,1024]{1,0:T(8,128)(2,1)S(1)}, bf16[144,1024]{1,0:T(8,128)(2,1)S(1)}, u32[]{:S(2)}, u32[]{:S(2)}) collective-permute-start(bf16[144,1024]{1,0:T(8,128)(2,1)S(1)} %pack_frames.1.refs_0_.value_ref), channel_id=1, source_target_pairs={{0,1},{1,2},{2,3},{3,0},{4,5},{5,6},{6,7},{7,4},{8,9},{9,10},{10,1... | collective-permute-start | bytes 884744 | tf_op jit(solution)/shard_map/ppermute | solution.py:452
  22.6 18.3 %collective-permute-start.4 = (bf16[64,3072]{1,0:T(8,128)(2,1)S(1)}, bf16[64,3072]{1,0:T(8,128)(2,1)}, u32[]{:S(2)}, u32[]{:S(2)}) collective-permute-start(bf16[64,3072]{1,0:T(8,128)(2,1)S(1)} %collective-permute-done.own_hbm.value_ref.refs_6_), channel_id=1, source_target_pairs={{0,32},{16,48},{32,64},{48,80},{64,96},{80,112},{96,0},{112,16},{1... | collective-permute-start | bytes 1179656 | tf_op jit(solution)/shard_map/ppermute | solution.py:451
  25.1 16.1 %collective-permute-start.6 = (bf16[64,3072]{1,0:T(8,128)(2,1)S(1)}, bf16[64,3072]{1,0:T(8,128)(2,1)}, u32[]{:S(2)}, u32[]{:S(2)}) collective-permute-start(bf16[64,3072]{1,0:T(8,128)(2,1)S(1)} %collective-permute-done.2.refs_7_), channel_id=1, source_target_pairs={{0,32},{16,48},{32,64},{48,80},{64,96},{80,112},{96,0},{112,16},{1... | collective-permute-start | bytes 1179656 | tf_op jit(solution)/shard_map/ppermute | solution.py:451
  34.0 7.4 %collective-permute-start.11 = (bf16[64,3072]{1,0:T(8,128)(2,1)S(1)}, bf16[64,3072]{1,0:T(8,128)(2,1)}, u32[]{:S(2)}, u32[]{:S(2)}) collective-permute-start(bf16[64,3072]{1,0:T(8,128)(2,1)S(1)} %collective-permute-done.2.refs_7_), channel_id=1, source_target_pairs={{0,16},{16,0},{32,48},{48,32},{64,80},{80,64},{96,112},{112,96},{1... | collective-permute-start | bytes 1179656 | tf_op jit(solution)/shard_map/ppermute | solution.py:451
  37.9 3.8 %collective-permute-start.12 = (bf16[64,3072]{1,0:T(8,128)(2,1)S(1)}, bf16[64,3072]{1,0:T(8,128)(2,1)}, u32[]{:S(2)}, u32[]{:S(2)}) collective-permute-start(bf16[64,3072]{1,0:T(8,128)(2,1)S(1)} %collective-permute-done.3.refs_8_), channel_id=1, source_target_pairs={{0,16},{16,0},{32,48},{48,32},{64,80},{80,64},{96,112},{112,96},{1... | collective-permute-start | bytes 1179656 | tf_op jit(solution)/shard_map/ppermute | solution.py:451
  37.9 12.8 %collective-permute-start.7 = (bf16[64,3072]{1,0:T(8,128)(2,1)S(1)}, bf16[64,3072]{1,0:T(8,128)(2,1)}, u32[]{:S(2)}, u32[]{:S(2)}) collective-permute-start(bf16[64,3072]{1,0:T(8,128)(2,1)S(1)} %collective-permute-done.5.refs_10_), channel_id=1, source_target_pairs={{0,96},{16,112},{32,0},{48,16},{64,32},{80,48},{96,64},{112,80},{1... | collective-permute-start | bytes 1179656 | tf_op jit(solution)/shard_map/ppermute | solution.py:451
  40.9 10.2 %collective-permute-start.10 = (bf16[64,3072]{1,0:T(8,128)(2,1)S(1)}, bf16[64,3072]{1,0:T(8,128)(2,1)S(1)}, u32[]{:S(2)}, u32[]{:S(2)}) collective-permute-start(bf16[64,3072]{1,0:T(8,128)(2,1)S(1)} %pass_after.2), channel_id=1, source_target_pairs={{0,16},{16,0},{32,48},{48,32},{64,80},{80,64},{96,112},{112,96},{1... | collective-permute-start | bytes 1179656 | tf_op jit(solution)/shard_map/ppermute | solution.py:451
  41.2 10.2 %collective-permute-start.14 = (bf16[64,3072]{1,0:T(8,128)(2,1)S(1)}, bf16[64,3072]{1,0:T(8,128)(2,1)S(1)}, u32[]{:S(2)}, u32[]{:S(2)}) collective-permute-start(bf16[64,3072]{1,0:T(8,128)(2,1)S(1)} %collective-permute-done.5.refs_10_), channel_id=1, source_target_pairs={{0,16},{16,0},{32,48},{48,32},{64,80},{80,64},{96,112},{112,96},{1... | collective-permute-start | bytes 1179656 | tf_op jit(solution)/shard_map/ppermute | solution.py:451
  41.5 9.9 %collective-permute-start.13 = (bf16[64,3072]{1,0:T(8,128)(2,1)}, bf16[64,3072]{1,0:T(8,128)(2,1)S(1)}, u32[]{:S(2)}, u32[]{:S(2)}) collective-permute-start(bf16[64,3072]{1,0:T(8,128)(2,1)} %collective-permute-done.4.refs_9_), channel_id=1, source_target_pairs={{0,16},{16,0},{32,48},{48,32},{64,80},{80,64},{96,112},{112,96},{1... | collective-permute-start | bytes 1179656 | tf_op jit(solution)/shard_map/ppermute | solution.py:451
  41.7 9.7 %collective-permute-start.15 = (bf16[64,3072]{1,0:T(8,128)(2,1)}, bf16[64,3072]{1,0:T(8,128)(2,1)S(1)}, u32[]{:S(2)}, u32[]{:S(2)}) collective-permute-start(bf16[64,3072]{1,0:T(8,128)(2,1)} %collective-permute-done.6.refs_11_), channel_id=1, source_target_pairs={{0,16},{16,0},{32,48},{48,32},{64,80},{80,64},{96,112},{112,96},{1... | collective-permute-start | bytes 1179656 | tf_op jit(solution)/shard_map/ppermute | solution.py:451
  50.7 1.9 %collective-permute-start.16 = (bf16[64,3072]{1,0:T(8,128)(2,1)}, bf16[64,3072]{1,0:T(8,128)(2,1)S(1)}, u32[]{:S(2)}, u32[]{:S(2)}) collective-permute-start(bf16[64,3072]{1,0:T(8,128)(2,1)} %collective-permute-done.7.refs_12_), channel_id=1, source_target_pairs={{0,16},{16,0},{32,48},{48,32},{64,80},{80,64},{96,112},{112,96},{1... | collective-permute-start | bytes 1179656 | tf_op jit(solution)/shard_map/ppermute | solution.py:451
  51.1 19.9 %collective-permute-start.19 = (bf16[144,1024]{1,0:T(8,128)(2,1)S(1)}, bf16[144,1024]{1,0:T(8,128)(2,1)S(1)}, u32[]{:S(2)}, u32[]{:S(2)}) collective-permute-start(bf16[144,1024]{1,0:T(8,128)(2,1)S(1)} %pass_after.3), channel_id=1, source_target_pairs={{0,2},{1,3},{2,0},{3,1},{4,6},{5,7},{6,4},{7,5},{8,10},{9,11},{10,... | collective-permute-start | bytes 884744 | tf_op jit(solution)/shard_map/ppermute | solution.py:452
  61.0 21.5 %copy-start = (bf16[1,1024,1024]{2,1,0:T(8,128)(2,1)S(1)}, bf16[1,1024,1024]{2,1,0:T(8,128)(2,1)}, u32[]{:S(2)}) copy-start(bf16[1,1024,1024]{2,1,0:T(8,128)(2,1)} %param.25) | copy-start | bytes 6291460
  61.0 21.5 %copy-start.1 = (bf16[1,16,4,8,1024]{4,3,2,1,0:T(8,128)(2,1)S(1)}, bf16[1,16,4,8,1024]{4,3,2,1,0:T(8,128)(2,1)}, u32[]{:S(2)}) copy-start(bf16[1,16,4,8,1024]{4,3,2,1,0:T(8,128)(2,1)} %param.29) | copy-start | bytes 3145732
  61.0 21.5 %copy-start.4 = (f32[1,1024]{1,0:T(1,128)S(1)}, f32[1,1024]{1,0:T(1,128)}, u32[]{:S(2)}) copy-start(f32[1,1024]{1,0:T(1,128)} %gain_ref.1) | copy-start | bytes 12292
  61.0 37.0 %collective-permute-start.17 = (bf16[272,1024]{1,0:T(8,128)(2,1)S(1)}, bf16[272,1024]{1,0:T(8,128)(2,1)S(1)}, u32[]{:S(2)}, u32[]{:S(2)}) collective-permute-start(bf16[272,1024]{1,0:T(8,128)(2,1)S(1)} %encode.2.after_hbm.refs_0_), channel_id=1, source_target_pairs={{0,4},{1,5},{2,6},{3,7},{4,8},{5,9},{6,10},{7,11},{8,12},{9,13},{1... | collective-permute-start | bytes 1671176 | tf_op jit(solution)/shard_map/ppermute | solution.py:452
  62.7 35.3 %collective-permute-start.23 = (bf16[272,1024]{1,0:T(8,128)(2,1)S(1)}, bf16[272,1024]{1,0:T(8,128)(2,1)S(1)}, u32[]{:S(2)}, u32[]{:S(2)}) collective-permute-start(bf16[272,1024]{1,0:T(8,128)(2,1)S(1)} %encode.2.after_hbm.refs_0_), channel_id=1, source_target_pairs={{0,12},{1,13},{2,14},{3,15},{4,0},{5,1},{6,2},{7,3},{8,4},{9,5},{1... | collective-permute-start | bytes 1671176 | tf_op jit(solution)/shard_map/ppermute | solution.py:452
  71.0 14.6 %copy-start.8 = (bf16[1,1024,1024]{2,1,0:T(8,128)(2,1)S(1)}, bf16[1,1024,1024]{2,1,0:T(8,128)(2,1)}, u32[]{:S(2)}) copy-start(bf16[1,1024,1024]{2,1,0:T(8,128)(2,1)} %param.28) | copy-start | bytes 6291460
  79.5 14.9 %collective-permute-start.20 = (bf16[272,1024]{1,0:T(8,128)(2,1)S(1)}, bf16[272,1024]{1,0:T(8,128)(2,1)S(1)}, u32[]{:S(2)}, u32[]{:S(2)}) collective-permute-start(bf16[272,1024]{1,0:T(8,128)(2,1)S(1)} %encode.3.refs_1_), channel_id=1, source_target_pairs={{0,12},{1,13},{2,14},{3,15},{4,0},{5,1},{6,2},{7,3},{8,4},{9,5},{1... | collective-permute-start | bytes 1671176 | tf_op jit(solution)/shard_map/ppermute | solution.py:452
  82.5 21.7 %collective-permute-start.22 = (bf16[272,1024]{1,0:T(8,128)(2,1)S(1)}, bf16[272,1024]{1,0:T(8,128)(2,1)S(1)}, u32[]{:S(2)}, u32[]{:S(2)}) collective-permute-start(bf16[272,1024]{1,0:T(8,128)(2,1)S(1)} %encode.3.refs_1_), channel_id=1, source_target_pairs={{0,4},{1,5},{2,6},{3,7},{4,8},{5,9},{6,10},{7,11},{8,12},{9,13},{1... | collective-permute-start | bytes 1671176 | tf_op jit(solution)/shard_map/ppermute | solution.py:452
  82.6 3.0 %copy-start.6 = (bf16[1,1024,1024]{2,1,0:T(8,128)(2,1)S(1)}, bf16[1,1024,1024]{2,1,0:T(8,128)(2,1)}, u32[]{:S(2)}) copy-start(bf16[1,1024,1024]{2,1,0:T(8,128)(2,1)} %param.26) | copy-start | bytes 6291460
  82.6 3.0 %copy-start.7 = (bf16[1,1024,1024]{2,1,0:T(8,128)(2,1)S(1)}, bf16[1,1024,1024]{2,1,0:T(8,128)(2,1)}, u32[]{:S(2)}) copy-start(bf16[1,1024,1024]{2,1,0:T(8,128)(2,1)} %param.27) | copy-start | bytes 6291460
  94.3 16.1 %collective-permute-start.21 = (bf16[272,1024]{1,0:T(8,128)(2,1)S(1)}, bf16[272,1024]{1,0:T(8,128)(2,1)S(1)}, u32[]{:S(2)}, u32[]{:S(2)}) collective-permute-start(bf16[272,1024]{1,0:T(8,128)(2,1)S(1)} %collective-permute-done.20.refs_1_), channel_id=1, source_target_pairs={{0,12},{1,13},{2,14},{3,15},{4,0},{5,1},{6,2},{7,3},{8,4},{9,5},{1... | collective-permute-start | bytes 1671176 | tf_op jit(solution)/shard_map/ppermute | solution.py:452
  98.0 14.3 %collective-permute-start.18 = (bf16[272,1024]{1,0:T(8,128)(2,1)S(1)}, bf16[272,1024]{1,0:T(8,128)(2,1)S(1)}, u32[]{:S(2)}, u32[]{:S(2)}) collective-permute-start(bf16[272,1024]{1,0:T(8,128)(2,1)S(1)} %collective-permute-done.17.refs_0_), channel_id=1, source_target_pairs={{0,4},{1,5},{2,6},{3,7},{4,8},{5,9},{6,10},{7,11},{8,12},{9,13},{1... | collective-permute-start | bytes 1671176 | tf_op jit(solution)/shard_map/ppermute | solution.py:452

commit v3 on v2

--- a/solution.py
+++ b/solution.py
@@ -109,10 +109,10 @@
 
 
 def query_kernel(hidden_ref, gain_ref, w_ref, after_hbm, out_ref, normed):
-    @pl.loop(0, hidden_ref.shape[0] // 64)
+    @pl.loop(0, hidden_ref.shape[0] // 32)
     def _(i):
-        for r in range(0, 64, 16):
-            rows = pl.ds(pl.multiple_of(i * 64 + r, 16), 16)
+        for r in range(0, 32, 16):
+            rows = pl.ds(pl.multiple_of(i * 32 + r, 16), 16)
             normed[rows, :] = norm_rows(hidden_ref[rows, :].astype(F32), gain_ref[...]).astype(BF)
 
     for j in range(D // 256):
@@ -465,7 +465,7 @@
     source = hidden.reshape(-1, D)
     turn = list(shards)
     turn[1] = pass_after(turn[1], from_b, from_a)
-    from_2 = along(pass_after(packed, from_a), 0, 2)
+    from_2 = along(from_b, 0, 1)
     shards += [across(v, TO_CORE) for v in turn]
 
     def encode_pair(first, second):

time: 119 us -> 115 us (0.966)
  waiting for transfers between devices: 41.2 us -> 32.7 us
  starting transfers between devices: 25.7 us -> 29.1 us
  Pallas kernels: 47 us -> 48.3 us
    ppermute x9, waiting for transfers between devices: 23.9 us -> 16.4 us  [body(): along = lambda v, dy, dz: lax.ppermute(v, 'section', section_perm(dy, dz))]
    ppermute x9, starting transfers between devices: 16.6 us -> 20.3 us  [body(): along = lambda v, dy, dz: lax.ppermute(v, 'section', section_perm(dy, dz))]
    pallas_call x1, Pallas kernels: 2.94 us -> 4.32 us  [project_query(): pl.pallas_call(query_kernel, out_shape=jax.ShapeDtypeStruct((rows, D), BF...]
  transfers between devices with their start and end apart: 24 -> 24, of which waited for: 8 -> 8; matrix products, arithmetic and copies ran while one was open for 2% -> 2% of each run, Pallas kernels for 33% -> 35%
where the time goes in v3:
time: 115 us
  Pallas kernels  48.3 us (42%)
  waiting for transfers between devices  32.7 us (28%)
  starting transfers between devices  29.1 us (25%)
  local copies, waits for them, and re-layouts  4.09 us (4%)
    pallas_call x4, Pallas kernels, decode(): pl.pallas_call(functools.partial(decode_kernel, len(mems), aliased), out_...  24.6 us
    ppermute x9, starting transfers between devices, body(): along = lambda v, dy, dz: lax.ppermute(v, 'section', section_perm(dy, dz))  20.3 us
    pallas_call x2, Pallas kernels, encode(): pl.pallas_call(functools.partial(encode_kernel, len(shards)), out_shape=j...  16.8 us
    ppermute x9, waiting for transfers between devices, body(): along = lambda v, dy, dz: lax.ppermute(v, 'section', section_perm(dy, dz))  16.4 us
    ppermute x15, waiting for transfers between devices, body(): across = lambda v, perm: lax.ppermute(v, 'dp', perm)  16.3 us
    ppermute x15, starting transfers between devices, body(): across = lambda v, perm: lax.ppermute(v, 'dp', perm)  8.81 us
    pallas_call x1, Pallas kernels, project_query(): pl.pallas_call(query_kernel, out_shape=jax.ShapeDtypeStruct((rows, D), BF...  4.32 us
    unnamed x25, local copies, waits for them, and re-layouts  2.44 us
  transfers between devices with their start and end apart: 24, of which 8 were waited for; matrix products, arithmetic and copies ran while one was open for 2% of the time, Pallas kernels for 35%

profile of v3, /device:TPU:6, one launch (start us, length us, event | category | flops | bytes accessed | tf_op | source)
XLA Modules:
  0.0 114.9 jit_solution(8704083683909139419)
XLA Ops:
  0.0 1.8 %join_shards.1.refs_5_ = bf16[64,3072]{1,0:T(8,128)(2,1)} custom-call(bf16[64,2048]{1,0:T(8,128)(2,1)} %w_in_hbm.1, bf16[64,1024]{1,0:T(8,128)(2,1)} %w_out_hbm.1), custom_call_target="tpu_custom_call" | custom-call | bytes 800000 | tf_op jit(solution)/shard_map/join_shards/pallas_call | solution.py:71
  1.8 0.0 copy-start.2
  1.8 2.0 %collective-permute-start = (bf16[64,3072]{1,0:T(8,128)(2,1)}, bf16[64,3072]{1,0:T(8,128)(2,1)S(1)}, u32[]{:S(2)}, u32[]{:S(2)}) collective-permute-start(bf16[64,3072]{1,0:T(8,128)(2,1)} %join_shards.1.refs_5_), channel_id=1, source_target_pairs={{0,128},{16,144},{32,160},{48,176},{64,192},{80,208},{96,224},{112... | collective-permute-start | bytes 1179656 | tf_op jit(solution)/shard_map/ppermute | solution.py:451
  3.8 0.5 collective-permute-start.2
  4.3 1.5 %collective-permute-start.3 = (bf16[64,3072]{1,0:T(8,128)(2,1)}, bf16[64,3072]{1,0:T(8,128)(2,1)S(1)}, u32[]{:S(2)}, u32[]{:S(2)}) collective-permute-start(bf16[64,3072]{1,0:T(8,128)(2,1)} %join_shards.1.refs_5_), channel_id=1, source_target_pairs={{0,96},{16,112},{32,0},{48,16},{64,32},{80,48},{96,64},{112,80},{1... | collective-permute-start | bytes 1179656 | tf_op jit(solution)/shard_map/ppermute | solution.py:451
  5.8 7.3 %collective-permute-done.own_hbm.value_ref.refs_6_ = bf16[64,3072]{1,0:T(8,128)(2,1)S(1)} collective-permute-done((bf16[64,3072]{1,0:T(8,128)(2,1)}, bf16[64,3072]{1,0:T(8,128)(2,1)S(1)}, u32[]{:S(2)}, u32[]{:S(2)}) %collective-permute-start) | collective-permute-done | bytes 393248 | tf_op jit(solution)/shard_map/ppermute | solution.py:451
  13.1 0.8 collective-permute-start.5
  14.0 1.0 copy-done.3
  14.9 0.7 copy-done.5
  15.6 0.8 pack_frames.1.refs_0_
  16.4 3.3 %collective-permute-start.1 = (bf16[144,1024]{1,0:T(8,128)(2,1)S(1)}, bf16[144,1024]{1,0:T(8,128)(2,1)S(1)}, u32[]{:S(2)}, u32[]{:S(2)}) collective-permute-start(bf16[144,1024]{1,0:T(8,128)(2,1)S(1)} %pack_frames.1.refs_0_), channel_id=1, source_target_pairs={{0,1},{1,2},{2,3},{3,0},{4,5},{5,6},{6,7},{7,4},{8,9},{9,10},{10,1... | collective-permute-start | bytes 884744 | tf_op jit(solution)/shard_map/ppermute | solution.py:452
  19.7 3.0 %collective-permute-start.9 = (bf16[144,1024]{1,0:T(8,128)(2,1)S(1)}, bf16[144,1024]{1,0:T(8,128)(2,1)S(1)}, u32[]{:S(2)}, u32[]{:S(2)}) collective-permute-start(bf16[144,1024]{1,0:T(8,128)(2,1)S(1)} %pack_frames.1.refs_0_), channel_id=1, source_target_pairs={{0,3},{1,0},{2,1},{3,2},{4,7},{5,4},{6,5},{7,6},{8,11},{9,8},{10,9... | collective-permute-start | bytes 884744 | tf_op jit(solution)/shard_map/ppermute | solution.py:452
  22.7 2.4 %collective-permute-start.4 = (bf16[64,3072]{1,0:T(8,128)(2,1)S(1)}, bf16[64,3072]{1,0:T(8,128)(2,1)}, u32[]{:S(2)}, u32[]{:S(2)}) collective-permute-start(bf16[64,3072]{1,0:T(8,128)(2,1)S(1)} %collective-permute-done.own_hbm.value_ref.refs_6_), channel_id=1, source_target_pairs={{0,32},{16,48},{32,64},{48,80},{64,96},{80,112},{96,0},{112,16},{1... | collective-permute-start | bytes 1179656 | tf_op jit(solution)/shard_map/ppermute | solution.py:451
  25.1 0.1 collective-permute-start.6
  25.2 5.3 %collective-permute-done.1.refs_0_.refs_1_ = bf16[144,1024]{1,0:T(8,128)(2,1)S(1)} collective-permute-done((bf16[144,1024]{1,0:T(8,128)(2,1)S(1)}, bf16[144,1024]{1,0:T(8,128)(2,1)S(1)}, u32[]{:S(2)}, u32[]{:S(2)}) %collective-permute-start.1) | collective-permute-done | bytes 294944 | tf_op jit(solution)/shard_map/ppermute | solution.py:452
  30.4 5.5 %collective-permute-done.9.refs_1_.refs_0_ = bf16[144,1024]{1,0:T(8,128)(2,1)S(1)} collective-permute-done((bf16[144,1024]{1,0:T(8,128)(2,1)S(1)}, bf16[144,1024]{1,0:T(8,128)(2,1)S(1)}, u32[]{:S(2)}, u32[]{:S(2)}) %collective-permute-start.9) | collective-permute-done | bytes 294944 | tf_op jit(solution)/shard_map/ppermute | solution.py:452
  35.9 0.5 collective-permute-start.7
  36.5 0.7 dynamic-slice_reduce_fusion
  37.2 0.1 reshape_squeeze.3
  37.2 0.8 copy.21
  38.0 0.1 reshape.23.tgt_ref
  38.1 0.7 dynamic-slice_bitcast_fusion.where_ref
  38.8 0.1 slice_bitcast_fusion.1
  38.9 0.3 collective-permute-start.10
  39.2 1.4 %collective-permute-done.6.refs_11_ = bf16[64,3072]{1,0:T(8,128)(2,1)} collective-permute-done((bf16[64,3072]{1,0:T(8,128)(2,1)S(1)}, bf16[64,3072]{1,0:T(8,128)(2,1)}, u32[]{:S(2)}, u32[]{:S(2)}) %collective-permute-start.6) | collective-permute-done | bytes 393248 | tf_op jit(solution)/shard_map/ppermute | solution.py:451
  40.6 0.5 collective-permute-start.13
  41.1 0.1 collective-permute-start.15
  41.2 7.5 %collective-permute-done.7.refs_12_ = bf16[64,3072]{1,0:T(8,128)(2,1)} collective-permute-done((bf16[64,3072]{1,0:T(8,128)(2,1)S(1)}, bf16[64,3072]{1,0:T(8,128)(2,1)}, u32[]{:S(2)}, u32[]{:S(2)}) %collective-permute-start.7) | collective-permute-done | bytes 393248 | tf_op jit(solution)/shard_map/ppermute | solution.py:451
  48.8 0.1 pad_add_fusion.3.micro_ref
  48.8 0.1 pad_add_fusion.2.micro_ref
  48.9 0.1 pad_add_fusion.1.micro_ref
  49.0 0.1 pad_add_fusion.micro_ref
  49.1 4.0 %collective-permute-start.19 = (bf16[144,1024]{1,0:T(8,128)(2,1)S(1)}, bf16[144,1024]{1,0:T(8,128)(2,1)S(1)}, u32[]{:S(2)}, u32[]{:S(2)}) collective-permute-start(bf16[144,1024]{1,0:T(8,128)(2,1)S(1)} %collective-permute-done.1.refs_0_.refs_1_), channel_id=1, source_target_pairs={{0,1},{1,2},{2,3},{3,0},{4,5},{5,6},{6,7},{7,4},{8,9},{9,10},{10,1... | collective-permute-start | bytes 884744 | tf_op jit(solution)/shard_map/ppermute | solution.py:452
  53.1 8.3 %encode.2.after_hbm.refs_0_ = bf16[272,1024]{1,0:T(8,128)(2,1)S(1)} custom-call(s32[16]{0:T(128)S(1)} %dynamic-slice_bitcast_fusion.where_ref, bf16[144,1024]{1,0:T(8,128)(2,1)S(1)} %pack_frames.1.refs_0_, bf16[144,1024]{1,0:T(8,128)(2,1)S(1)} %collective-permute-done.1.refs_0_.refs_1_, f32[1,1024]{1,0:T(1,128)S(1)} %bitcast.48, ...), custom_call_target="tpu_custom_call" | custom-call | flops 8000000000 | bytes 8388608 | tf_op jit(solution)/shard_map/encode/pallas_call | solution.py:239
  61.4 0.0 copy-start
  61.5 1.7 %collective-permute-start.17 = (bf16[272,1024]{1,0:T(8,128)(2,1)S(1)}, bf16[272,1024]{1,0:T(8,128)(2,1)S(1)}, u32[]{:S(2)}, u32[]{:S(2)}) collective-permute-start(bf16[272,1024]{1,0:T(8,128)(2,1)S(1)} %encode.2.after_hbm.refs_0_), channel_id=1, source_target_pairs={{0,4},{1,5},{2,6},{3,7},{4,8},{5,9},{6,10},{7,11},{8,12},{9,13},{1... | collective-permute-start | bytes 1671176 | tf_op jit(solution)/shard_map/ppermute | solution.py:452
  63.1 1.7 %collective-permute-start.23 = (bf16[272,1024]{1,0:T(8,128)(2,1)S(1)}, bf16[272,1024]{1,0:T(8,128)(2,1)S(1)}, u32[]{:S(2)}, u32[]{:S(2)}) collective-permute-start(bf16[272,1024]{1,0:T(8,128)(2,1)S(1)} %encode.2.after_hbm.refs_0_), channel_id=1, source_target_pairs={{0,12},{1,13},{2,14},{3,15},{4,0},{5,1},{6,2},{7,3},{8,4},{9,5},{1... | collective-permute-start | bytes 1671176 | tf_op jit(solution)/shard_map/ppermute | solution.py:452
  64.8 1.7 %collective-permute-done.19.refs_1_ = bf16[144,1024]{1,0:T(8,128)(2,1)S(1)} collective-permute-done((bf16[144,1024]{1,0:T(8,128)(2,1)S(1)}, bf16[144,1024]{1,0:T(8,128)(2,1)S(1)}, u32[]{:S(2)}, u32[]{:S(2)}) %collective-permute-start.19) | collective-permute-done | bytes 294944 | tf_op jit(solution)/shard_map/ppermute | solution.py:452
  66.5 8.5 %encode.3.refs_1_ = bf16[272,1024]{1,0:T(8,128)(2,1)S(1)} custom-call(s32[16]{0:T(128)S(1)} %dynamic-slice_bitcast_fusion.where_ref, bf16[144,1024]{1,0:T(8,128)(2,1)S(1)} %collective-permute-done.9.refs_1_.refs_0_, bf16[144,1024]{1,0:T(8,128)(2,1)S(1)} %collective-permute-done.19.refs_1_, f32[1,1024]{1,0:T(1,128)S(1)} %bitcast.49, ...), custom_call_target="tpu_custom_call" | custom-call | flops 8000000000 | bytes 8388608 | tf_op jit(solution)/shard_map/encode/pallas_call | solution.py:239
  75.0 3.1 %collective-permute-start.20 = (bf16[272,1024]{1,0:T(8,128)(2,1)S(1)}, bf16[272,1024]{1,0:T(8,128)(2,1)S(1)}, u32[]{:S(2)}, u32[]{:S(2)}) collective-permute-start(bf16[272,1024]{1,0:T(8,128)(2,1)S(1)} %encode.3.refs_1_), channel_id=1, source_target_pairs={{0,12},{1,13},{2,14},{3,15},{4,0},{5,1},{6,2},{7,3},{8,4},{9,5},{1... | collective-permute-start | bytes 1671176 | tf_op jit(solution)/shard_map/ppermute | solution.py:452
  78.1 4.3 %project_query.1.refs_2_ = bf16[512,1024]{1,0:T(8,128)(2,1)S(1)} custom-call(bf16[512,1024]{1,0:T(8,128)(2,1)S(1)} %bitcast.29, f32[1,1024]{1,0:T(1,128)S(1)} %copy-done.4, bf16[1024,1024]{1,0:T(8,128)(2,1)S(1)} %bitcast.28, bf16[272,1024]{1,0:T(8,128)(2,1)S(1)} %encode.2.after_hbm.refs_0_), custom_call_target="tpu_custom_call" | custom-call | flops 1073741824 | bytes 4194304 | tf_op jit(solution)/shard_map/project_query/pallas_call | solution.py:126
  82.5 6.1 %decode.4.refs_7_ = bf16[512,1024]{1,0:T(8,128)(2,1)} custom-call(s32[4]{0:T(128)S(1)} %pad_add_fusion.3.micro_ref, s32[64]{0:T(128)S(1)} %reshape.23.tgt_ref, bf16[272,1024]{1,0:T(8,128)(2,1)S(1)} %encode.2.after_hbm.refs_0_, bf16[272,1024]{1,0:T(8,128)(2,1)S(1)} %encode.3.refs_1_, bf16[512,1024]{1,0:T(8,128)(2,1)S(1)} %project_query.1.refs_2_, ...), custom_call_target="tpu_custom_call" | custom-call | flops 8589934592 | bytes 8388608 | tf_op jit(solution)/shard_map/decode/pallas_call | solution.py:353
  88.6 1.6 %collective-permute-done.20.refs_1_ = bf16[272,1024]{1,0:T(8,128)(2,1)S(1)} collective-permute-done((bf16[272,1024]{1,0:T(8,128)(2,1)S(1)}, bf16[272,1024]{1,0:T(8,128)(2,1)S(1)}, u32[]{:S(2)}, u32[]{:S(2)}) %collective-permute-start.20) | collective-permute-done | bytes 557088 | tf_op jit(solution)/shard_map/ppermute | solution.py:452
  90.2 3.7 %collective-permute-start.21 = (bf16[272,1024]{1,0:T(8,128)(2,1)S(1)}, bf16[272,1024]{1,0:T(8,128)(2,1)S(1)}, u32[]{:S(2)}, u32[]{:S(2)}) collective-permute-start(bf16[272,1024]{1,0:T(8,128)(2,1)S(1)} %collective-permute-done.20.refs_1_), channel_id=1, source_target_pairs={{0,12},{1,13},{2,14},{3,15},{4,0},{5,1},{6,2},{7,3},{8,4},{9,5},{1... | collective-permute-start | bytes 1671176 | tf_op jit(solution)/shard_map/ppermute | solution.py:452
  93.9 6.1 %decode.5.refs_7_ = bf16[512,1024]{1,0:T(8,128)(2,1)} custom-call(s32[4]{0:T(128)S(1)} %pad_add_fusion.2.micro_ref, s32[64]{0:T(128)S(1)} %reshape.23.tgt_ref, bf16[272,1024]{1,0:T(8,128)(2,1)S(1)} %collective-permute-done.17.refs_0_, bf16[272,1024]{1,0:T(8,128)(2,1)S(1)} %collective-permute-done.23.refs_1_, ...), custom_call_target="tpu_custom_call", output_to_operand_aliasing={{}: (9, {})} | custom-call | flops 8589934592 | bytes 8388608 | tf_op jit(solution)/shard_map/decode/pallas_call | solution.py:353
  100.1 6.2 %decode.6.refs_7_ = bf16[512,1024]{1,0:T(8,128)(2,1)} custom-call(s32[4]{0:T(128)S(1)} %pad_add_fusion.1.micro_ref, s32[64]{0:T(128)S(1)} %reshape.23.tgt_ref, bf16[272,1024]{1,0:T(8,128)(2,1)S(1)} %collective-permute-done.22.refs_0_, bf16[272,1024]{1,0:T(8,128)(2,1)S(1)} %collective-permute-done.20.refs_1_, ...), custom_call_target="tpu_custom_call", output_to_operand_aliasing={{}: (9, {})} | custom-call | flops 8589934592 | bytes 8388608 | tf_op jit(solution)/shard_map/decode/pallas_call | solution.py:353
  106.3 2.3 %collective-permute-done.18.refs_0_ = bf16[272,1024]{1,0:T(8,128)(2,1)S(1)} collective-permute-done((bf16[272,1024]{1,0:T(8,128)(2,1)S(1)}, bf16[272,1024]{1,0:T(8,128)(2,1)S(1)}, u32[]{:S(2)}, u32[]{:S(2)}) %collective-permute-start.18) | collective-permute-done | bytes 557088 | tf_op jit(solution)/shard_map/ppermute | solution.py:452
  108.6 6.1 %decode.7 = bf16[512,1024]{1,0:T(8,128)(2,1)} custom-call(s32[4]{0:T(128)S(1)} %pad_add_fusion.micro_ref, s32[64]{0:T(128)S(1)} %reshape.23.tgt_ref, bf16[272,1024]{1,0:T(8,128)(2,1)S(1)} %collective-permute-done.18.refs_0_, bf16[272,1024]{1,0:T(8,128)(2,1)S(1)} %collective-permute-done.21.refs_1_, ...), custom_call_target="tpu_custom_call", output_to_operand_aliasing={{}: (9, {})} | custom-call | flops 8589934592 | bytes 8388608 | tf_op jit(solution)/shard_map/decode/pallas_call | solution.py:353
  (44 shorter events, 0.1 us)
Async XLA Ops:
  0.0 53.1 %copy-start.10 = (f32[1024]{0:T(1024)S(1)}, f32[1024]{0:T(1024)}, u32[]{:S(2)}) copy-start(f32[1024]{0:T(1024)} %param.19) | copy-start | bytes 12292
  0.0 53.1 %copy-start.11 = (f32[1024]{0:T(1024)S(1)}, f32[1024]{0:T(1024)}, u32[]{:S(2)}) copy-start(f32[1024]{0:T(1024)} %param.22) | copy-start | bytes 12292
  0.0 53.1 %copy-start.9 = (bf16[31,1024]{1,0:T(8,128)(2,1)S(1)}, bf16[31,1024]{1,0:T(8,128)(2,1)}, u32[]{:S(2)}) copy-start(bf16[31,1024]{1,0:T(8,128)(2,1)} %refs_3_.3) | copy-start | bytes 190468
  1.8 51.3 %copy-start.2 = (bf16[64,3072]{1,0:T(8,128)(2,1)S(1)}, bf16[64,3072]{1,0:T(8,128)(2,1)}, u32[]{:S(2)}) copy-start(bf16[64,3072]{1,0:T(8,128)(2,1)} %join_shards.1.refs_5_) | copy-start | bytes 1179652
  1.8 11.3 %collective-permute-start = (bf16[64,3072]{1,0:T(8,128)(2,1)}, bf16[64,3072]{1,0:T(8,128)(2,1)S(1)}, u32[]{:S(2)}, u32[]{:S(2)}) collective-permute-start(bf16[64,3072]{1,0:T(8,128)(2,1)} %join_shards.1.refs_5_), channel_id=1, source_target_pairs={{0,128},{16,144},{32,160},{48,176},{64,192},{80,208},{96,224},{112... | collective-permute-start | bytes 1179656 | tf_op jit(solution)/shard_map/ppermute | solution.py:451
  3.8 15.9 %collective-permute-start.2 = (bf16[64,3072]{1,0:T(8,128)(2,1)}, bf16[64,3072]{1,0:T(8,128)(2,1)S(1)}, u32[]{:S(2)}, u32[]{:S(2)}) collective-permute-start(bf16[64,3072]{1,0:T(8,128)(2,1)} %join_shards.1.refs_5_), channel_id=1, source_target_pairs={{0,32},{16,48},{32,64},{48,80},{64,96},{80,112},{96,0},{112,16},{1... | collective-permute-start | bytes 1179656 | tf_op jit(solution)/shard_map/ppermute | solution.py:451
  4.3 18.4 %collective-permute-start.3 = (bf16[64,3072]{1,0:T(8,128)(2,1)}, bf16[64,3072]{1,0:T(8,128)(2,1)S(1)}, u32[]{:S(2)}, u32[]{:S(2)}) collective-permute-start(bf16[64,3072]{1,0:T(8,128)(2,1)} %join_shards.1.refs_5_), channel_id=1, source_target_pairs={{0,96},{16,112},{32,0},{48,16},{64,32},{80,48},{96,64},{112,80},{1... | collective-permute-start | bytes 1179656 | tf_op jit(solution)/shard_map/ppermute | solution.py:451
  5.8 19.2 %collective-permute-start.8 = (bf16[64,3072]{1,0:T(8,128)(2,1)}, bf16[64,3072]{1,0:T(8,128)(2,1)S(1)}, u32[]{:S(2)}, u32[]{:S(2)}) collective-permute-start(bf16[64,3072]{1,0:T(8,128)(2,1)} %join_shards.1.refs_5_), channel_id=1, source_target_pairs={{0,16},{16,0},{32,48},{48,32},{64,80},{80,64},{96,112},{112,96},{1... | collective-permute-start | bytes 1179656 | tf_op jit(solution)/shard_map/ppermute | solution.py:451
  13.1 22.8 %collective-permute-start.5 = (bf16[64,3072]{1,0:T(8,128)(2,1)S(1)}, bf16[64,3072]{1,0:T(8,128)(2,1)S(1)}, u32[]{:S(2)}, u32[]{:S(2)}) collective-permute-start(bf16[64,3072]{1,0:T(8,128)(2,1)S(1)} %collective-permute-done.own_hbm.value_ref.refs_6_), channel_id=1, source_target_pairs={{0,96},{16,112},{32,0},{48,16},{64,32},{80,48},{96,64},{112,80},{1... | collective-permute-start | bytes 1179656 | tf_op jit(solution)/shard_map/ppermute | solution.py:451
  14.0 1.0 copy-start.3
  14.9 0.7 copy-start.5
  16.4 14.1 %collective-permute-start.1 = (bf16[144,1024]{1,0:T(8,128)(2,1)S(1)}, bf16[144,1024]{1,0:T(8,128)(2,1)S(1)}, u32[]{:S(2)}, u32[]{:S(2)}) collective-permute-start(bf16[144,1024]{1,0:T(8,128)(2,1)S(1)} %pack_frames.1.refs_0_), channel_id=1, source_target_pairs={{0,1},{1,2},{2,3},{3,0},{4,5},{5,6},{6,7},{7,4},{8,9},{9,10},{10,1... | collective-permute-start | bytes 884744 | tf_op jit(solution)/shard_map/ppermute | solution.py:452
  19.7 16.2 %collective-permute-start.9 = (bf16[144,1024]{1,0:T(8,128)(2,1)S(1)}, bf16[144,1024]{1,0:T(8,128)(2,1)S(1)}, u32[]{:S(2)}, u32[]{:S(2)}) collective-permute-start(bf16[144,1024]{1,0:T(8,128)(2,1)S(1)} %pack_frames.1.refs_0_), channel_id=1, source_target_pairs={{0,3},{1,0},{2,1},{3,2},{4,7},{5,4},{6,5},{7,6},{8,11},{9,8},{10,9... | collective-permute-start | bytes 884744 | tf_op jit(solution)/shard_map/ppermute | solution.py:452
  22.7 16.2 %collective-permute-start.4 = (bf16[64,3072]{1,0:T(8,128)(2,1)S(1)}, bf16[64,3072]{1,0:T(8,128)(2,1)}, u32[]{:S(2)}, u32[]{:S(2)}) collective-permute-start(bf16[64,3072]{1,0:T(8,128)(2,1)S(1)} %collective-permute-done.own_hbm.value_ref.refs_6_), channel_id=1, source_target_pairs={{0,32},{16,48},{32,64},{48,80},{64,96},{80,112},{96,0},{112,16},{1... | collective-permute-start | bytes 1179656 | tf_op jit(solution)/shard_map/ppermute | solution.py:451
  25.1 15.5 %collective-permute-start.6 = (bf16[64,3072]{1,0:T(8,128)(2,1)S(1)}, bf16[64,3072]{1,0:T(8,128)(2,1)}, u32[]{:S(2)}, u32[]{:S(2)}) collective-permute-start(bf16[64,3072]{1,0:T(8,128)(2,1)S(1)} %collective-permute-done.2.refs_7_), channel_id=1, source_target_pairs={{0,32},{16,48},{32,64},{48,80},{64,96},{80,112},{96,0},{112,16},{1... | collective-permute-start | bytes 1179656 | tf_op jit(solution)/shard_map/ppermute | solution.py:451
  30.4 10.2 %collective-permute-start.11 = (bf16[64,3072]{1,0:T(8,128)(2,1)S(1)}, bf16[64,3072]{1,0:T(8,128)(2,1)}, u32[]{:S(2)}, u32[]{:S(2)}) collective-permute-start(bf16[64,3072]{1,0:T(8,128)(2,1)S(1)} %collective-permute-done.2.refs_7_), channel_id=1, source_target_pairs={{0,16},{16,0},{32,48},{48,32},{64,80},{80,64},{96,112},{112,96},{1... | collective-permute-start | bytes 1179656 | tf_op jit(solution)/shard_map/ppermute | solution.py:451
  35.9 5.2 %collective-permute-start.12 = (bf16[64,3072]{1,0:T(8,128)(2,1)S(1)}, bf16[64,3072]{1,0:T(8,128)(2,1)}, u32[]{:S(2)}, u32[]{:S(2)}) collective-permute-start(bf16[64,3072]{1,0:T(8,128)(2,1)S(1)} %collective-permute-done.3.refs_8_), channel_id=1, source_target_pairs={{0,16},{16,0},{32,48},{48,32},{64,80},{80,64},{96,112},{112,96},{1... | collective-permute-start | bytes 1179656 | tf_op jit(solution)/shard_map/ppermute | solution.py:451
  35.9 12.8 %collective-permute-start.7 = (bf16[64,3072]{1,0:T(8,128)(2,1)S(1)}, bf16[64,3072]{1,0:T(8,128)(2,1)}, u32[]{:S(2)}, u32[]{:S(2)}) collective-permute-start(bf16[64,3072]{1,0:T(8,128)(2,1)S(1)} %collective-permute-done.5.refs_10_), channel_id=1, source_target_pairs={{0,96},{16,112},{32,0},{48,16},{64,32},{80,48},{96,64},{112,80},{1... | collective-permute-start | bytes 1179656 | tf_op jit(solution)/shard_map/ppermute | solution.py:451
  38.9 10.2 %collective-permute-start.10 = (bf16[64,3072]{1,0:T(8,128)(2,1)S(1)}, bf16[64,3072]{1,0:T(8,128)(2,1)S(1)}, u32[]{:S(2)}, u32[]{:S(2)}) collective-permute-start(bf16[64,3072]{1,0:T(8,128)(2,1)S(1)} %pass_after.1), channel_id=1, source_target_pairs={{0,16},{16,0},{32,48},{48,32},{64,80},{80,64},{96,112},{112,96},{1... | collective-permute-start | bytes 1179656 | tf_op jit(solution)/shard_map/ppermute | solution.py:451
  40.6 12.4 %collective-permute-start.14 = (bf16[64,3072]{1,0:T(8,128)(2,1)S(1)}, bf16[64,3072]{1,0:T(8,128)(2,1)S(1)}, u32[]{:S(2)}, u32[]{:S(2)}) collective-permute-start(bf16[64,3072]{1,0:T(8,128)(2,1)S(1)} %collective-permute-done.5.refs_10_), channel_id=1, source_target_pairs={{0,16},{16,0},{32,48},{48,32},{64,80},{80,64},{96,112},{112,96},{1... | collective-permute-start | bytes 1179656 | tf_op jit(solution)/shard_map/ppermute | solution.py:451
  40.6 12.4 %collective-permute-start.13 = (bf16[64,3072]{1,0:T(8,128)(2,1)}, bf16[64,3072]{1,0:T(8,128)(2,1)S(1)}, u32[]{:S(2)}, u32[]{:S(2)}) collective-permute-start(bf16[64,3072]{1,0:T(8,128)(2,1)} %collective-permute-done.4.refs_9_), channel_id=1, source_target_pairs={{0,16},{16,0},{32,48},{48,32},{64,80},{80,64},{96,112},{112,96},{1... | collective-permute-start | bytes 1179656 | tf_op jit(solution)/shard_map/ppermute | solution.py:451
  41.1 11.9 %collective-permute-start.15 = (bf16[64,3072]{1,0:T(8,128)(2,1)}, bf16[64,3072]{1,0:T(8,128)(2,1)S(1)}, u32[]{:S(2)}, u32[]{:S(2)}) collective-permute-start(bf16[64,3072]{1,0:T(8,128)(2,1)} %collective-permute-done.6.refs_11_), channel_id=1, source_target_pairs={{0,16},{16,0},{32,48},{48,32},{64,80},{80,64},{96,112},{112,96},{1... | collective-permute-start | bytes 1179656 | tf_op jit(solution)/shard_map/ppermute | solution.py:451
  48.8 4.3 %collective-permute-start.16 = (bf16[64,3072]{1,0:T(8,128)(2,1)}, bf16[64,3072]{1,0:T(8,128)(2,1)S(1)}, u32[]{:S(2)}, u32[]{:S(2)}) collective-permute-start(bf16[64,3072]{1,0:T(8,128)(2,1)} %collective-permute-done.7.refs_12_), channel_id=1, source_target_pairs={{0,16},{16,0},{32,48},{48,32},{64,80},{80,64},{96,112},{112,96},{1... | collective-permute-start | bytes 1179656 | tf_op jit(solution)/shard_map/ppermute | solution.py:451
  49.1 17.5 %collective-permute-start.19 = (bf16[144,1024]{1,0:T(8,128)(2,1)S(1)}, bf16[144,1024]{1,0:T(8,128)(2,1)S(1)}, u32[]{:S(2)}, u32[]{:S(2)}) collective-permute-start(bf16[144,1024]{1,0:T(8,128)(2,1)S(1)} %collective-permute-done.1.refs_0_.refs_1_), channel_id=1, source_target_pairs={{0,1},{1,2},{2,3},{3,0},{4,5},{5,6},{6,7},{7,4},{8,9},{9,10},{10,1... | collective-permute-start | bytes 884744 | tf_op jit(solution)/shard_map/ppermute | solution.py:452
  61.4 16.7 %copy-start = (bf16[1,1024,1024]{2,1,0:T(8,128)(2,1)S(1)}, bf16[1,1024,1024]{2,1,0:T(8,128)(2,1)}, u32[]{:S(2)}) copy-start(bf16[1,1024,1024]{2,1,0:T(8,128)(2,1)} %param.25) | copy-start | bytes 6291460
  61.5 16.7 %copy-start.1 = (bf16[1,16,4,8,1024]{4,3,2,1,0:T(8,128)(2,1)S(1)}, bf16[1,16,4,8,1024]{4,3,2,1,0:T(8,128)(2,1)}, u32[]{:S(2)}) copy-start(bf16[1,16,4,8,1024]{4,3,2,1,0:T(8,128)(2,1)} %param.29) | copy-start | bytes 3145732
  61.5 16.6 %copy-start.4 = (f32[1,1024]{1,0:T(1,128)S(1)}, f32[1,1024]{1,0:T(1,128)}, u32[]{:S(2)}) copy-start(f32[1,1024]{1,0:T(1,128)} %gain_ref.1) | copy-start | bytes 12292
  61.5 32.4 %collective-permute-start.17 = (bf16[272,1024]{1,0:T(8,128)(2,1)S(1)}, bf16[272,1024]{1,0:T(8,128)(2,1)S(1)}, u32[]{:S(2)}, u32[]{:S(2)}) collective-permute-start(bf16[272,1024]{1,0:T(8,128)(2,1)S(1)} %encode.2.after_hbm.refs_0_), channel_id=1, source_target_pairs={{0,4},{1,5},{2,6},{3,7},{4,8},{5,9},{6,10},{7,11},{8,12},{9,13},{1... | collective-permute-start | bytes 1671176 | tf_op jit(solution)/shard_map/ppermute | solution.py:452
  63.1 30.8 %collective-permute-start.23 = (bf16[272,1024]{1,0:T(8,128)(2,1)S(1)}, bf16[272,1024]{1,0:T(8,128)(2,1)S(1)}, u32[]{:S(2)}, u32[]{:S(2)}) collective-permute-start(bf16[272,1024]{1,0:T(8,128)(2,1)S(1)} %encode.2.after_hbm.refs_0_), channel_id=1, source_target_pairs={{0,12},{1,13},{2,14},{3,15},{4,0},{5,1},{6,2},{7,3},{8,4},{9,5},{1... | collective-permute-start | bytes 1671176 | tf_op jit(solution)/shard_map/ppermute | solution.py:452
  66.5 15.9 %copy-start.8 = (bf16[1,1024,1024]{2,1,0:T(8,128)(2,1)S(1)}, bf16[1,1024,1024]{2,1,0:T(8,128)(2,1)}, u32[]{:S(2)}) copy-start(bf16[1,1024,1024]{2,1,0:T(8,128)(2,1)} %param.28) | copy-start | bytes 6291460
  75.0 15.2 %collective-permute-start.20 = (bf16[272,1024]{1,0:T(8,128)(2,1)S(1)}, bf16[272,1024]{1,0:T(8,128)(2,1)S(1)}, u32[]{:S(2)}, u32[]{:S(2)}) collective-permute-start(bf16[272,1024]{1,0:T(8,128)(2,1)S(1)} %encode.3.refs_1_), channel_id=1, source_target_pairs={{0,12},{1,13},{2,14},{3,15},{4,0},{5,1},{6,2},{7,3},{8,4},{9,5},{1... | collective-permute-start | bytes 1671176 | tf_op jit(solution)/shard_map/ppermute | solution.py:452
  78.1 22.0 %collective-permute-start.22 = (bf16[272,1024]{1,0:T(8,128)(2,1)S(1)}, bf16[272,1024]{1,0:T(8,128)(2,1)S(1)}, u32[]{:S(2)}, u32[]{:S(2)}) collective-permute-start(bf16[272,1024]{1,0:T(8,128)(2,1)S(1)} %encode.3.refs_1_), channel_id=1, source_target_pairs={{0,4},{1,5},{2,6},{3,7},{4,8},{5,9},{6,10},{7,11},{8,12},{9,13},{1... | collective-permute-start | bytes 1671176 | tf_op jit(solution)/shard_map/ppermute | solution.py:452
  78.1 4.4 %copy-start.6 = (bf16[1,1024,1024]{2,1,0:T(8,128)(2,1)S(1)}, bf16[1,1024,1024]{2,1,0:T(8,128)(2,1)}, u32[]{:S(2)}) copy-start(bf16[1,1024,1024]{2,1,0:T(8,128)(2,1)} %param.26) | copy-start | bytes 6291460
  78.1 4.4 %copy-start.7 = (bf16[1,1024,1024]{2,1,0:T(8,128)(2,1)S(1)}, bf16[1,1024,1024]{2,1,0:T(8,128)(2,1)}, u32[]{:S(2)}) copy-start(bf16[1,1024,1024]{2,1,0:T(8,128)(2,1)} %param.27) | copy-start | bytes 6291460
  90.2 16.0 %collective-permute-start.21 = (bf16[272,1024]{1,0:T(8,128)(2,1)S(1)}, bf16[272,1024]{1,0:T(8,128)(2,1)S(1)}, u32[]{:S(2)}, u32[]{:S(2)}) collective-permute-start(bf16[272,1024]{1,0:T(8,128)(2,1)S(1)} %collective-permute-done.20.refs_1_), channel_id=1, source_target_pairs={{0,12},{1,13},{2,14},{3,15},{4,0},{5,1},{6,2},{7,3},{8,4},{9,5},{1... | collective-permute-start | bytes 1671176 | tf_op jit(solution)/shard_map/ppermute | solution.py:452
  93.9 14.7 %collective-permute-start.18 = (bf16[272,1024]{1,0:T(8,128)(2,1)S(1)}, bf16[272,1024]{1,0:T(8,128)(2,1)S(1)}, u32[]{:S(2)}, u32[]{:S(2)}) collective-permute-start(bf16[272,1024]{1,0:T(8,128)(2,1)S(1)} %collective-permute-done.17.refs_0_), channel_id=1, source_target_pairs={{0,4},{1,5},{2,6},{3,7},{4,8},{5,9},{6,10},{7,11},{8,12},{9,13},{1... | collective-permute-start | bytes 1671176 | tf_op jit(solution)/shard_map/ppermute | solution.py:452

commit v4 on v3

--- a/solution.py
+++ b/solution.py
@@ -162,20 +162,33 @@
     return total
 
 
+LATE = (6, 7, 10, 11)
+
+
 def encode_kernel(n_w, where_ref, *refs):
     x_refs = refs[:2]
     gain_in_ref, dw_ref, gain_mid_ref = refs[2:5]
-    blocks = []
-    for ref in refs[5 : 5 + n_w]:
-        blocks += [(ref, row) for row in range(0, ref.shape[0], 64)]
-    w_refs = blocks[: len(blocks) // 2], blocks[len(blocks) // 2 :]
-    out_ref, plain, normed, spread, conv, taps, act = refs[5 + n_w :]
+    blocks = [(ref, 0) for ref in refs[5 : 5 + n_w]]
+    out_ref, plain, normed, spread, conv, taps, act, late, sems = refs[5 + n_w :]
+    depth = late.shape[0] // len(LATE)
+    copies = []
+    for i, shard in enumerate(LATE):
+        rows = pl.ds(i * depth, depth)
+        copies.append(pltpu.make_async_copy(blocks[shard][0], late.at[rows, :], sems.at[i]))
+        copies[-1].start()
+        blocks[shard] = (late, i * depth)
+    w_refs = blocks[: n_w // 2], blocks[n_w // 2 :]
     step = 16
     for i, x in enumerate(x_refs):
-        for r in range(0, TOT, step):
-            plain[i * TOT + r : i * TOT + r + step, :] = norm_rows(
-                x[r : r + step, :].astype(F32), gain_in_ref[...]
-            ).astype(BF)
+
+        @pl.loop(0, 2)
+        def _(h):
+            for r in range(0, TOT // 2, step):
+                at = pl.multiple_of(h * (TOT // 2) + r, step)
+                plain[pl.ds(i * TOT + at, step), :] = norm_rows(
+                    x[pl.ds(at, step), :].astype(F32), gain_in_ref[...]
+                ).astype(BF)
+
     order_columns(normed, plain, where_ref)
     taps[...] = dw_ref[...].astype(F32)
     rows = normed.shape[0]
@@ -190,6 +203,8 @@
     expand = one_hot(target.astype(jnp.int32) == spot)
     column = jnp.broadcast_to(target, (8, rows)).T[:, 0:1].astype(jnp.int32)
     shrink = one_hot(column == lax.broadcasted_iota(jnp.int32, (rows, frame_rows), 1))
+    for copy in copies:
+        copy.wait()
     for j in range(D // 256):
         value = dot_shards(normed, w_refs, slice(j * 256, (j + 1) * 256))
         gate = dot_shards(normed, w_refs, slice(D + j * 256, D + (j + 1) * 256))
@@ -239,7 +254,7 @@
     return pl.pallas_call(
         functools.partial(encode_kernel, len(shards)),
         out_shape=jax.ShapeDtypeStruct((rows + EXTRA, D), BF),
-        in_specs=[SM] + [VM] * (5 + len(shards)),
+        in_specs=[SM] + [VM] * 5 + [HBM if i in LATE else VM for i in range(len(shards))],
         out_specs=VM,
         scratch_shapes=[
             pltpu.VMEM((rows, D), BF),
@@ -248,6 +263,8 @@
             pltpu.VMEM((frame_rows, D), F32),
             pltpu.VMEM((TAPS, D), F32),
             pltpu.VMEM((frame_rows, D), BF),
+            pltpu.VMEM((len(LATE) * D // 16, 3 * D), BF),
+            pltpu.SemaphoreType.DMA((len(LATE),)),
         ],
         compiler_params=params(9),
         cost_estimate=cost(8_000_000_000, 8 << 20),

time: 115 us -> 116 us (level)
  transfers between devices with their start and end apart: 24 -> 24, of which waited for: 8 -> 8; matrix products, arithmetic and copies ran while one was open for 2% -> 2% of each run, Pallas kernels for 35% -> 36%
where the time goes in v4:
time: 116 us; the launch traced here: 115 us
  Pallas kernels  49.1 us (42%)
  waiting for transfers between devices  32.3 us (28%)
  starting transfers between devices  29.1 us (25%)
  local copies, waits for them, and re-layouts  4.09 us (4%)
    pallas_call x4, Pallas kernels, decode(): pl.pallas_call(functools.partial(decode_kernel, len(mems), aliased), out_...  24.6 us
    ppermute x9, starting transfers between devices, body(): along = lambda v, dy, dz: lax.ppermute(v, 'section', section_perm(dy, dz))  20.3 us
    pallas_call x2, Pallas kernels, encode(): pl.pallas_call(functools.partial(encode_kernel, len(shards)), out_shape=j...  17.6 us
    ppermute x15, waiting for transfers between devices, body(): across = lambda v, perm: lax.ppermute(v, 'dp', perm)  16.3 us
    ppermute x9, waiting for transfers between devices, body(): along = lambda v, dy, dz: lax.ppermute(v, 'section', section_perm(dy, dz))  16 us
    ppermute x15, starting transfers between devices, body(): across = lambda v, perm: lax.ppermute(v, 'dp', perm)  8.81 us
    pallas_call x1, Pallas kernels, project_query(): pl.pallas_call(query_kernel, out_shape=jax.ShapeDtypeStruct((rows, D), BF...  4.32 us
    unnamed x25, local copies, waits for them, and re-layouts  2.44 us
  transfers between devices with their start and end apart: 24, of which 8 were waited for; matrix products, arithmetic and copies ran while one was open for 2% of the time, Pallas kernels for 36%

profile of v4, /device:TPU:6, one launch (start us, length us, event | category | flops | bytes accessed | tf_op | source)
XLA Modules:
  0.0 115.3 jit_solution(5599297939457286409)
XLA Ops:
  0.0 1.8 %join_shards.1.refs_5_ = bf16[64,3072]{1,0:T(8,128)(2,1)} custom-call(bf16[64,2048]{1,0:T(8,128)(2,1)} %w_in_hbm.1, bf16[64,1024]{1,0:T(8,128)(2,1)} %w_out_hbm.1), custom_call_target="tpu_custom_call" | custom-call | bytes 800000 | tf_op jit(solution)/shard_map/join_shards/pallas_call | solution.py:71
  1.8 0.0 copy-start.2
  1.8 2.0 %collective-permute-start = (bf16[64,3072]{1,0:T(8,128)(2,1)}, bf16[64,3072]{1,0:T(8,128)(2,1)S(1)}, u32[]{:S(2)}, u32[]{:S(2)}) collective-permute-start(bf16[64,3072]{1,0:T(8,128)(2,1)} %join_shards.1.refs_5_), channel_id=1, source_target_pairs={{0,128},{16,144},{32,160},{48,176},{64,192},{80,208},{96,224},{112... | collective-permute-start | bytes 1179656 | tf_op jit(solution)/shard_map/ppermute | solution.py:468
  3.8 0.5 collective-permute-start.2
  4.3 1.5 %collective-permute-start.3 = (bf16[64,3072]{1,0:T(8,128)(2,1)}, bf16[64,3072]{1,0:T(8,128)(2,1)S(1)}, u32[]{:S(2)}, u32[]{:S(2)}) collective-permute-start(bf16[64,3072]{1,0:T(8,128)(2,1)} %join_shards.1.refs_5_), channel_id=1, source_target_pairs={{0,96},{16,112},{32,0},{48,16},{64,32},{80,48},{96,64},{112,80},{1... | collective-permute-start | bytes 1179656 | tf_op jit(solution)/shard_map/ppermute | solution.py:468
  5.8 7.3 %collective-permute-done.own_hbm.value_ref.refs_6_ = bf16[64,3072]{1,0:T(8,128)(2,1)S(1)} collective-permute-done((bf16[64,3072]{1,0:T(8,128)(2,1)}, bf16[64,3072]{1,0:T(8,128)(2,1)S(1)}, u32[]{:S(2)}, u32[]{:S(2)}) %collective-permute-start) | collective-permute-done | bytes 393248 | tf_op jit(solution)/shard_map/ppermute | solution.py:468
  13.1 0.8 collective-permute-start.5
  14.0 1.0 copy-done.3
  14.9 0.7 copy-done.5
  15.6 0.8 pack_frames.1.refs_0_
  16.4 3.3 %collective-permute-start.1 = (bf16[144,1024]{1,0:T(8,128)(2,1)S(1)}, bf16[144,1024]{1,0:T(8,128)(2,1)S(1)}, u32[]{:S(2)}, u32[]{:S(2)}) collective-permute-start(bf16[144,1024]{1,0:T(8,128)(2,1)S(1)} %pack_frames.1.refs_0_), channel_id=1, source_target_pairs={{0,1},{1,2},{2,3},{3,0},{4,5},{5,6},{6,7},{7,4},{8,9},{9,10},{10,1... | collective-permute-start | bytes 884744 | tf_op jit(solution)/shard_map/ppermute | solution.py:469
  19.7 3.0 %collective-permute-start.9 = (bf16[144,1024]{1,0:T(8,128)(2,1)S(1)}, bf16[144,1024]{1,0:T(8,128)(2,1)S(1)}, u32[]{:S(2)}, u32[]{:S(2)}) collective-permute-start(bf16[144,1024]{1,0:T(8,128)(2,1)S(1)} %pack_frames.1.refs_0_), channel_id=1, source_target_pairs={{0,3},{1,0},{2,1},{3,2},{4,7},{5,4},{6,5},{7,6},{8,11},{9,8},{10,9... | collective-permute-start | bytes 884744 | tf_op jit(solution)/shard_map/ppermute | solution.py:469
  22.7 2.4 %collective-permute-start.4 = (bf16[64,3072]{1,0:T(8,128)(2,1)S(1)}, bf16[64,3072]{1,0:T(8,128)(2,1)}, u32[]{:S(2)}, u32[]{:S(2)}) collective-permute-start(bf16[64,3072]{1,0:T(8,128)(2,1)S(1)} %collective-permute-done.own_hbm.value_ref.refs_6_), channel_id=1, source_target_pairs={{0,32},{16,48},{32,64},{48,80},{64,96},{80,112},{96,0},{112,16},{1... | collective-permute-start | bytes 1179656 | tf_op jit(solution)/shard_map/ppermute | solution.py:468
  25.1 0.1 collective-permute-start.6
  25.2 5.3 %collective-permute-done.1.refs_0_.refs_1_ = bf16[144,1024]{1,0:T(8,128)(2,1)S(1)} collective-permute-done((bf16[144,1024]{1,0:T(8,128)(2,1)S(1)}, bf16[144,1024]{1,0:T(8,128)(2,1)S(1)}, u32[]{:S(2)}, u32[]{:S(2)}) %collective-permute-start.1) | collective-permute-done | bytes 294944 | tf_op jit(solution)/shard_map/ppermute | solution.py:469
  30.4 5.5 %collective-permute-done.9.refs_1_.refs_0_ = bf16[144,1024]{1,0:T(8,128)(2,1)S(1)} collective-permute-done((bf16[144,1024]{1,0:T(8,128)(2,1)S(1)}, bf16[144,1024]{1,0:T(8,128)(2,1)S(1)}, u32[]{:S(2)}, u32[]{:S(2)}) %collective-permute-start.9) | collective-permute-done | bytes 294944 | tf_op jit(solution)/shard_map/ppermute | solution.py:469
  35.9 0.5 collective-permute-start.7
  36.5 0.7 dynamic-slice_reduce_fusion
  37.2 0.1 reshape_squeeze.3
  37.2 0.8 copy.21
  38.0 0.1 reshape.23.tgt_ref
  38.1 0.7 dynamic-slice_bitcast_fusion.where_ref
  38.8 0.1 slice_bitcast_fusion.1
  38.9 0.3 collective-permute-start.10
  39.2 1.4 %collective-permute-done.6.refs_11_ = bf16[64,3072]{1,0:T(8,128)(2,1)} collective-permute-done((bf16[64,3072]{1,0:T(8,128)(2,1)S(1)}, bf16[64,3072]{1,0:T(8,128)(2,1)}, u32[]{:S(2)}, u32[]{:S(2)}) %collective-permute-start.6) | collective-permute-done | bytes 393248 | tf_op jit(solution)/shard_map/ppermute | solution.py:468
  40.6 0.5 collective-permute-start.13
  41.1 0.1 collective-permute-start.15
  41.2 7.5 %collective-permute-done.7.refs_12_ = bf16[64,3072]{1,0:T(8,128)(2,1)} collective-permute-done((bf16[64,3072]{1,0:T(8,128)(2,1)S(1)}, bf16[64,3072]{1,0:T(8,128)(2,1)}, u32[]{:S(2)}, u32[]{:S(2)}) %collective-permute-start.7) | collective-permute-done | bytes 393248 | tf_op jit(solution)/shard_map/ppermute | solution.py:468
  48.8 0.1 pad_add_fusion.3.micro_ref
  48.8 0.1 pad_add_fusion.2.micro_ref
  48.9 0.1 pad_add_fusion.1.micro_ref
  49.0 0.1 pad_add_fusion.micro_ref
  49.1 4.0 %collective-permute-start.19 = (bf16[144,1024]{1,0:T(8,128)(2,1)S(1)}, bf16[144,1024]{1,0:T(8,128)(2,1)S(1)}, u32[]{:S(2)}, u32[]{:S(2)}) collective-permute-start(bf16[144,1024]{1,0:T(8,128)(2,1)S(1)} %collective-permute-done.1.refs_0_.refs_1_), channel_id=1, source_target_pairs={{0,1},{1,2},{2,3},{3,0},{4,5},{5,6},{6,7},{7,4},{8,9},{9,10},{10,1... | collective-permute-start | bytes 884744 | tf_op jit(solution)/shard_map/ppermute | solution.py:469
  53.1 8.7 %encode.2.after_hbm.refs_0_ = bf16[272,1024]{1,0:T(8,128)(2,1)S(1)} custom-call(s32[16]{0:T(128)S(1)} %dynamic-slice_bitcast_fusion.where_ref, bf16[144,1024]{1,0:T(8,128)(2,1)S(1)} %pack_frames.1.refs_0_, bf16[144,1024]{1,0:T(8,128)(2,1)S(1)} %collective-permute-done.1.refs_0_.refs_1_, f32[1,1024]{1,0:T(1,128)S(1)} %bitcast.48, ...), custom_call_target="tpu_custom_call" | custom-call | flops 8000000000 | bytes 8388608 | tf_op jit(solution)/shard_map/encode/pallas_call | solution.py:254
  61.8 0.0 copy-start
  61.9 1.7 %collective-permute-start.17 = (bf16[272,1024]{1,0:T(8,128)(2,1)S(1)}, bf16[272,1024]{1,0:T(8,128)(2,1)S(1)}, u32[]{:S(2)}, u32[]{:S(2)}) collective-permute-start(bf16[272,1024]{1,0:T(8,128)(2,1)S(1)} %encode.2.after_hbm.refs_0_), channel_id=1, source_target_pairs={{0,4},{1,5},{2,6},{3,7},{4,8},{5,9},{6,10},{7,11},{8,12},{9,13},{1... | collective-permute-start | bytes 1671176 | tf_op jit(solution)/shard_map/ppermute | solution.py:469
  63.5 1.7 %collective-permute-start.23 = (bf16[272,1024]{1,0:T(8,128)(2,1)S(1)}, bf16[272,1024]{1,0:T(8,128)(2,1)S(1)}, u32[]{:S(2)}, u32[]{:S(2)}) collective-permute-start(bf16[272,1024]{1,0:T(8,128)(2,1)S(1)} %encode.2.after_hbm.refs_0_), channel_id=1, source_target_pairs={{0,12},{1,13},{2,14},{3,15},{4,0},{5,1},{6,2},{7,3},{8,4},{9,5},{1... | collective-permute-start | bytes 1671176 | tf_op jit(solution)/shard_map/ppermute | solution.py:469
  65.2 1.3 %collective-permute-done.19.refs_1_ = bf16[144,1024]{1,0:T(8,128)(2,1)S(1)} collective-permute-done((bf16[144,1024]{1,0:T(8,128)(2,1)S(1)}, bf16[144,1024]{1,0:T(8,128)(2,1)S(1)}, u32[]{:S(2)}, u32[]{:S(2)}) %collective-permute-start.19) | collective-permute-done | bytes 294944 | tf_op jit(solution)/shard_map/ppermute | solution.py:469
  66.5 8.9 %encode.3.refs_1_ = bf16[272,1024]{1,0:T(8,128)(2,1)S(1)} custom-call(s32[16]{0:T(128)S(1)} %dynamic-slice_bitcast_fusion.where_ref, bf16[144,1024]{1,0:T(8,128)(2,1)S(1)} %collective-permute-done.9.refs_1_.refs_0_, bf16[144,1024]{1,0:T(8,128)(2,1)S(1)} %collective-permute-done.19.refs_1_, f32[1,1024]{1,0:T(1,128)S(1)} %bitcast.49, ...), custom_call_target="tpu_custom_call" | custom-call | flops 8000000000 | bytes 8388608 | tf_op jit(solution)/shard_map/encode/pallas_call | solution.py:254
  75.4 3.1 %collective-permute-start.20 = (bf16[272,1024]{1,0:T(8,128)(2,1)S(1)}, bf16[272,1024]{1,0:T(8,128)(2,1)S(1)}, u32[]{:S(2)}, u32[]{:S(2)}) collective-permute-start(bf16[272,1024]{1,0:T(8,128)(2,1)S(1)} %encode.3.refs_1_), channel_id=1, source_target_pairs={{0,12},{1,13},{2,14},{3,15},{4,0},{5,1},{6,2},{7,3},{8,4},{9,5},{1... | collective-permute-start | bytes 1671176 | tf_op jit(solution)/shard_map/ppermute | solution.py:469
  78.6 4.3 %project_query.1.refs_2_ = bf16[512,1024]{1,0:T(8,128)(2,1)S(1)} custom-call(bf16[512,1024]{1,0:T(8,128)(2,1)S(1)} %bitcast.29, f32[1,1024]{1,0:T(1,128)S(1)} %copy-done.4, bf16[1024,1024]{1,0:T(8,128)(2,1)S(1)} %bitcast.28, bf16[272,1024]{1,0:T(8,128)(2,1)S(1)} %encode.2.after_hbm.refs_0_), custom_call_target="tpu_custom_call" | custom-call | flops 1073741824 | bytes 4194304 | tf_op jit(solution)/shard_map/project_query/pallas_call | solution.py:126
  82.9 6.1 %decode.4.refs_7_ = bf16[512,1024]{1,0:T(8,128)(2,1)} custom-call(s32[4]{0:T(128)S(1)} %pad_add_fusion.3.micro_ref, s32[64]{0:T(128)S(1)} %reshape.23.tgt_ref, bf16[272,1024]{1,0:T(8,128)(2,1)S(1)} %encode.2.after_hbm.refs_0_, bf16[272,1024]{1,0:T(8,128)(2,1)S(1)} %encode.3.refs_1_, bf16[512,1024]{1,0:T(8,128)(2,1)S(1)} %project_query.1.refs_2_, ...), custom_call_target="tpu_custom_call" | custom-call | flops 8589934592 | bytes 8388608 | tf_op jit(solution)/shard_map/decode/pallas_call | solution.py:370
  89.0 1.6 %collective-permute-done.20.refs_1_ = bf16[272,1024]{1,0:T(8,128)(2,1)S(1)} collective-permute-done((bf16[272,1024]{1,0:T(8,128)(2,1)S(1)}, bf16[272,1024]{1,0:T(8,128)(2,1)S(1)}, u32[]{:S(2)}, u32[]{:S(2)}) %collective-permute-start.20) | collective-permute-done | bytes 557088 | tf_op jit(solution)/shard_map/ppermute | solution.py:469
  90.6 3.7 %collective-permute-start.21 = (bf16[272,1024]{1,0:T(8,128)(2,1)S(1)}, bf16[272,1024]{1,0:T(8,128)(2,1)S(1)}, u32[]{:S(2)}, u32[]{:S(2)}) collective-permute-start(bf16[272,1024]{1,0:T(8,128)(2,1)S(1)} %collective-permute-done.20.refs_1_), channel_id=1, source_target_pairs={{0,12},{1,13},{2,14},{3,15},{4,0},{5,1},{6,2},{7,3},{8,4},{9,5},{1... | collective-permute-start | bytes 1671176 | tf_op jit(solution)/shard_map/ppermute | solution.py:469
  94.3 6.1 %decode.5.refs_7_ = bf16[512,1024]{1,0:T(8,128)(2,1)} custom-call(s32[4]{0:T(128)S(1)} %pad_add_fusion.2.micro_ref, s32[64]{0:T(128)S(1)} %reshape.23.tgt_ref, bf16[272,1024]{1,0:T(8,128)(2,1)S(1)} %collective-permute-done.17.refs_0_, bf16[272,1024]{1,0:T(8,128)(2,1)S(1)} %collective-permute-done.23.refs_1_, ...), custom_call_target="tpu_custom_call", output_to_operand_aliasing={{}: (9, {})} | custom-call | flops 8589934592 | bytes 8388608 | tf_op jit(solution)/shard_map/decode/pallas_call | solution.py:370
  100.5 6.2 %decode.6.refs_7_ = bf16[512,1024]{1,0:T(8,128)(2,1)} custom-call(s32[4]{0:T(128)S(1)} %pad_add_fusion.1.micro_ref, s32[64]{0:T(128)S(1)} %reshape.23.tgt_ref, bf16[272,1024]{1,0:T(8,128)(2,1)S(1)} %collective-permute-done.22.refs_0_, bf16[272,1024]{1,0:T(8,128)(2,1)S(1)} %collective-permute-done.20.refs_1_, ...), custom_call_target="tpu_custom_call", output_to_operand_aliasing={{}: (9, {})} | custom-call | flops 8589934592 | bytes 8388608 | tf_op jit(solution)/shard_map/decode/pallas_call | solution.py:370
  106.7 2.3 %collective-permute-done.18.refs_0_ = bf16[272,1024]{1,0:T(8,128)(2,1)S(1)} collective-permute-done((bf16[272,1024]{1,0:T(8,128)(2,1)S(1)}, bf16[272,1024]{1,0:T(8,128)(2,1)S(1)}, u32[]{:S(2)}, u32[]{:S(2)}) %collective-permute-start.18) | collective-permute-done | bytes 557088 | tf_op jit(solution)/shard_map/ppermute | solution.py:469
  109.0 6.1 %decode.7 = bf16[512,1024]{1,0:T(8,128)(2,1)} custom-call(s32[4]{0:T(128)S(1)} %pad_add_fusion.micro_ref, s32[64]{0:T(128)S(1)} %reshape.23.tgt_ref, bf16[272,1024]{1,0:T(8,128)(2,1)S(1)} %collective-permute-done.18.refs_0_, bf16[272,1024]{1,0:T(8,128)(2,1)S(1)} %collective-permute-done.21.refs_1_, ...), custom_call_target="tpu_custom_call", output_to_operand_aliasing={{}: (9, {})} | custom-call | flops 8589934592 | bytes 8388608 | tf_op jit(solution)/shard_map/decode/pallas_call | solution.py:370
  (44 shorter events, 0.1 us)
Async XLA Ops:
  0.0 53.1 %copy-start.10 = (f32[1024]{0:T(1024)S(1)}, f32[1024]{0:T(1024)}, u32[]{:S(2)}) copy-start(f32[1024]{0:T(1024)} %param.19) | copy-start | bytes 12292
  0.0 53.1 %copy-start.11 = (f32[1024]{0:T(1024)S(1)}, f32[1024]{0:T(1024)}, u32[]{:S(2)}) copy-start(f32[1024]{0:T(1024)} %param.22) | copy-start | bytes 12292
  0.0 53.1 %copy-start.9 = (bf16[31,1024]{1,0:T(8,128)(2,1)S(1)}, bf16[31,1024]{1,0:T(8,128)(2,1)}, u32[]{:S(2)}) copy-start(bf16[31,1024]{1,0:T(8,128)(2,1)} %refs_3_.3) | copy-start | bytes 190468
  1.8 51.3 %copy-start.2 = (bf16[64,3072]{1,0:T(8,128)(2,1)S(1)}, bf16[64,3072]{1,0:T(8,128)(2,1)}, u32[]{:S(2)}) copy-start(bf16[64,3072]{1,0:T(8,128)(2,1)} %join_shards.1.refs_5_) | copy-start | bytes 1179652
  1.8 11.3 %collective-permute-start = (bf16[64,3072]{1,0:T(8,128)(2,1)}, bf16[64,3072]{1,0:T(8,128)(2,1)S(1)}, u32[]{:S(2)}, u32[]{:S(2)}) collective-permute-start(bf16[64,3072]{1,0:T(8,128)(2,1)} %join_shards.1.refs_5_), channel_id=1, source_target_pairs={{0,128},{16,144},{32,160},{48,176},{64,192},{80,208},{96,224},{112... | collective-permute-start | bytes 1179656 | tf_op jit(solution)/shard_map/ppermute | solution.py:468
  3.8 15.9 %collective-permute-start.2 = (bf16[64,3072]{1,0:T(8,128)(2,1)}, bf16[64,3072]{1,0:T(8,128)(2,1)S(1)}, u32[]{:S(2)}, u32[]{:S(2)}) collective-permute-start(bf16[64,3072]{1,0:T(8,128)(2,1)} %join_shards.1.refs_5_), channel_id=1, source_target_pairs={{0,32},{16,48},{32,64},{48,80},{64,96},{80,112},{96,0},{112,16},{1... | collective-permute-start | bytes 1179656 | tf_op jit(solution)/shard_map/ppermute | solution.py:468
  4.3 18.4 %collective-permute-start.3 = (bf16[64,3072]{1,0:T(8,128)(2,1)}, bf16[64,3072]{1,0:T(8,128)(2,1)S(1)}, u32[]{:S(2)}, u32[]{:S(2)}) collective-permute-start(bf16[64,3072]{1,0:T(8,128)(2,1)} %join_shards.1.refs_5_), channel_id=1, source_target_pairs={{0,96},{16,112},{32,0},{48,16},{64,32},{80,48},{96,64},{112,80},{1... | collective-permute-start | bytes 1179656 | tf_op jit(solution)/shard_map/ppermute | solution.py:468
  5.8 19.2 %collective-permute-start.8 = (bf16[64,3072]{1,0:T(8,128)(2,1)}, bf16[64,3072]{1,0:T(8,128)(2,1)S(1)}, u32[]{:S(2)}, u32[]{:S(2)}) collective-permute-start(bf16[64,3072]{1,0:T(8,128)(2,1)} %join_shards.1.refs_5_), channel_id=1, source_target_pairs={{0,16},{16,0},{32,48},{48,32},{64,80},{80,64},{96,112},{112,96},{1... | collective-permute-start | bytes 1179656 | tf_op jit(solution)/shard_map/ppermute | solution.py:468
  13.1 22.8 %collective-permute-start.5 = (bf16[64,3072]{1,0:T(8,128)(2,1)S(1)}, bf16[64,3072]{1,0:T(8,128)(2,1)S(1)}, u32[]{:S(2)}, u32[]{:S(2)}) collective-permute-start(bf16[64,3072]{1,0:T(8,128)(2,1)S(1)} %collective-permute-done.own_hbm.value_ref.refs_6_), channel_id=1, source_target_pairs={{0,96},{16,112},{32,0},{48,16},{64,32},{80,48},{96,64},{112,80},{1... | collective-permute-start | bytes 1179656 | tf_op jit(solution)/shard_map/ppermute | solution.py:468
  14.0 1.0 copy-start.3
  14.9 0.7 copy-start.5
  16.4 14.1 %collective-permute-start.1 = (bf16[144,1024]{1,0:T(8,128)(2,1)S(1)}, bf16[144,1024]{1,0:T(8,128)(2,1)S(1)}, u32[]{:S(2)}, u32[]{:S(2)}) collective-permute-start(bf16[144,1024]{1,0:T(8,128)(2,1)S(1)} %pack_frames.1.refs_0_), channel_id=1, source_target_pairs={{0,1},{1,2},{2,3},{3,0},{4,5},{5,6},{6,7},{7,4},{8,9},{9,10},{10,1... | collective-permute-start | bytes 884744 | tf_op jit(solution)/shard_map/ppermute | solution.py:469
  19.7 16.2 %collective-permute-start.9 = (bf16[144,1024]{1,0:T(8,128)(2,1)S(1)}, bf16[144,1024]{1,0:T(8,128)(2,1)S(1)}, u32[]{:S(2)}, u32[]{:S(2)}) collective-permute-start(bf16[144,1024]{1,0:T(8,128)(2,1)S(1)} %pack_frames.1.refs_0_), channel_id=1, source_target_pairs={{0,3},{1,0},{2,1},{3,2},{4,7},{5,4},{6,5},{7,6},{8,11},{9,8},{10,9... | collective-permute-start | bytes 884744 | tf_op jit(solution)/shard_map/ppermute | solution.py:469
  22.7 16.2 %collective-permute-start.4 = (bf16[64,3072]{1,0:T(8,128)(2,1)S(1)}, bf16[64,3072]{1,0:T(8,128)(2,1)}, u32[]{:S(2)}, u32[]{:S(2)}) collective-permute-start(bf16[64,3072]{1,0:T(8,128)(2,1)S(1)} %collective-permute-done.own_hbm.value_ref.refs_6_), channel_id=1, source_target_pairs={{0,32},{16,48},{32,64},{48,80},{64,96},{80,112},{96,0},{112,16},{1... | collective-permute-start | bytes 1179656 | tf_op jit(solution)/shard_map/ppermute | solution.py:468
  25.1 15.5 %collective-permute-start.6 = (bf16[64,3072]{1,0:T(8,128)(2,1)S(1)}, bf16[64,3072]{1,0:T(8,128)(2,1)}, u32[]{:S(2)}, u32[]{:S(2)}) collective-permute-start(bf16[64,3072]{1,0:T(8,128)(2,1)S(1)} %collective-permute-done.2.refs_7_), channel_id=1, source_target_pairs={{0,32},{16,48},{32,64},{48,80},{64,96},{80,112},{96,0},{112,16},{1... | collective-permute-start | bytes 1179656 | tf_op jit(solution)/shard_map/ppermute | solution.py:468
  30.4 10.2 %collective-permute-start.11 = (bf16[64,3072]{1,0:T(8,128)(2,1)S(1)}, bf16[64,3072]{1,0:T(8,128)(2,1)}, u32[]{:S(2)}, u32[]{:S(2)}) collective-permute-start(bf16[64,3072]{1,0:T(8,128)(2,1)S(1)} %collective-permute-done.2.refs_7_), channel_id=1, source_target_pairs={{0,16},{16,0},{32,48},{48,32},{64,80},{80,64},{96,112},{112,96},{1... | collective-permute-start | bytes 1179656 | tf_op jit(solution)/shard_map/ppermute | solution.py:468
  35.9 5.2 %collective-permute-start.12 = (bf16[64,3072]{1,0:T(8,128)(2,1)S(1)}, bf16[64,3072]{1,0:T(8,128)(2,1)}, u32[]{:S(2)}, u32[]{:S(2)}) collective-permute-start(bf16[64,3072]{1,0:T(8,128)(2,1)S(1)} %collective-permute-done.3.refs_8_), channel_id=1, source_target_pairs={{0,16},{16,0},{32,48},{48,32},{64,80},{80,64},{96,112},{112,96},{1... | collective-permute-start | bytes 1179656 | tf_op jit(solution)/shard_map/ppermute | solution.py:468
  35.9 12.8 %collective-permute-start.7 = (bf16[64,3072]{1,0:T(8,128)(2,1)S(1)}, bf16[64,3072]{1,0:T(8,128)(2,1)}, u32[]{:S(2)}, u32[]{:S(2)}) collective-permute-start(bf16[64,3072]{1,0:T(8,128)(2,1)S(1)} %collective-permute-done.5.refs_10_), channel_id=1, source_target_pairs={{0,96},{16,112},{32,0},{48,16},{64,32},{80,48},{96,64},{112,80},{1... | collective-permute-start | bytes 1179656 | tf_op jit(solution)/shard_map/ppermute | solution.py:468
  38.9 10.2 %collective-permute-start.10 = (bf16[64,3072]{1,0:T(8,128)(2,1)S(1)}, bf16[64,3072]{1,0:T(8,128)(2,1)S(1)}, u32[]{:S(2)}, u32[]{:S(2)}) collective-permute-start(bf16[64,3072]{1,0:T(8,128)(2,1)S(1)} %pass_after.1), channel_id=1, source_target_pairs={{0,16},{16,0},{32,48},{48,32},{64,80},{80,64},{96,112},{112,96},{1... | collective-permute-start | bytes 1179656 | tf_op jit(solution)/shard_map/ppermute | solution.py:468
  40.6 12.4 %collective-permute-start.14 = (bf16[64,3072]{1,0:T(8,128)(2,1)S(1)}, bf16[64,3072]{1,0:T(8,128)(2,1)S(1)}, u32[]{:S(2)}, u32[]{:S(2)}) collective-permute-start(bf16[64,3072]{1,0:T(8,128)(2,1)S(1)} %collective-permute-done.5.refs_10_), channel_id=1, source_target_pairs={{0,16},{16,0},{32,48},{48,32},{64,80},{80,64},{96,112},{112,96},{1... | collective-permute-start | bytes 1179656 | tf_op jit(solution)/shard_map/ppermute | solution.py:468
  40.6 12.4 %collective-permute-start.13 = (bf16[64,3072]{1,0:T(8,128)(2,1)}, bf16[64,3072]{1,0:T(8,128)(2,1)S(1)}, u32[]{:S(2)}, u32[]{:S(2)}) collective-permute-start(bf16[64,3072]{1,0:T(8,128)(2,1)} %collective-permute-done.4.refs_9_), channel_id=1, source_target_pairs={{0,16},{16,0},{32,48},{48,32},{64,80},{80,64},{96,112},{112,96},{1... | collective-permute-start | bytes 1179656 | tf_op jit(solution)/shard_map/ppermute | solution.py:468
  41.1 11.9 %collective-permute-start.15 = (bf16[64,3072]{1,0:T(8,128)(2,1)}, bf16[64,3072]{1,0:T(8,128)(2,1)S(1)}, u32[]{:S(2)}, u32[]{:S(2)}) collective-permute-start(bf16[64,3072]{1,0:T(8,128)(2,1)} %collective-permute-done.6.refs_11_), channel_id=1, source_target_pairs={{0,16},{16,0},{32,48},{48,32},{64,80},{80,64},{96,112},{112,96},{1... | collective-permute-start | bytes 1179656 | tf_op jit(solution)/shard_map/ppermute | solution.py:468
  48.8 4.3 %collective-permute-start.16 = (bf16[64,3072]{1,0:T(8,128)(2,1)}, bf16[64,3072]{1,0:T(8,128)(2,1)S(1)}, u32[]{:S(2)}, u32[]{:S(2)}) collective-permute-start(bf16[64,3072]{1,0:T(8,128)(2,1)} %collective-permute-done.7.refs_12_), channel_id=1, source_target_pairs={{0,16},{16,0},{32,48},{48,32},{64,80},{80,64},{96,112},{112,96},{1... | collective-permute-start | bytes 1179656 | tf_op jit(solution)/shard_map/ppermute | solution.py:468
  49.1 17.5 %collective-permute-start.19 = (bf16[144,1024]{1,0:T(8,128)(2,1)S(1)}, bf16[144,1024]{1,0:T(8,128)(2,1)S(1)}, u32[]{:S(2)}, u32[]{:S(2)}) collective-permute-start(bf16[144,1024]{1,0:T(8,128)(2,1)S(1)} %collective-permute-done.1.refs_0_.refs_1_), channel_id=1, source_target_pairs={{0,1},{1,2},{2,3},{3,0},{4,5},{5,6},{6,7},{7,4},{8,9},{9,10},{10,1... | collective-permute-start | bytes 884744 | tf_op jit(solution)/shard_map/ppermute | solution.py:469
  61.8 16.7 %copy-start = (bf16[1,1024,1024]{2,1,0:T(8,128)(2,1)S(1)}, bf16[1,1024,1024]{2,1,0:T(8,128)(2,1)}, u32[]{:S(2)}) copy-start(bf16[1,1024,1024]{2,1,0:T(8,128)(2,1)} %param.25) | copy-start | bytes 6291460
  61.9 16.7 %copy-start.1 = (bf16[1,16,4,8,1024]{4,3,2,1,0:T(8,128)(2,1)S(1)}, bf16[1,16,4,8,1024]{4,3,2,1,0:T(8,128)(2,1)}, u32[]{:S(2)}) copy-start(bf16[1,16,4,8,1024]{4,3,2,1,0:T(8,128)(2,1)} %param.29) | copy-start | bytes 3145732
  61.9 16.7 %copy-start.4 = (f32[1,1024]{1,0:T(1,128)S(1)}, f32[1,1024]{1,0:T(1,128)}, u32[]{:S(2)}) copy-start(f32[1,1024]{1,0:T(1,128)} %gain_ref.1) | copy-start | bytes 12292
  61.9 32.5 %collective-permute-start.17 = (bf16[272,1024]{1,0:T(8,128)(2,1)S(1)}, bf16[272,1024]{1,0:T(8,128)(2,1)S(1)}, u32[]{:S(2)}, u32[]{:S(2)}) collective-permute-start(bf16[272,1024]{1,0:T(8,128)(2,1)S(1)} %encode.2.after_hbm.refs_0_), channel_id=1, source_target_pairs={{0,4},{1,5},{2,6},{3,7},{4,8},{5,9},{6,10},{7,11},{8,12},{9,13},{1... | collective-permute-start | bytes 1671176 | tf_op jit(solution)/shard_map/ppermute | solution.py:469
  63.5 30.8 %collective-permute-start.23 = (bf16[272,1024]{1,0:T(8,128)(2,1)S(1)}, bf16[272,1024]{1,0:T(8,128)(2,1)S(1)}, u32[]{:S(2)}, u32[]{:S(2)}) collective-permute-start(bf16[272,1024]{1,0:T(8,128)(2,1)S(1)} %encode.2.after_hbm.refs_0_), channel_id=1, source_target_pairs={{0,12},{1,13},{2,14},{3,15},{4,0},{5,1},{6,2},{7,3},{8,4},{9,5},{1... | collective-permute-start | bytes 1671176 | tf_op jit(solution)/shard_map/ppermute | solution.py:469
  66.5 16.3 %copy-start.8 = (bf16[1,1024,1024]{2,1,0:T(8,128)(2,1)S(1)}, bf16[1,1024,1024]{2,1,0:T(8,128)(2,1)}, u32[]{:S(2)}) copy-start(bf16[1,1024,1024]{2,1,0:T(8,128)(2,1)} %param.28) | copy-start | bytes 6291460
  75.4 15.2 %collective-permute-start.20 = (bf16[272,1024]{1,0:T(8,128)(2,1)S(1)}, bf16[272,1024]{1,0:T(8,128)(2,1)S(1)}, u32[]{:S(2)}, u32[]{:S(2)}) collective-permute-start(bf16[272,1024]{1,0:T(8,128)(2,1)S(1)} %encode.3.refs_1_), channel_id=1, source_target_pairs={{0,12},{1,13},{2,14},{3,15},{4,0},{5,1},{6,2},{7,3},{8,4},{9,5},{1... | collective-permute-start | bytes 1671176 | tf_op jit(solution)/shard_map/ppermute | solution.py:469
  78.5 22.0 %collective-permute-start.22 = (bf16[272,1024]{1,0:T(8,128)(2,1)S(1)}, bf16[272,1024]{1,0:T(8,128)(2,1)S(1)}, u32[]{:S(2)}, u32[]{:S(2)}) collective-permute-start(bf16[272,1024]{1,0:T(8,128)(2,1)S(1)} %encode.3.refs_1_), channel_id=1, source_target_pairs={{0,4},{1,5},{2,6},{3,7},{4,8},{5,9},{6,10},{7,11},{8,12},{9,13},{1... | collective-permute-start | bytes 1671176 | tf_op jit(solution)/shard_map/ppermute | solution.py:469
  78.5 4.4 %copy-start.6 = (bf16[1,1024,1024]{2,1,0:T(8,128)(2,1)S(1)}, bf16[1,1024,1024]{2,1,0:T(8,128)(2,1)}, u32[]{:S(2)}) copy-start(bf16[1,1024,1024]{2,1,0:T(8,128)(2,1)} %param.26) | copy-start | bytes 6291460
  78.5 4.4 %copy-start.7 = (bf16[1,1024,1024]{2,1,0:T(8,128)(2,1)S(1)}, bf16[1,1024,1024]{2,1,0:T(8,128)(2,1)}, u32[]{:S(2)}) copy-start(bf16[1,1024,1024]{2,1,0:T(8,128)(2,1)} %param.27) | copy-start | bytes 6291460
  90.6 16.0 %collective-permute-start.21 = (bf16[272,1024]{1,0:T(8,128)(2,1)S(1)}, bf16[272,1024]{1,0:T(8,128)(2,1)S(1)}, u32[]{:S(2)}, u32[]{:S(2)}) collective-permute-start(bf16[272,1024]{1,0:T(8,128)(2,1)S(1)} %collective-permute-done.20.refs_1_), channel_id=1, source_target_pairs={{0,12},{1,13},{2,14},{3,15},{4,0},{5,1},{6,2},{7,3},{8,4},{9,5},{1... | collective-permute-start | bytes 1671176 | tf_op jit(solution)/shard_map/ppermute | solution.py:469
  94.3 14.7 %collective-permute-start.18 = (bf16[272,1024]{1,0:T(8,128)(2,1)S(1)}, bf16[272,1024]{1,0:T(8,128)(2,1)S(1)}, u32[]{:S(2)}, u32[]{:S(2)}) collective-permute-start(bf16[272,1024]{1,0:T(8,128)(2,1)S(1)} %collective-permute-done.17.refs_0_), channel_id=1, source_target_pairs={{0,4},{1,5},{2,6},{3,7},{4,8},{5,9},{6,10},{7,11},{8,12},{9,13},{1... | collective-permute-start | bytes 1671176 | tf_op jit(solution)/shard_map/ppermute | solution.py:469

commit v5 on v4

--- a/solution.py
+++ b/solution.py
@@ -180,15 +180,10 @@
     w_refs = blocks[: n_w // 2], blocks[n_w // 2 :]
     step = 16
     for i, x in enumerate(x_refs):
-
-        @pl.loop(0, 2)
-        def _(h):
-            for r in range(0, TOT // 2, step):
-                at = pl.multiple_of(h * (TOT // 2) + r, step)
-                plain[pl.ds(i * TOT + at, step), :] = norm_rows(
-                    x[pl.ds(at, step), :].astype(F32), gain_in_ref[...]
-                ).astype(BF)
-
+        for r in range(0, TOT, step):
+            plain[i * TOT + r : i * TOT + r + step, :] = norm_rows(
+                x[r : r + step, :].astype(F32), gain_in_ref[...]
+            ).astype(BF)
     order_columns(normed, plain, where_ref)
     taps[...] = dw_ref[...].astype(F32)
     rows = normed.shape[0]
@@ -334,10 +329,9 @@
 
     pos = lax.broadcasted_iota(jnp.int32, (slots, 256), 0)
 
-    @pl.loop(0, D // 512)
-    def _(h):
-      for half in range(2):
-        cols = pl.ds(pl.multiple_of(h * 512 + half * 256, 256), 256)
+    @pl.loop(0, D // 256)
+    def _(j):
+        cols = pl.ds(pl.multiple_of(j * 256, 256), 256)
         proj = jnp.dot(ctx[...], wo[:, cols], preferred_element_type=F32)
         for i in range(micros):
             mine = slice(i * slots, (i + 1) * slots)

time: 116 us -> 117 us (level)
  Pallas kernels: 49.1 us -> 51.6 us
  waiting for transfers between devices: 32.3 us -> 30.6 us
    ppermute x9, waiting for transfers between devices: 16 us -> 14.4 us  [body(): along = lambda v, dy, dz: lax.ppermute(v, 'section', section_perm(dy, dz))]
    pallas_call x4, Pallas kernels: 24.6 us -> 26 us  [decode(): pl.pallas_call(functools.partial(decode_kernel, len(mems), aliased), out_...]
  transfers between devices with their start and end apart: 24 -> 24, of which waited for: 8 -> 8; matrix products, arithmetic and copies ran while one was open for 2% -> 2% of each run, Pallas kernels for 36% -> 37%
where the time goes in v5:
time: 117 us; the launch traced here: 116 us
  Pallas kernels  51.6 us (44%)
  waiting for transfers between devices  30.6 us (26%)
  starting transfers between devices  29.2 us (25%)
  local copies, waits for them, and re-layouts  4.09 us (3%)
    pallas_call x4, Pallas kernels, decode(): pl.pallas_call(functools.partial(decode_kernel, len(mems), aliased), out_...  26 us
    ppermute x9, starting transfers between devices, body(): along = lambda v, dy, dz: lax.ppermute(v, 'section', section_perm(dy, dz))  20.4 us
    pallas_call x2, Pallas kernels, encode(): pl.pallas_call(functools.partial(encode_kernel, len(shards)), out_shape=j...  18.7 us
    ppermute x15, waiting for transfers between devices, body(): across = lambda v, perm: lax.ppermute(v, 'dp', perm)  16.3 us
    ppermute x9, waiting for transfers between devices, body(): along = lambda v, dy, dz: lax.ppermute(v, 'section', section_perm(dy, dz))  14.4 us
    ppermute x15, starting transfers between devices, body(): across = lambda v, perm: lax.ppermute(v, 'dp', perm)  8.81 us
    pallas_call x1, Pallas kernels, project_query(): pl.pallas_call(query_kernel, out_shape=jax.ShapeDtypeStruct((rows, D), BF...  4.32 us
    unnamed x25, local copies, waits for them, and re-layouts  2.44 us
  transfers between devices with their start and end apart: 24, of which 8 were waited for; matrix products, arithmetic and copies ran while one was open for 2% of the time, Pallas kernels for 37%

profile of v5, /device:TPU:6, one launch (start us, length us, event | category | flops | bytes accessed | tf_op | source)
XLA Modules:
  0.0 116.2 jit_solution(886120246433801314)
XLA Ops:
  0.0 1.8 %join_shards.1.refs_5_ = bf16[64,3072]{1,0:T(8,128)(2,1)} custom-call(bf16[64,2048]{1,0:T(8,128)(2,1)} %w_in_hbm.1, bf16[64,1024]{1,0:T(8,128)(2,1)} %w_out_hbm.1), custom_call_target="tpu_custom_call" | custom-call | bytes 800000 | tf_op jit(solution)/shard_map/join_shards/pallas_call | solution.py:71
  1.8 2.0 %collective-permute-start = (bf16[64,3072]{1,0:T(8,128)(2,1)}, bf16[64,3072]{1,0:T(8,128)(2,1)S(1)}, u32[]{:S(2)}, u32[]{:S(2)}) collective-permute-start(bf16[64,3072]{1,0:T(8,128)(2,1)} %join_shards.1.refs_5_), channel_id=1, source_target_pairs={{0,128},{16,144},{32,160},{48,176},{64,192},{80,208},{96,224},{112... | collective-permute-start | bytes 1179656 | tf_op jit(solution)/shard_map/ppermute | solution.py:462
  3.8 0.5 collective-permute-start.2
  4.3 1.5 %collective-permute-start.3 = (bf16[64,3072]{1,0:T(8,128)(2,1)}, bf16[64,3072]{1,0:T(8,128)(2,1)S(1)}, u32[]{:S(2)}, u32[]{:S(2)}) collective-permute-start(bf16[64,3072]{1,0:T(8,128)(2,1)} %join_shards.1.refs_5_), channel_id=1, source_target_pairs={{0,96},{16,112},{32,0},{48,16},{64,32},{80,48},{96,64},{112,80},{1... | collective-permute-start | bytes 1179656 | tf_op jit(solution)/shard_map/ppermute | solution.py:462
  5.8 7.3 %collective-permute-done.own_hbm.value_ref.refs_6_ = bf16[64,3072]{1,0:T(8,128)(2,1)S(1)} collective-permute-done((bf16[64,3072]{1,0:T(8,128)(2,1)}, bf16[64,3072]{1,0:T(8,128)(2,1)S(1)}, u32[]{:S(2)}, u32[]{:S(2)}) %collective-permute-start) | collective-permute-done | bytes 393248 | tf_op jit(solution)/shard_map/ppermute | solution.py:462
  13.1 0.8 collective-permute-start.5
  14.0 1.0 copy-done.3
  14.9 0.7 copy-done.5
  15.6 0.8 pack_frames.1.refs_0_
  16.4 3.3 %collective-permute-start.1 = (bf16[144,1024]{1,0:T(8,128)(2,1)S(1)}, bf16[144,1024]{1,0:T(8,128)(2,1)S(1)}, u32[]{:S(2)}, u32[]{:S(2)}) collective-permute-start(bf16[144,1024]{1,0:T(8,128)(2,1)S(1)} %pack_frames.1.refs_0_), channel_id=1, source_target_pairs={{0,1},{1,2},{2,3},{3,0},{4,5},{5,6},{6,7},{7,4},{8,9},{9,10},{10,1... | collective-permute-start | bytes 884744 | tf_op jit(solution)/shard_map/ppermute | solution.py:463
  19.7 3.0 %collective-permute-start.9 = (bf16[144,1024]{1,0:T(8,128)(2,1)S(1)}, bf16[144,1024]{1,0:T(8,128)(2,1)S(1)}, u32[]{:S(2)}, u32[]{:S(2)}) collective-permute-start(bf16[144,1024]{1,0:T(8,128)(2,1)S(1)} %pack_frames.1.refs_0_), channel_id=1, source_target_pairs={{0,3},{1,0},{2,1},{3,2},{4,7},{5,4},{6,5},{7,6},{8,11},{9,8},{10,9... | collective-permute-start | bytes 884744 | tf_op jit(solution)/shard_map/ppermute | solution.py:463
  22.7 2.4 %collective-permute-start.4 = (bf16[64,3072]{1,0:T(8,128)(2,1)S(1)}, bf16[64,3072]{1,0:T(8,128)(2,1)}, u32[]{:S(2)}, u32[]{:S(2)}) collective-permute-start(bf16[64,3072]{1,0:T(8,128)(2,1)S(1)} %collective-permute-done.own_hbm.value_ref.refs_6_), channel_id=1, source_target_pairs={{0,32},{16,48},{32,64},{48,80},{64,96},{80,112},{96,0},{112,16},{1... | collective-permute-start | bytes 1179656 | tf_op jit(solution)/shard_map/ppermute | solution.py:462
  25.1 0.1 collective-permute-start.6
  25.2 5.3 %collective-permute-done.1.refs_0_.refs_1_ = bf16[144,1024]{1,0:T(8,128)(2,1)S(1)} collective-permute-done((bf16[144,1024]{1,0:T(8,128)(2,1)S(1)}, bf16[144,1024]{1,0:T(8,128)(2,1)S(1)}, u32[]{:S(2)}, u32[]{:S(2)}) %collective-permute-start.1) | collective-permute-done | bytes 294944 | tf_op jit(solution)/shard_map/ppermute | solution.py:463
  30.4 5.5 %collective-permute-done.9.refs_1_.refs_0_ = bf16[144,1024]{1,0:T(8,128)(2,1)S(1)} collective-permute-done((bf16[144,1024]{1,0:T(8,128)(2,1)S(1)}, bf16[144,1024]{1,0:T(8,128)(2,1)S(1)}, u32[]{:S(2)}, u32[]{:S(2)}) %collective-permute-start.9) | collective-permute-done | bytes 294944 | tf_op jit(solution)/shard_map/ppermute | solution.py:463
  35.9 0.5 collective-permute-start.7
  36.5 0.7 dynamic-slice_reduce_fusion
  37.2 0.1 reshape_squeeze.3
  37.2 0.8 copy.21
  38.0 0.1 reshape.23.tgt_ref
  38.1 0.7 dynamic-slice_bitcast_fusion.where_ref
  38.8 0.1 slice_bitcast_fusion.1
  38.9 0.3 collective-permute-start.10
  39.2 1.4 %collective-permute-done.6.refs_11_ = bf16[64,3072]{1,0:T(8,128)(2,1)} collective-permute-done((bf16[64,3072]{1,0:T(8,128)(2,1)S(1)}, bf16[64,3072]{1,0:T(8,128)(2,1)}, u32[]{:S(2)}, u32[]{:S(2)}) %collective-permute-start.6) | collective-permute-done | bytes 393248 | tf_op jit(solution)/shard_map/ppermute | solution.py:462
  40.6 0.5 collective-permute-start.13
  41.1 0.1 collective-permute-start.15
  41.2 7.5 %collective-permute-done.7.refs_12_ = bf16[64,3072]{1,0:T(8,128)(2,1)} collective-permute-done((bf16[64,3072]{1,0:T(8,128)(2,1)S(1)}, bf16[64,3072]{1,0:T(8,128)(2,1)}, u32[]{:S(2)}, u32[]{:S(2)}) %collective-permute-start.7) | collective-permute-done | bytes 393248 | tf_op jit(solution)/shard_map/ppermute | solution.py:462
  48.8 0.1 pad_add_fusion.3.micro_ref
  48.8 0.1 pad_add_fusion.2.micro_ref
  48.9 0.1 pad_add_fusion.1.micro_ref
  49.0 0.1 pad_add_fusion.micro_ref
  49.1 4.0 %collective-permute-start.19 = (bf16[144,1024]{1,0:T(8,128)(2,1)S(1)}, bf16[144,1024]{1,0:T(8,128)(2,1)S(1)}, u32[]{:S(2)}, u32[]{:S(2)}) collective-permute-start(bf16[144,1024]{1,0:T(8,128)(2,1)S(1)} %collective-permute-done.1.refs_0_.refs_1_), channel_id=1, source_target_pairs={{0,1},{1,2},{2,3},{3,0},{4,5},{5,6},{6,7},{7,4},{8,9},{9,10},{10,1... | collective-permute-start | bytes 884744 | tf_op jit(solution)/shard_map/ppermute | solution.py:463
  53.1 9.3 %encode.2.after_hbm.refs_0_ = bf16[272,1024]{1,0:T(8,128)(2,1)S(1)} custom-call(s32[16]{0:T(128)S(1)} %dynamic-slice_bitcast_fusion.where_ref, bf16[144,1024]{1,0:T(8,128)(2,1)S(1)} %pack_frames.1.refs_0_, bf16[144,1024]{1,0:T(8,128)(2,1)S(1)} %collective-permute-done.1.refs_0_.refs_1_, f32[1,1024]{1,0:T(1,128)S(1)} %bitcast.48, ...), custom_call_target="tpu_custom_call" | custom-call | flops 8000000000 | bytes 8388608 | tf_op jit(solution)/shard_map/encode/pallas_call | solution.py:249
  62.4 0.0 copy-start
  62.4 0.0 copy-start.1
  62.4 1.7 %collective-permute-start.17 = (bf16[272,1024]{1,0:T(8,128)(2,1)S(1)}, bf16[272,1024]{1,0:T(8,128)(2,1)S(1)}, u32[]{:S(2)}, u32[]{:S(2)}) collective-permute-start(bf16[272,1024]{1,0:T(8,128)(2,1)S(1)} %encode.2.after_hbm.refs_0_), channel_id=1, source_target_pairs={{0,4},{1,5},{2,6},{3,7},{4,8},{5,9},{6,10},{7,11},{8,12},{9,13},{1... | collective-permute-start | bytes 1671176 | tf_op jit(solution)/shard_map/ppermute | solution.py:463
  64.1 1.7 %collective-permute-start.23 = (bf16[272,1024]{1,0:T(8,128)(2,1)S(1)}, bf16[272,1024]{1,0:T(8,128)(2,1)S(1)}, u32[]{:S(2)}, u32[]{:S(2)}) collective-permute-start(bf16[272,1024]{1,0:T(8,128)(2,1)S(1)} %encode.2.after_hbm.refs_0_), channel_id=1, source_target_pairs={{0,12},{1,13},{2,14},{3,15},{4,0},{5,1},{6,2},{7,3},{8,4},{9,5},{1... | collective-permute-start | bytes 1671176 | tf_op jit(solution)/shard_map/ppermute | solution.py:463
  65.7 0.8 collective-permute-done.19.refs_1_
  66.5 9.4 %encode.3.refs_1_ = bf16[272,1024]{1,0:T(8,128)(2,1)S(1)} custom-call(s32[16]{0:T(128)S(1)} %dynamic-slice_bitcast_fusion.where_ref, bf16[144,1024]{1,0:T(8,128)(2,1)S(1)} %collective-permute-done.9.refs_1_.refs_0_, bf16[144,1024]{1,0:T(8,128)(2,1)S(1)} %collective-permute-done.19.refs_1_, f32[1,1024]{1,0:T(1,128)S(1)} %bitcast.49, ...), custom_call_target="tpu_custom_call" | custom-call | flops 8000000000 | bytes 8388608 | tf_op jit(solution)/shard_map/encode/pallas_call | solution.py:249
  76.0 3.1 %collective-permute-start.20 = (bf16[272,1024]{1,0:T(8,128)(2,1)S(1)}, bf16[272,1024]{1,0:T(8,128)(2,1)S(1)}, u32[]{:S(2)}, u32[]{:S(2)}) collective-permute-start(bf16[272,1024]{1,0:T(8,128)(2,1)S(1)} %encode.3.refs_1_), channel_id=1, source_target_pairs={{0,12},{1,13},{2,14},{3,15},{4,0},{5,1},{6,2},{7,3},{8,4},{9,5},{1... | collective-permute-start | bytes 1671176 | tf_op jit(solution)/shard_map/ppermute | solution.py:463
  79.1 4.3 %project_query.1.refs_2_ = bf16[512,1024]{1,0:T(8,128)(2,1)S(1)} custom-call(bf16[512,1024]{1,0:T(8,128)(2,1)S(1)} %bitcast.29, f32[1,1024]{1,0:T(1,128)S(1)} %copy-done.4, bf16[1024,1024]{1,0:T(8,128)(2,1)S(1)} %bitcast.28, bf16[272,1024]{1,0:T(8,128)(2,1)S(1)} %encode.2.after_hbm.refs_0_), custom_call_target="tpu_custom_call" | custom-call | flops 1073741824 | bytes 4194304 | tf_op jit(solution)/shard_map/project_query/pallas_call | solution.py:126
  83.5 6.5 %decode.4.refs_7_ = bf16[512,1024]{1,0:T(8,128)(2,1)} custom-call(s32[4]{0:T(128)S(1)} %pad_add_fusion.3.micro_ref, s32[64]{0:T(128)S(1)} %reshape.23.tgt_ref, bf16[272,1024]{1,0:T(8,128)(2,1)S(1)} %encode.2.after_hbm.refs_0_, bf16[272,1024]{1,0:T(8,128)(2,1)S(1)} %encode.3.refs_1_, bf16[512,1024]{1,0:T(8,128)(2,1)S(1)} %project_query.1.refs_2_, ...), custom_call_target="tpu_custom_call" | custom-call | flops 8589934592 | bytes 8388608 | tf_op jit(solution)/shard_map/decode/pallas_call | solution.py:364
  90.0 1.2 %collective-permute-done.20.refs_1_ = bf16[272,1024]{1,0:T(8,128)(2,1)S(1)} collective-permute-done((bf16[272,1024]{1,0:T(8,128)(2,1)S(1)}, bf16[272,1024]{1,0:T(8,128)(2,1)S(1)}, u32[]{:S(2)}, u32[]{:S(2)}) %collective-permute-start.20) | collective-permute-done | bytes 557088 | tf_op jit(solution)/shard_map/ppermute | solution.py:463
  91.2 3.7 %collective-permute-start.21 = (bf16[272,1024]{1,0:T(8,128)(2,1)S(1)}, bf16[272,1024]{1,0:T(8,128)(2,1)S(1)}, u32[]{:S(2)}, u32[]{:S(2)}) collective-permute-start(bf16[272,1024]{1,0:T(8,128)(2,1)S(1)} %collective-permute-done.20.refs_1_), channel_id=1, source_target_pairs={{0,12},{1,13},{2,14},{3,15},{4,0},{5,1},{6,2},{7,3},{8,4},{9,5},{1... | collective-permute-start | bytes 1671176 | tf_op jit(solution)/shard_map/ppermute | solution.py:463
  94.9 6.5 %decode.5.refs_7_ = bf16[512,1024]{1,0:T(8,128)(2,1)} custom-call(s32[4]{0:T(128)S(1)} %pad_add_fusion.2.micro_ref, s32[64]{0:T(128)S(1)} %reshape.23.tgt_ref, bf16[272,1024]{1,0:T(8,128)(2,1)S(1)} %collective-permute-done.17.refs_0_, bf16[272,1024]{1,0:T(8,128)(2,1)S(1)} %collective-permute-done.23.refs_1_, ...), custom_call_target="tpu_custom_call", output_to_operand_aliasing={{}: (9, {})} | custom-call | flops 8589934592 | bytes 8388608 | tf_op jit(solution)/shard_map/decode/pallas_call | solution.py:364
  101.4 6.5 %decode.6.refs_7_ = bf16[512,1024]{1,0:T(8,128)(2,1)} custom-call(s32[4]{0:T(128)S(1)} %pad_add_fusion.1.micro_ref, s32[64]{0:T(128)S(1)} %reshape.23.tgt_ref, bf16[272,1024]{1,0:T(8,128)(2,1)S(1)} %collective-permute-done.22.refs_0_, bf16[272,1024]{1,0:T(8,128)(2,1)S(1)} %collective-permute-done.20.refs_1_, ...), custom_call_target="tpu_custom_call", output_to_operand_aliasing={{}: (9, {})} | custom-call | flops 8589934592 | bytes 8388608 | tf_op jit(solution)/shard_map/decode/pallas_call | solution.py:364
  107.9 1.6 %collective-permute-done.18.refs_0_ = bf16[272,1024]{1,0:T(8,128)(2,1)S(1)} collective-permute-done((bf16[272,1024]{1,0:T(8,128)(2,1)S(1)}, bf16[272,1024]{1,0:T(8,128)(2,1)S(1)}, u32[]{:S(2)}, u32[]{:S(2)}) %collective-permute-start.18) | collective-permute-done | bytes 557088 | tf_op jit(solution)/shard_map/ppermute | solution.py:463
  109.6 6.5 %decode.7 = bf16[512,1024]{1,0:T(8,128)(2,1)} custom-call(s32[4]{0:T(128)S(1)} %pad_add_fusion.micro_ref, s32[64]{0:T(128)S(1)} %reshape.23.tgt_ref, bf16[272,1024]{1,0:T(8,128)(2,1)S(1)} %collective-permute-done.18.refs_0_, bf16[272,1024]{1,0:T(8,128)(2,1)S(1)} %collective-permute-done.21.refs_1_, ...), custom_call_target="tpu_custom_call", output_to_operand_aliasing={{}: (9, {})} | custom-call | flops 8589934592 | bytes 8388608 | tf_op jit(solution)/shard_map/decode/pallas_call | solution.py:364
  (44 shorter events, 0.1 us)
Async XLA Ops:
  0.0 53.1 %copy-start.10 = (f32[1024]{0:T(1024)S(1)}, f32[1024]{0:T(1024)}, u32[]{:S(2)}) copy-start(f32[1024]{0:T(1024)} %param.19) | copy-start | bytes 12292
  0.0 53.1 %copy-start.11 = (f32[1024]{0:T(1024)S(1)}, f32[1024]{0:T(1024)}, u32[]{:S(2)}) copy-start(f32[1024]{0:T(1024)} %param.22) | copy-start | bytes 12292
  0.0 53.1 %copy-start.9 = (bf16[31,1024]{1,0:T(8,128)(2,1)S(1)}, bf16[31,1024]{1,0:T(8,128)(2,1)}, u32[]{:S(2)}) copy-start(bf16[31,1024]{1,0:T(8,128)(2,1)} %refs_3_.3) | copy-start | bytes 190468
  1.8 51.3 %copy-start.2 = (bf16[64,3072]{1,0:T(8,128)(2,1)S(1)}, bf16[64,3072]{1,0:T(8,128)(2,1)}, u32[]{:S(2)}) copy-start(bf16[64,3072]{1,0:T(8,128)(2,1)} %join_shards.1.refs_5_) | copy-start | bytes 1179652
  1.8 11.3 %collective-permute-start = (bf16[64,3072]{1,0:T(8,128)(2,1)}, bf16[64,3072]{1,0:T(8,128)(2,1)S(1)}, u32[]{:S(2)}, u32[]{:S(2)}) collective-permute-start(bf16[64,3072]{1,0:T(8,128)(2,1)} %join_shards.1.refs_5_), channel_id=1, source_target_pairs={{0,128},{16,144},{32,160},{48,176},{64,192},{80,208},{96,224},{112... | collective-permute-start | bytes 1179656 | tf_op jit(solution)/shard_map/ppermute | solution.py:462
  3.8 15.9 %collective-permute-start.2 = (bf16[64,3072]{1,0:T(8,128)(2,1)}, bf16[64,3072]{1,0:T(8,128)(2,1)S(1)}, u32[]{:S(2)}, u32[]{:S(2)}) collective-permute-start(bf16[64,3072]{1,0:T(8,128)(2,1)} %join_shards.1.refs_5_), channel_id=1, source_target_pairs={{0,32},{16,48},{32,64},{48,80},{64,96},{80,112},{96,0},{112,16},{1... | collective-permute-start | bytes 1179656 | tf_op jit(solution)/shard_map/ppermute | solution.py:462
  4.3 18.4 %collective-permute-start.3 = (bf16[64,3072]{1,0:T(8,128)(2,1)}, bf16[64,3072]{1,0:T(8,128)(2,1)S(1)}, u32[]{:S(2)}, u32[]{:S(2)}) collective-permute-start(bf16[64,3072]{1,0:T(8,128)(2,1)} %join_shards.1.refs_5_), channel_id=1, source_target_pairs={{0,96},{16,112},{32,0},{48,16},{64,32},{80,48},{96,64},{112,80},{1... | collective-permute-start | bytes 1179656 | tf_op jit(solution)/shard_map/ppermute | solution.py:462
  5.8 19.2 %collective-permute-start.8 = (bf16[64,3072]{1,0:T(8,128)(2,1)}, bf16[64,3072]{1,0:T(8,128)(2,1)S(1)}, u32[]{:S(2)}, u32[]{:S(2)}) collective-permute-start(bf16[64,3072]{1,0:T(8,128)(2,1)} %join_shards.1.refs_5_), channel_id=1, source_target_pairs={{0,16},{16,0},{32,48},{48,32},{64,80},{80,64},{96,112},{112,96},{1... | collective-permute-start | bytes 1179656 | tf_op jit(solution)/shard_map/ppermute | solution.py:462
  13.1 22.8 %collective-permute-start.5 = (bf16[64,3072]{1,0:T(8,128)(2,1)S(1)}, bf16[64,3072]{1,0:T(8,128)(2,1)S(1)}, u32[]{:S(2)}, u32[]{:S(2)}) collective-permute-start(bf16[64,3072]{1,0:T(8,128)(2,1)S(1)} %collective-permute-done.own_hbm.value_ref.refs_6_), channel_id=1, source_target_pairs={{0,96},{16,112},{32,0},{48,16},{64,32},{80,48},{96,64},{112,80},{1... | collective-permute-start | bytes 1179656 | tf_op jit(solution)/shard_map/ppermute | solution.py:462
  14.0 1.0 copy-start.3
  14.9 0.7 copy-start.5
  16.4 14.1 %collective-permute-start.1 = (bf16[144,1024]{1,0:T(8,128)(2,1)S(1)}, bf16[144,1024]{1,0:T(8,128)(2,1)S(1)}, u32[]{:S(2)}, u32[]{:S(2)}) collective-permute-start(bf16[144,1024]{1,0:T(8,128)(2,1)S(1)} %pack_frames.1.refs_0_), channel_id=1, source_target_pairs={{0,1},{1,2},{2,3},{3,0},{4,5},{5,6},{6,7},{7,4},{8,9},{9,10},{10,1... | collective-permute-start | bytes 884744 | tf_op jit(solution)/shard_map/ppermute | solution.py:463
  19.7 16.2 %collective-permute-start.9 = (bf16[144,1024]{1,0:T(8,128)(2,1)S(1)}, bf16[144,1024]{1,0:T(8,128)(2,1)S(1)}, u32[]{:S(2)}, u32[]{:S(2)}) collective-permute-start(bf16[144,1024]{1,0:T(8,128)(2,1)S(1)} %pack_frames.1.refs_0_), channel_id=1, source_target_pairs={{0,3},{1,0},{2,1},{3,2},{4,7},{5,4},{6,5},{7,6},{8,11},{9,8},{10,9... | collective-permute-start | bytes 884744 | tf_op jit(solution)/shard_map/ppermute | solution.py:463
  22.7 16.2 %collective-permute-start.4 = (bf16[64,3072]{1,0:T(8,128)(2,1)S(1)}, bf16[64,3072]{1,0:T(8,128)(2,1)}, u32[]{:S(2)}, u32[]{:S(2)}) collective-permute-start(bf16[64,3072]{1,0:T(8,128)(2,1)S(1)} %collective-permute-done.own_hbm.value_ref.refs_6_), channel_id=1, source_target_pairs={{0,32},{16,48},{32,64},{48,80},{64,96},{80,112},{96,0},{112,16},{1... | collective-permute-start | bytes 1179656 | tf_op jit(solution)/shard_map/ppermute | solution.py:462
  25.1 15.5 %collective-permute-start.6 = (bf16[64,3072]{1,0:T(8,128)(2,1)S(1)}, bf16[64,3072]{1,0:T(8,128)(2,1)}, u32[]{:S(2)}, u32[]{:S(2)}) collective-permute-start(bf16[64,3072]{1,0:T(8,128)(2,1)S(1)} %collective-permute-done.2.refs_7_), channel_id=1, source_target_pairs={{0,32},{16,48},{32,64},{48,80},{64,96},{80,112},{96,0},{112,16},{1... | collective-permute-start | bytes 1179656 | tf_op jit(solution)/shard_map/ppermute | solution.py:462
  30.4 10.2 %collective-permute-start.11 = (bf16[64,3072]{1,0:T(8,128)(2,1)S(1)}, bf16[64,3072]{1,0:T(8,128)(2,1)}, u32[]{:S(2)}, u32[]{:S(2)}) collective-permute-start(bf16[64,3072]{1,0:T(8,128)(2,1)S(1)} %collective-permute-done.2.refs_7_), channel_id=1, source_target_pairs={{0,16},{16,0},{32,48},{48,32},{64,80},{80,64},{96,112},{112,96},{1... | collective-permute-start | bytes 1179656 | tf_op jit(solution)/shard_map/ppermute | solution.py:462
  35.9 5.2 %collective-permute-start.12 = (bf16[64,3072]{1,0:T(8,128)(2,1)S(1)}, bf16[64,3072]{1,0:T(8,128)(2,1)}, u32[]{:S(2)}, u32[]{:S(2)}) collective-permute-start(bf16[64,3072]{1,0:T(8,128)(2,1)S(1)} %collective-permute-done.3.refs_8_), channel_id=1, source_target_pairs={{0,16},{16,0},{32,48},{48,32},{64,80},{80,64},{96,112},{112,96},{1... | collective-permute-start | bytes 1179656 | tf_op jit(solution)/shard_map/ppermute | solution.py:462
  35.9 12.8 %collective-permute-start.7 = (bf16[64,3072]{1,0:T(8,128)(2,1)S(1)}, bf16[64,3072]{1,0:T(8,128)(2,1)}, u32[]{:S(2)}, u32[]{:S(2)}) collective-permute-start(bf16[64,3072]{1,0:T(8,128)(2,1)S(1)} %collective-permute-done.5.refs_10_), channel_id=1, source_target_pairs={{0,96},{16,112},{32,0},{48,16},{64,32},{80,48},{96,64},{112,80},{1... | collective-permute-start | bytes 1179656 | tf_op jit(solution)/shard_map/ppermute | solution.py:462
  38.9 10.2 %collective-permute-start.10 = (bf16[64,3072]{1,0:T(8,128)(2,1)S(1)}, bf16[64,3072]{1,0:T(8,128)(2,1)S(1)}, u32[]{:S(2)}, u32[]{:S(2)}) collective-permute-start(bf16[64,3072]{1,0:T(8,128)(2,1)S(1)} %pass_after.1), channel_id=1, source_target_pairs={{0,16},{16,0},{32,48},{48,32},{64,80},{80,64},{96,112},{112,96},{1... | collective-permute-start | bytes 1179656 | tf_op jit(solution)/shard_map/ppermute | solution.py:462
  40.6 12.4 %collective-permute-start.14 = (bf16[64,3072]{1,0:T(8,128)(2,1)S(1)}, bf16[64,3072]{1,0:T(8,128)(2,1)S(1)}, u32[]{:S(2)}, u32[]{:S(2)}) collective-permute-start(bf16[64,3072]{1,0:T(8,128)(2,1)S(1)} %collective-permute-done.5.refs_10_), channel_id=1, source_target_pairs={{0,16},{16,0},{32,48},{48,32},{64,80},{80,64},{96,112},{112,96},{1... | collective-permute-start | bytes 1179656 | tf_op jit(solution)/shard_map/ppermute | solution.py:462
  40.6 12.4 %collective-permute-start.13 = (bf16[64,3072]{1,0:T(8,128)(2,1)}, bf16[64,3072]{1,0:T(8,128)(2,1)S(1)}, u32[]{:S(2)}, u32[]{:S(2)}) collective-permute-start(bf16[64,3072]{1,0:T(8,128)(2,1)} %collective-permute-done.4.refs_9_), channel_id=1, source_target_pairs={{0,16},{16,0},{32,48},{48,32},{64,80},{80,64},{96,112},{112,96},{1... | collective-permute-start | bytes 1179656 | tf_op jit(solution)/shard_map/ppermute | solution.py:462
  41.1 11.9 %collective-permute-start.15 = (bf16[64,3072]{1,0:T(8,128)(2,1)}, bf16[64,3072]{1,0:T(8,128)(2,1)S(1)}, u32[]{:S(2)}, u32[]{:S(2)}) collective-permute-start(bf16[64,3072]{1,0:T(8,128)(2,1)} %collective-permute-done.6.refs_11_), channel_id=1, source_target_pairs={{0,16},{16,0},{32,48},{48,32},{64,80},{80,64},{96,112},{112,96},{1... | collective-permute-start | bytes 1179656 | tf_op jit(solution)/shard_map/ppermute | solution.py:462
  48.8 4.3 %collective-permute-start.16 = (bf16[64,3072]{1,0:T(8,128)(2,1)}, bf16[64,3072]{1,0:T(8,128)(2,1)S(1)}, u32[]{:S(2)}, u32[]{:S(2)}) collective-permute-start(bf16[64,3072]{1,0:T(8,128)(2,1)} %collective-permute-done.7.refs_12_), channel_id=1, source_target_pairs={{0,16},{16,0},{32,48},{48,32},{64,80},{80,64},{96,112},{112,96},{1... | collective-permute-start | bytes 1179656 | tf_op jit(solution)/shard_map/ppermute | solution.py:462
  49.1 17.5 %collective-permute-start.19 = (bf16[144,1024]{1,0:T(8,128)(2,1)S(1)}, bf16[144,1024]{1,0:T(8,128)(2,1)S(1)}, u32[]{:S(2)}, u32[]{:S(2)}) collective-permute-start(bf16[144,1024]{1,0:T(8,128)(2,1)S(1)} %collective-permute-done.1.refs_0_.refs_1_), channel_id=1, source_target_pairs={{0,1},{1,2},{2,3},{3,0},{4,5},{5,6},{6,7},{7,4},{8,9},{9,10},{10,1... | collective-permute-start | bytes 884744 | tf_op jit(solution)/shard_map/ppermute | solution.py:463
  62.4 16.7 %copy-start = (bf16[1,1024,1024]{2,1,0:T(8,128)(2,1)S(1)}, bf16[1,1024,1024]{2,1,0:T(8,128)(2,1)}, u32[]{:S(2)}) copy-start(bf16[1,1024,1024]{2,1,0:T(8,128)(2,1)} %param.25) | copy-start | bytes 6291460
  62.4 16.7 %copy-start.1 = (bf16[1,16,4,8,1024]{4,3,2,1,0:T(8,128)(2,1)S(1)}, bf16[1,16,4,8,1024]{4,3,2,1,0:T(8,128)(2,1)}, u32[]{:S(2)}) copy-start(bf16[1,16,4,8,1024]{4,3,2,1,0:T(8,128)(2,1)} %param.29) | copy-start | bytes 3145732
  62.4 16.7 %copy-start.4 = (f32[1,1024]{1,0:T(1,128)S(1)}, f32[1,1024]{1,0:T(1,128)}, u32[]{:S(2)}) copy-start(f32[1,1024]{1,0:T(1,128)} %gain_ref.1) | copy-start | bytes 12292
  62.4 32.5 %collective-permute-start.17 = (bf16[272,1024]{1,0:T(8,128)(2,1)S(1)}, bf16[272,1024]{1,0:T(8,128)(2,1)S(1)}, u32[]{:S(2)}, u32[]{:S(2)}) collective-permute-start(bf16[272,1024]{1,0:T(8,128)(2,1)S(1)} %encode.2.after_hbm.refs_0_), channel_id=1, source_target_pairs={{0,4},{1,5},{2,6},{3,7},{4,8},{5,9},{6,10},{7,11},{8,12},{9,13},{1... | collective-permute-start | bytes 1671176 | tf_op jit(solution)/shard_map/ppermute | solution.py:463
  64.1 30.8 %collective-permute-start.23 = (bf16[272,1024]{1,0:T(8,128)(2,1)S(1)}, bf16[272,1024]{1,0:T(8,128)(2,1)S(1)}, u32[]{:S(2)}, u32[]{:S(2)}) collective-permute-start(bf16[272,1024]{1,0:T(8,128)(2,1)S(1)} %encode.2.after_hbm.refs_0_), channel_id=1, source_target_pairs={{0,12},{1,13},{2,14},{3,15},{4,0},{5,1},{6,2},{7,3},{8,4},{9,5},{1... | collective-permute-start | bytes 1671176 | tf_op jit(solution)/shard_map/ppermute | solution.py:463
  66.5 16.9 %copy-start.8 = (bf16[1,1024,1024]{2,1,0:T(8,128)(2,1)S(1)}, bf16[1,1024,1024]{2,1,0:T(8,128)(2,1)}, u32[]{:S(2)}) copy-start(bf16[1,1024,1024]{2,1,0:T(8,128)(2,1)} %param.28) | copy-start | bytes 6291460
  76.0 15.2 %collective-permute-start.20 = (bf16[272,1024]{1,0:T(8,128)(2,1)S(1)}, bf16[272,1024]{1,0:T(8,128)(2,1)S(1)}, u32[]{:S(2)}, u32[]{:S(2)}) collective-permute-start(bf16[272,1024]{1,0:T(8,128)(2,1)S(1)} %encode.3.refs_1_), channel_id=1, source_target_pairs={{0,12},{1,13},{2,14},{3,15},{4,0},{5,1},{6,2},{7,3},{8,4},{9,5},{1... | collective-permute-start | bytes 1671176 | tf_op jit(solution)/shard_map/ppermute | solution.py:463
  79.1 22.3 %collective-permute-start.22 = (bf16[272,1024]{1,0:T(8,128)(2,1)S(1)}, bf16[272,1024]{1,0:T(8,128)(2,1)S(1)}, u32[]{:S(2)}, u32[]{:S(2)}) collective-permute-start(bf16[272,1024]{1,0:T(8,128)(2,1)S(1)} %encode.3.refs_1_), channel_id=1, source_target_pairs={{0,4},{1,5},{2,6},{3,7},{4,8},{5,9},{6,10},{7,11},{8,12},{9,13},{1... | collective-permute-start | bytes 1671176 | tf_op jit(solution)/shard_map/ppermute | solution.py:463
  79.1 4.4 %copy-start.6 = (bf16[1,1024,1024]{2,1,0:T(8,128)(2,1)S(1)}, bf16[1,1024,1024]{2,1,0:T(8,128)(2,1)}, u32[]{:S(2)}) copy-start(bf16[1,1024,1024]{2,1,0:T(8,128)(2,1)} %param.26) | copy-start | bytes 6291460
  79.1 4.4 %copy-start.7 = (bf16[1,1024,1024]{2,1,0:T(8,128)(2,1)S(1)}, bf16[1,1024,1024]{2,1,0:T(8,128)(2,1)}, u32[]{:S(2)}) copy-start(bf16[1,1024,1024]{2,1,0:T(8,128)(2,1)} %param.27) | copy-start | bytes 6291460
  91.2 16.7 %collective-permute-start.21 = (bf16[272,1024]{1,0:T(8,128)(2,1)S(1)}, bf16[272,1024]{1,0:T(8,128)(2,1)S(1)}, u32[]{:S(2)}, u32[]{:S(2)}) collective-permute-start(bf16[272,1024]{1,0:T(8,128)(2,1)S(1)} %collective-permute-done.20.refs_1_), channel_id=1, source_target_pairs={{0,12},{1,13},{2,14},{3,15},{4,0},{5,1},{6,2},{7,3},{8,4},{9,5},{1... | collective-permute-start | bytes 1671176 | tf_op jit(solution)/shard_map/ppermute | solution.py:463
  94.9 14.7 %collective-permute-start.18 = (bf16[272,1024]{1,0:T(8,128)(2,1)S(1)}, bf16[272,1024]{1,0:T(8,128)(2,1)S(1)}, u32[]{:S(2)}, u32[]{:S(2)}) collective-permute-start(bf16[272,1024]{1,0:T(8,128)(2,1)S(1)} %collective-permute-done.17.refs_0_), channel_id=1, source_target_pairs={{0,4},{1,5},{2,6},{3,7},{4,8},{5,9},{6,10},{7,11},{8,12},{9,13},{1... | collective-permute-start | bytes 1671176 | tf_op jit(solution)/shard_map/ppermute | solution.py:463

commit v6 on v3

--- a/solution.py
+++ b/solution.py
@@ -464,7 +464,7 @@
     from_b, from_a = along(packed, 0, 1), along(packed, 0, -1)
     source = hidden.reshape(-1, D)
     turn = list(shards)
-    turn[1] = pass_after(turn[1], from_b, from_a)
+    turn[1] = pass_after(turn[1], from_b)
     from_2 = along(from_b, 0, 1)
     shards += [across(v, TO_CORE) for v in turn]
 

time: 115 us -> 115 us (level)
  starting transfers between devices: 29.1 us -> 27.5 us
  waiting for transfers between devices: 32.7 us -> 34.2 us
    ppermute x9, starting transfers between devices: 20.3 us -> 18.7 us  [body(): along = lambda v, dy, dz: lax.ppermute(v, 'section', section_perm(dy, dz))]
    ppermute x9, waiting for transfers between devices: 16.4 us -> 18 us  [body(): along = lambda v, dy, dz: lax.ppermute(v, 'section', section_perm(dy, dz))]
where the time goes in v6:
time: 115 us
  Pallas kernels  48.2 us (42%)
  waiting for transfers between devices  34.2 us (30%)
  starting transfers between devices  27.5 us (24%)
  local copies, waits for them, and re-layouts  4.09 us (4%)
    pallas_call x4, Pallas kernels, decode(): pl.pallas_call(functools.partial(decode_kernel, len(mems), aliased), out_...  24.7 us
    ppermute x9, starting transfers between devices, body(): along = lambda v, dy, dz: lax.ppermute(v, 'section', section_perm(dy, dz))  18.7 us
    ppermute x9, waiting for transfers between devices, body(): along = lambda v, dy, dz: lax.ppermute(v, 'section', section_perm(dy, dz))  18 us
    pallas_call x2, Pallas kernels, encode(): pl.pallas_call(functools.partial(encode_kernel, len(shards)), out_shape=j...  16.6 us
    ppermute x15, waiting for transfers between devices, body(): across = lambda v, perm: lax.ppermute(v, 'dp', perm)  16.3 us
    ppermute x15, starting transfers between devices, body(): across = lambda v, perm: lax.ppermute(v, 'dp', perm)  8.82 us
    pallas_call x1, Pallas kernels, project_query(): pl.pallas_call(query_kernel, out_shape=jax.ShapeDtypeStruct((rows, D), BF...  4.32 us
    unnamed x25, local copies, waits for them, and re-layouts  2.44 us
  transfers between devices with their start and end apart: 24, of which 8 were waited for; matrix products, arithmetic and copies ran while one was open for 2% of the time, Pallas kernels for 35%

profile of v6, /device:TPU:6, one launch (start us, length us, event | category | flops | bytes accessed | tf_op | source)
XLA Modules:
  0.0 114.7 jit_solution(2285622336007997962)
XLA Ops:
  0.0 1.8 %join_shards.1.refs_5_ = bf16[64,3072]{1,0:T(8,128)(2,1)} custom-call(bf16[64,2048]{1,0:T(8,128)(2,1)} %w_in_hbm.1, bf16[64,1024]{1,0:T(8,128)(2,1)} %w_out_hbm.1), custom_call_target="tpu_custom_call" | custom-call | bytes 800000 | tf_op jit(solution)/shard_map/join_shards/pallas_call | solution.py:71
  1.8 2.0 %collective-permute-start = (bf16[64,3072]{1,0:T(8,128)(2,1)}, bf16[64,3072]{1,0:T(8,128)(2,1)S(1)}, u32[]{:S(2)}, u32[]{:S(2)}) collective-permute-start(bf16[64,3072]{1,0:T(8,128)(2,1)} %join_shards.1.refs_5_), channel_id=1, source_target_pairs={{0,128},{16,144},{32,160},{48,176},{64,192},{80,208},{96,224},{112... | collective-permute-start | bytes 1179656 | tf_op jit(solution)/shard_map/ppermute | solution.py:451
  3.8 0.5 collective-permute-start.2
  4.3 1.5 %collective-permute-start.3 = (bf16[64,3072]{1,0:T(8,128)(2,1)}, bf16[64,3072]{1,0:T(8,128)(2,1)S(1)}, u32[]{:S(2)}, u32[]{:S(2)}) collective-permute-start(bf16[64,3072]{1,0:T(8,128)(2,1)} %join_shards.1.refs_5_), channel_id=1, source_target_pairs={{0,96},{16,112},{32,0},{48,16},{64,32},{80,48},{96,64},{112,80},{1... | collective-permute-start | bytes 1179656 | tf_op jit(solution)/shard_map/ppermute | solution.py:451
  5.8 7.3 %collective-permute-done.own_hbm.value_ref.refs_6_ = bf16[64,3072]{1,0:T(8,128)(2,1)S(1)} collective-permute-done((bf16[64,3072]{1,0:T(8,128)(2,1)}, bf16[64,3072]{1,0:T(8,128)(2,1)S(1)}, u32[]{:S(2)}, u32[]{:S(2)}) %collective-permute-start) | collective-permute-done | bytes 393248 | tf_op jit(solution)/shard_map/ppermute | solution.py:451
  13.1 0.8 collective-permute-start.5
  14.0 1.0 copy-done.3
  14.9 0.7 copy-done.5
  15.6 0.8 pack_frames.1.refs_0_
  16.4 3.3 %collective-permute-start.1 = (bf16[144,1024]{1,0:T(8,128)(2,1)S(1)}, bf16[144,1024]{1,0:T(8,128)(2,1)S(1)}, u32[]{:S(2)}, u32[]{:S(2)}) collective-permute-start(bf16[144,1024]{1,0:T(8,128)(2,1)S(1)} %pack_frames.1.refs_0_), channel_id=1, source_target_pairs={{0,1},{1,2},{2,3},{3,0},{4,5},{5,6},{6,7},{7,4},{8,9},{9,10},{10,1... | collective-permute-start | bytes 884744 | tf_op jit(solution)/shard_map/ppermute | solution.py:452
  19.7 2.4 %collective-permute-start.4 = (bf16[64,3072]{1,0:T(8,128)(2,1)S(1)}, bf16[64,3072]{1,0:T(8,128)(2,1)S(1)}, u32[]{:S(2)}, u32[]{:S(2)}) collective-permute-start(bf16[64,3072]{1,0:T(8,128)(2,1)S(1)} %collective-permute-done.own_hbm.value_ref.refs_6_), channel_id=1, source_target_pairs={{0,32},{16,48},{32,64},{48,80},{64,96},{80,112},{96,0},{112,16},{1... | collective-permute-start | bytes 1179656 | tf_op jit(solution)/shard_map/ppermute | solution.py:451
  22.1 0.1 collective-permute-start.6
  22.2 0.0 collective-permute-start.10
  22.2 8.2 %collective-permute-done.1.refs_0_.refs_1_ = bf16[144,1024]{1,0:T(8,128)(2,1)S(1)} collective-permute-done((bf16[144,1024]{1,0:T(8,128)(2,1)S(1)}, bf16[144,1024]{1,0:T(8,128)(2,1)S(1)}, u32[]{:S(2)}, u32[]{:S(2)}) %collective-permute-start.1) | collective-permute-done | bytes 294944 | tf_op jit(solution)/shard_map/ppermute | solution.py:452
  30.4 0.5 collective-permute-start.7
  31.0 0.7 dynamic-slice_reduce_fusion
  31.7 0.1 reshape_squeeze.3
  31.8 0.8 copy.21
  32.5 0.1 reshape.23.tgt_ref
  32.6 0.7 dynamic-slice_bitcast_fusion.where_ref
  33.3 0.1 slice_bitcast_fusion.1
  33.4 0.3 collective-permute-start.9
  33.7 4.1 %collective-permute-done.6.refs_11_ = bf16[64,3072]{1,0:T(8,128)(2,1)} collective-permute-done((bf16[64,3072]{1,0:T(8,128)(2,1)S(1)}, bf16[64,3072]{1,0:T(8,128)(2,1)}, u32[]{:S(2)}, u32[]{:S(2)}) %collective-permute-start.6) | collective-permute-done | bytes 393248 | tf_op jit(solution)/shard_map/ppermute | solution.py:451
  37.9 0.5 collective-permute-start.12
  38.4 0.1 collective-permute-start.14
  38.5 4.8 %collective-permute-done.7.refs_12_ = bf16[64,3072]{1,0:T(8,128)(2,1)} collective-permute-done((bf16[64,3072]{1,0:T(8,128)(2,1)S(1)}, bf16[64,3072]{1,0:T(8,128)(2,1)}, u32[]{:S(2)}, u32[]{:S(2)}) %collective-permute-start.7) | collective-permute-done | bytes 393248 | tf_op jit(solution)/shard_map/ppermute | solution.py:451
  43.3 0.1 pad_add_fusion.3.micro_ref
  43.4 0.1 pad_add_fusion.2.micro_ref
  43.4 0.1 pad_add_fusion.1.micro_ref
  43.5 0.1 pad_add_fusion.micro_ref
  43.6 3.2 %collective-permute-start.18 = (bf16[144,1024]{1,0:T(8,128)(2,1)S(1)}, bf16[144,1024]{1,0:T(8,128)(2,1)S(1)}, u32[]{:S(2)}, u32[]{:S(2)}) collective-permute-start(bf16[144,1024]{1,0:T(8,128)(2,1)S(1)} %pack_frames.1.refs_0_), channel_id=1, source_target_pairs={{0,3},{1,0},{2,1},{3,2},{4,7},{5,4},{6,5},{7,6},{8,11},{9,8},{10,9... | collective-permute-start | bytes 884744 | tf_op jit(solution)/shard_map/ppermute | solution.py:452
  46.8 2.1 %collective-permute-start.19 = (bf16[144,1024]{1,0:T(8,128)(2,1)S(1)}, bf16[144,1024]{1,0:T(8,128)(2,1)S(1)}, u32[]{:S(2)}, u32[]{:S(2)}) collective-permute-start(bf16[144,1024]{1,0:T(8,128)(2,1)S(1)} %collective-permute-done.1.refs_0_.refs_1_), channel_id=1, source_target_pairs={{0,1},{1,2},{2,3},{3,0},{4,5},{5,6},{6,7},{7,4},{8,9},{9,10},{10,1... | collective-permute-start | bytes 884744 | tf_op jit(solution)/shard_map/ppermute | solution.py:452
  48.9 8.2 %encode.2.after_hbm.refs_0_ = bf16[272,1024]{1,0:T(8,128)(2,1)S(1)} custom-call(s32[16]{0:T(128)S(1)} %dynamic-slice_bitcast_fusion.where_ref, bf16[144,1024]{1,0:T(8,128)(2,1)S(1)} %pack_frames.1.refs_0_, bf16[144,1024]{1,0:T(8,128)(2,1)S(1)} %collective-permute-done.1.refs_0_.refs_1_, f32[1,1024]{1,0:T(1,128)S(1)} %bitcast.48, ...), custom_call_target="tpu_custom_call" | custom-call | flops 8000000000 | bytes 8388608 | tf_op jit(solution)/shard_map/encode/pallas_call | solution.py:239
  57.1 0.0 copy-start.4
  57.2 1.7 %collective-permute-start.16 = (bf16[272,1024]{1,0:T(8,128)(2,1)S(1)}, bf16[272,1024]{1,0:T(8,128)(2,1)S(1)}, u32[]{:S(2)}, u32[]{:S(2)}) collective-permute-start(bf16[272,1024]{1,0:T(8,128)(2,1)S(1)} %encode.2.after_hbm.refs_0_), channel_id=1, source_target_pairs={{0,4},{1,5},{2,6},{3,7},{4,8},{5,9},{6,10},{7,11},{8,12},{9,13},{1... | collective-permute-start | bytes 1671176 | tf_op jit(solution)/shard_map/ppermute | solution.py:452
  58.8 1.7 %collective-permute-start.23 = (bf16[272,1024]{1,0:T(8,128)(2,1)S(1)}, bf16[272,1024]{1,0:T(8,128)(2,1)S(1)}, u32[]{:S(2)}, u32[]{:S(2)}) collective-permute-start(bf16[272,1024]{1,0:T(8,128)(2,1)S(1)} %encode.2.after_hbm.refs_0_), channel_id=1, source_target_pairs={{0,12},{1,13},{2,14},{3,15},{4,0},{5,1},{6,2},{7,3},{8,4},{9,5},{1... | collective-permute-start | bytes 1671176 | tf_op jit(solution)/shard_map/ppermute | solution.py:452
  60.5 2.2 %collective-permute-done.18.refs_0_ = bf16[144,1024]{1,0:T(8,128)(2,1)S(1)} collective-permute-done((bf16[144,1024]{1,0:T(8,128)(2,1)S(1)}, bf16[144,1024]{1,0:T(8,128)(2,1)S(1)}, u32[]{:S(2)}, u32[]{:S(2)}) %collective-permute-start.18) | collective-permute-done | bytes 294944 | tf_op jit(solution)/shard_map/ppermute | solution.py:452
  62.6 4.3 %collective-permute-done.19.refs_1_ = bf16[144,1024]{1,0:T(8,128)(2,1)S(1)} collective-permute-done((bf16[144,1024]{1,0:T(8,128)(2,1)S(1)}, bf16[144,1024]{1,0:T(8,128)(2,1)S(1)}, u32[]{:S(2)}, u32[]{:S(2)}) %collective-permute-start.19) | collective-permute-done | bytes 294944 | tf_op jit(solution)/shard_map/ppermute | solution.py:452
  66.9 8.4 %encode.3.refs_1_ = bf16[272,1024]{1,0:T(8,128)(2,1)S(1)} custom-call(s32[16]{0:T(128)S(1)} %dynamic-slice_bitcast_fusion.where_ref, bf16[144,1024]{1,0:T(8,128)(2,1)S(1)} %collective-permute-done.18.refs_0_, bf16[144,1024]{1,0:T(8,128)(2,1)S(1)} %collective-permute-done.19.refs_1_, f32[1,1024]{1,0:T(1,128)S(1)} %bitcast.49, bf16[31,1024]{1,0:T(8,128)(2,1)S(1)} %copy-done.9, ...), custom_call_target="tpu_custom_call" | custom-call | flops 8000000000 | bytes 8388608 | tf_op jit(solution)/shard_map/encode/pallas_call | solution.py:239
  75.3 3.1 %collective-permute-start.20 = (bf16[272,1024]{1,0:T(8,128)(2,1)S(1)}, bf16[272,1024]{1,0:T(8,128)(2,1)S(1)}, u32[]{:S(2)}, u32[]{:S(2)}) collective-permute-start(bf16[272,1024]{1,0:T(8,128)(2,1)S(1)} %encode.3.refs_1_), channel_id=1, source_target_pairs={{0,12},{1,13},{2,14},{3,15},{4,0},{5,1},{6,2},{7,3},{8,4},{9,5},{1... | collective-permute-start | bytes 1671176 | tf_op jit(solution)/shard_map/ppermute | solution.py:452
  78.4 4.3 %project_query.1.refs_2_ = bf16[512,1024]{1,0:T(8,128)(2,1)S(1)} custom-call(bf16[512,1024]{1,0:T(8,128)(2,1)S(1)} %bitcast.29, f32[1,1024]{1,0:T(1,128)S(1)} %copy-done.4, bf16[1024,1024]{1,0:T(8,128)(2,1)S(1)} %bitcast.28, bf16[272,1024]{1,0:T(8,128)(2,1)S(1)} %encode.2.after_hbm.refs_0_), custom_call_target="tpu_custom_call" | custom-call | flops 1073741824 | bytes 4194304 | tf_op jit(solution)/shard_map/project_query/pallas_call | solution.py:126
  82.8 6.2 %decode.4.refs_7_ = bf16[512,1024]{1,0:T(8,128)(2,1)} custom-call(s32[4]{0:T(128)S(1)} %pad_add_fusion.3.micro_ref, s32[64]{0:T(128)S(1)} %reshape.23.tgt_ref, bf16[272,1024]{1,0:T(8,128)(2,1)S(1)} %encode.2.after_hbm.refs_0_, bf16[272,1024]{1,0:T(8,128)(2,1)S(1)} %encode.3.refs_1_, bf16[512,1024]{1,0:T(8,128)(2,1)S(1)} %project_query.1.refs_2_, ...), custom_call_target="tpu_custom_call" | custom-call | flops 8589934592 | bytes 8388608 | tf_op jit(solution)/shard_map/decode/pallas_call | solution.py:353
  89.0 1.3 %collective-permute-done.20.refs_1_ = bf16[272,1024]{1,0:T(8,128)(2,1)S(1)} collective-permute-done((bf16[272,1024]{1,0:T(8,128)(2,1)S(1)}, bf16[272,1024]{1,0:T(8,128)(2,1)S(1)}, u32[]{:S(2)}, u32[]{:S(2)}) %collective-permute-start.20) | collective-permute-done | bytes 557088 | tf_op jit(solution)/shard_map/ppermute | solution.py:452
  90.3 3.7 %collective-permute-start.21 = (bf16[272,1024]{1,0:T(8,128)(2,1)S(1)}, bf16[272,1024]{1,0:T(8,128)(2,1)S(1)}, u32[]{:S(2)}, u32[]{:S(2)}) collective-permute-start(bf16[272,1024]{1,0:T(8,128)(2,1)S(1)} %collective-permute-done.20.refs_1_), channel_id=1, source_target_pairs={{0,12},{1,13},{2,14},{3,15},{4,0},{5,1},{6,2},{7,3},{8,4},{9,5},{1... | collective-permute-start | bytes 1671176 | tf_op jit(solution)/shard_map/ppermute | solution.py:452
  94.0 6.1 %decode.5.refs_7_ = bf16[512,1024]{1,0:T(8,128)(2,1)} custom-call(s32[4]{0:T(128)S(1)} %pad_add_fusion.2.micro_ref, s32[64]{0:T(128)S(1)} %reshape.23.tgt_ref, bf16[272,1024]{1,0:T(8,128)(2,1)S(1)} %collective-permute-done.16.refs_0_, bf16[272,1024]{1,0:T(8,128)(2,1)S(1)} %collective-permute-done.23.refs_1_, ...), custom_call_target="tpu_custom_call", output_to_operand_aliasing={{}: (9, {})} | custom-call | flops 8589934592 | bytes 8388608 | tf_op jit(solution)/shard_map/decode/pallas_call | solution.py:353
  100.1 6.2 %decode.6.refs_7_ = bf16[512,1024]{1,0:T(8,128)(2,1)} custom-call(s32[4]{0:T(128)S(1)} %pad_add_fusion.1.micro_ref, s32[64]{0:T(128)S(1)} %reshape.23.tgt_ref, bf16[272,1024]{1,0:T(8,128)(2,1)S(1)} %collective-permute-done.22.refs_0_, bf16[272,1024]{1,0:T(8,128)(2,1)S(1)} %collective-permute-done.20.refs_1_, ...), custom_call_target="tpu_custom_call", output_to_operand_aliasing={{}: (9, {})} | custom-call | flops 8589934592 | bytes 8388608 | tf_op jit(solution)/shard_map/decode/pallas_call | solution.py:353
  106.3 2.1 %collective-permute-done.17.refs_0_ = bf16[272,1024]{1,0:T(8,128)(2,1)S(1)} collective-permute-done((bf16[272,1024]{1,0:T(8,128)(2,1)S(1)}, bf16[272,1024]{1,0:T(8,128)(2,1)S(1)}, u32[]{:S(2)}, u32[]{:S(2)}) %collective-permute-start.17) | collective-permute-done | bytes 557088 | tf_op jit(solution)/shard_map/ppermute | solution.py:452
  108.4 6.2 %decode.7 = bf16[512,1024]{1,0:T(8,128)(2,1)} custom-call(s32[4]{0:T(128)S(1)} %pad_add_fusion.micro_ref, s32[64]{0:T(128)S(1)} %reshape.23.tgt_ref, bf16[272,1024]{1,0:T(8,128)(2,1)S(1)} %collective-permute-done.17.refs_0_, bf16[272,1024]{1,0:T(8,128)(2,1)S(1)} %collective-permute-done.21.refs_1_, ...), custom_call_target="tpu_custom_call", output_to_operand_aliasing={{}: (9, {})} | custom-call | flops 8589934592 | bytes 8388608 | tf_op jit(solution)/shard_map/decode/pallas_call | solution.py:353
  (44 shorter events, 0.1 us)
Async XLA Ops:
  0.0 48.8 %copy-start.10 = (f32[1024]{0:T(1024)S(1)}, f32[1024]{0:T(1024)}, u32[]{:S(2)}) copy-start(f32[1024]{0:T(1024)} %param.19) | copy-start | bytes 12292
  0.0 48.8 %copy-start.11 = (f32[1024]{0:T(1024)S(1)}, f32[1024]{0:T(1024)}, u32[]{:S(2)}) copy-start(f32[1024]{0:T(1024)} %param.22) | copy-start | bytes 12292
  0.0 48.8 %copy-start.9 = (bf16[31,1024]{1,0:T(8,128)(2,1)S(1)}, bf16[31,1024]{1,0:T(8,128)(2,1)}, u32[]{:S(2)}) copy-start(bf16[31,1024]{1,0:T(8,128)(2,1)} %refs_3_.3) | copy-start | bytes 190468
  1.8 47.1 %copy-start.2 = (bf16[64,3072]{1,0:T(8,128)(2,1)S(1)}, bf16[64,3072]{1,0:T(8,128)(2,1)}, u32[]{:S(2)}) copy-start(bf16[64,3072]{1,0:T(8,128)(2,1)} %join_shards.1.refs_5_) | copy-start | bytes 1179652
  1.8 11.3 %collective-permute-start = (bf16[64,3072]{1,0:T(8,128)(2,1)}, bf16[64,3072]{1,0:T(8,128)(2,1)S(1)}, u32[]{:S(2)}, u32[]{:S(2)}) collective-permute-start(bf16[64,3072]{1,0:T(8,128)(2,1)} %join_shards.1.refs_5_), channel_id=1, source_target_pairs={{0,128},{16,144},{32,160},{48,176},{64,192},{80,208},{96,224},{112... | collective-permute-start | bytes 1179656 | tf_op jit(solution)/shard_map/ppermute | solution.py:451
  3.8 15.9 %collective-permute-start.2 = (bf16[64,3072]{1,0:T(8,128)(2,1)}, bf16[64,3072]{1,0:T(8,128)(2,1)S(1)}, u32[]{:S(2)}, u32[]{:S(2)}) collective-permute-start(bf16[64,3072]{1,0:T(8,128)(2,1)} %join_shards.1.refs_5_), channel_id=1, source_target_pairs={{0,32},{16,48},{32,64},{48,80},{64,96},{80,112},{96,0},{112,16},{1... | collective-permute-start | bytes 1179656 | tf_op jit(solution)/shard_map/ppermute | solution.py:451
  4.3 17.8 %collective-permute-start.3 = (bf16[64,3072]{1,0:T(8,128)(2,1)}, bf16[64,3072]{1,0:T(8,128)(2,1)S(1)}, u32[]{:S(2)}, u32[]{:S(2)}) collective-permute-start(bf16[64,3072]{1,0:T(8,128)(2,1)} %join_shards.1.refs_5_), channel_id=1, source_target_pairs={{0,96},{16,112},{32,0},{48,16},{64,32},{80,48},{96,64},{112,80},{1... | collective-permute-start | bytes 1179656 | tf_op jit(solution)/shard_map/ppermute | solution.py:451
  5.8 16.4 %collective-permute-start.8 = (bf16[64,3072]{1,0:T(8,128)(2,1)}, bf16[64,3072]{1,0:T(8,128)(2,1)S(1)}, u32[]{:S(2)}, u32[]{:S(2)}) collective-permute-start(bf16[64,3072]{1,0:T(8,128)(2,1)} %join_shards.1.refs_5_), channel_id=1, source_target_pairs={{0,16},{16,0},{32,48},{48,32},{64,80},{80,64},{96,112},{112,96},{1... | collective-permute-start | bytes 1179656 | tf_op jit(solution)/shard_map/ppermute | solution.py:451
  13.1 17.3 %collective-permute-start.5 = (bf16[64,3072]{1,0:T(8,128)(2,1)S(1)}, bf16[64,3072]{1,0:T(8,128)(2,1)S(1)}, u32[]{:S(2)}, u32[]{:S(2)}) collective-permute-start(bf16[64,3072]{1,0:T(8,128)(2,1)S(1)} %collective-permute-done.own_hbm.value_ref.refs_6_), channel_id=1, source_target_pairs={{0,96},{16,112},{32,0},{48,16},{64,32},{80,48},{96,64},{112,80},{1... | collective-permute-start | bytes 1179656 | tf_op jit(solution)/shard_map/ppermute | solution.py:451
  14.0 1.0 copy-start.3
  14.9 0.7 copy-start.5
  16.4 14.1 %collective-permute-start.1 = (bf16[144,1024]{1,0:T(8,128)(2,1)S(1)}, bf16[144,1024]{1,0:T(8,128)(2,1)S(1)}, u32[]{:S(2)}, u32[]{:S(2)}) collective-permute-start(bf16[144,1024]{1,0:T(8,128)(2,1)S(1)} %pack_frames.1.refs_0_), channel_id=1, source_target_pairs={{0,1},{1,2},{2,3},{3,0},{4,5},{5,6},{6,7},{7,4},{8,9},{9,10},{10,1... | collective-permute-start | bytes 884744 | tf_op jit(solution)/shard_map/ppermute | solution.py:452
  19.7 13.7 %collective-permute-start.4 = (bf16[64,3072]{1,0:T(8,128)(2,1)S(1)}, bf16[64,3072]{1,0:T(8,128)(2,1)S(1)}, u32[]{:S(2)}, u32[]{:S(2)}) collective-permute-start(bf16[64,3072]{1,0:T(8,128)(2,1)S(1)} %collective-permute-done.own_hbm.value_ref.refs_6_), channel_id=1, source_target_pairs={{0,32},{16,48},{32,64},{48,80},{64,96},{80,112},{96,0},{112,16},{1... | collective-permute-start | bytes 1179656 | tf_op jit(solution)/shard_map/ppermute | solution.py:451
  22.1 15.7 %collective-permute-start.6 = (bf16[64,3072]{1,0:T(8,128)(2,1)S(1)}, bf16[64,3072]{1,0:T(8,128)(2,1)}, u32[]{:S(2)}, u32[]{:S(2)}) collective-permute-start(bf16[64,3072]{1,0:T(8,128)(2,1)S(1)} %collective-permute-done.2.refs_7_), channel_id=1, source_target_pairs={{0,32},{16,48},{32,64},{48,80},{64,96},{80,112},{96,0},{112,16},{1... | collective-permute-start | bytes 1179656 | tf_op jit(solution)/shard_map/ppermute | solution.py:451
  22.2 15.7 %collective-permute-start.10 = (bf16[64,3072]{1,0:T(8,128)(2,1)S(1)}, bf16[64,3072]{1,0:T(8,128)(2,1)}, u32[]{:S(2)}, u32[]{:S(2)}) collective-permute-start(bf16[64,3072]{1,0:T(8,128)(2,1)S(1)} %collective-permute-done.2.refs_7_), channel_id=1, source_target_pairs={{0,16},{16,0},{32,48},{48,32},{64,80},{80,64},{96,112},{112,96},{1... | collective-permute-start | bytes 1179656 | tf_op jit(solution)/shard_map/ppermute | solution.py:451
  30.4 7.9 %collective-permute-start.11 = (bf16[64,3072]{1,0:T(8,128)(2,1)S(1)}, bf16[64,3072]{1,0:T(8,128)(2,1)}, u32[]{:S(2)}, u32[]{:S(2)}) collective-permute-start(bf16[64,3072]{1,0:T(8,128)(2,1)S(1)} %collective-permute-done.3.refs_8_), channel_id=1, source_target_pairs={{0,16},{16,0},{32,48},{48,32},{64,80},{80,64},{96,112},{112,96},{1... | collective-permute-start | bytes 1179656 | tf_op jit(solution)/shard_map/ppermute | solution.py:451
  30.4 12.8 %collective-permute-start.7 = (bf16[64,3072]{1,0:T(8,128)(2,1)S(1)}, bf16[64,3072]{1,0:T(8,128)(2,1)}, u32[]{:S(2)}, u32[]{:S(2)}) collective-permute-start(bf16[64,3072]{1,0:T(8,128)(2,1)S(1)} %collective-permute-done.5.refs_10_), channel_id=1, source_target_pairs={{0,96},{16,112},{32,0},{48,16},{64,32},{80,48},{96,64},{112,80},{1... | collective-permute-start | bytes 1179656 | tf_op jit(solution)/shard_map/ppermute | solution.py:451
  33.4 10.2 %collective-permute-start.9 = (bf16[64,3072]{1,0:T(8,128)(2,1)S(1)}, bf16[64,3072]{1,0:T(8,128)(2,1)S(1)}, u32[]{:S(2)}, u32[]{:S(2)}) collective-permute-start(bf16[64,3072]{1,0:T(8,128)(2,1)S(1)} %pass_after.1), channel_id=1, source_target_pairs={{0,16},{16,0},{32,48},{48,32},{64,80},{80,64},{96,112},{112,96},{1... | collective-permute-start | bytes 1179656 | tf_op jit(solution)/shard_map/ppermute | solution.py:451
  37.9 8.9 %collective-permute-start.13 = (bf16[64,3072]{1,0:T(8,128)(2,1)S(1)}, bf16[64,3072]{1,0:T(8,128)(2,1)S(1)}, u32[]{:S(2)}, u32[]{:S(2)}) collective-permute-start(bf16[64,3072]{1,0:T(8,128)(2,1)S(1)} %collective-permute-done.5.refs_10_), channel_id=1, source_target_pairs={{0,16},{16,0},{32,48},{48,32},{64,80},{80,64},{96,112},{112,96},{1... | collective-permute-start | bytes 1179656 | tf_op jit(solution)/shard_map/ppermute | solution.py:451
  37.9 10.9 %collective-permute-start.12 = (bf16[64,3072]{1,0:T(8,128)(2,1)S(1)}, bf16[64,3072]{1,0:T(8,128)(2,1)S(1)}, u32[]{:S(2)}, u32[]{:S(2)}) collective-permute-start(bf16[64,3072]{1,0:T(8,128)(2,1)S(1)} %collective-permute-done.4.refs_9_), channel_id=1, source_target_pairs={{0,16},{16,0},{32,48},{48,32},{64,80},{80,64},{96,112},{112,96},{1... | collective-permute-start | bytes 1179656 | tf_op jit(solution)/shard_map/ppermute | solution.py:451
  38.4 10.4 %collective-permute-start.14 = (bf16[64,3072]{1,0:T(8,128)(2,1)}, bf16[64,3072]{1,0:T(8,128)(2,1)S(1)}, u32[]{:S(2)}, u32[]{:S(2)}) collective-permute-start(bf16[64,3072]{1,0:T(8,128)(2,1)} %collective-permute-done.6.refs_11_), channel_id=1, source_target_pairs={{0,16},{16,0},{32,48},{48,32},{64,80},{80,64},{96,112},{112,96},{1... | collective-permute-start | bytes 1179656 | tf_op jit(solution)/shard_map/ppermute | solution.py:451
  43.3 5.5 %collective-permute-start.15 = (bf16[64,3072]{1,0:T(8,128)(2,1)}, bf16[64,3072]{1,0:T(8,128)(2,1)S(1)}, u32[]{:S(2)}, u32[]{:S(2)}) collective-permute-start(bf16[64,3072]{1,0:T(8,128)(2,1)} %collective-permute-done.7.refs_12_), channel_id=1, source_target_pairs={{0,16},{16,0},{32,48},{48,32},{64,80},{80,64},{96,112},{112,96},{1... | collective-permute-start | bytes 1179656 | tf_op jit(solution)/shard_map/ppermute | solution.py:451
  43.6 19.0 %collective-permute-start.18 = (bf16[144,1024]{1,0:T(8,128)(2,1)S(1)}, bf16[144,1024]{1,0:T(8,128)(2,1)S(1)}, u32[]{:S(2)}, u32[]{:S(2)}) collective-permute-start(bf16[144,1024]{1,0:T(8,128)(2,1)S(1)} %pack_frames.1.refs_0_), channel_id=1, source_target_pairs={{0,3},{1,0},{2,1},{3,2},{4,7},{5,4},{6,5},{7,6},{8,11},{9,8},{10,9... | collective-permute-start | bytes 884744 | tf_op jit(solution)/shard_map/ppermute | solution.py:452
  46.8 20.1 %collective-permute-start.19 = (bf16[144,1024]{1,0:T(8,128)(2,1)S(1)}, bf16[144,1024]{1,0:T(8,128)(2,1)S(1)}, u32[]{:S(2)}, u32[]{:S(2)}) collective-permute-start(bf16[144,1024]{1,0:T(8,128)(2,1)S(1)} %collective-permute-done.1.refs_0_.refs_1_), channel_id=1, source_target_pairs={{0,1},{1,2},{2,3},{3,0},{4,5},{5,6},{6,7},{7,4},{8,9},{9,10},{10,1... | collective-permute-start | bytes 884744 | tf_op jit(solution)/shard_map/ppermute | solution.py:452
  57.1 21.3 %copy-start = (bf16[1,1024,1024]{2,1,0:T(8,128)(2,1)S(1)}, bf16[1,1024,1024]{2,1,0:T(8,128)(2,1)}, u32[]{:S(2)}) copy-start(bf16[1,1024,1024]{2,1,0:T(8,128)(2,1)} %param.25) | copy-start | bytes 6291460
  57.1 21.2 %copy-start.1 = (bf16[1,16,4,8,1024]{4,3,2,1,0:T(8,128)(2,1)S(1)}, bf16[1,16,4,8,1024]{4,3,2,1,0:T(8,128)(2,1)}, u32[]{:S(2)}) copy-start(bf16[1,16,4,8,1024]{4,3,2,1,0:T(8,128)(2,1)} %param.29) | copy-start | bytes 3145732
  57.1 21.2 %copy-start.4 = (f32[1,1024]{1,0:T(1,128)S(1)}, f32[1,1024]{1,0:T(1,128)}, u32[]{:S(2)}) copy-start(f32[1,1024]{1,0:T(1,128)} %gain_ref.1) | copy-start | bytes 12292
  57.2 36.8 %collective-permute-start.16 = (bf16[272,1024]{1,0:T(8,128)(2,1)S(1)}, bf16[272,1024]{1,0:T(8,128)(2,1)S(1)}, u32[]{:S(2)}, u32[]{:S(2)}) collective-permute-start(bf16[272,1024]{1,0:T(8,128)(2,1)S(1)} %encode.2.after_hbm.refs_0_), channel_id=1, source_target_pairs={{0,4},{1,5},{2,6},{3,7},{4,8},{5,9},{6,10},{7,11},{8,12},{9,13},{1... | collective-permute-start | bytes 1671176 | tf_op jit(solution)/shard_map/ppermute | solution.py:452
  58.8 35.1 %collective-permute-start.23 = (bf16[272,1024]{1,0:T(8,128)(2,1)S(1)}, bf16[272,1024]{1,0:T(8,128)(2,1)S(1)}, u32[]{:S(2)}, u32[]{:S(2)}) collective-permute-start(bf16[272,1024]{1,0:T(8,128)(2,1)S(1)} %encode.2.after_hbm.refs_0_), channel_id=1, source_target_pairs={{0,12},{1,13},{2,14},{3,15},{4,0},{5,1},{6,2},{7,3},{8,4},{9,5},{1... | collective-permute-start | bytes 1671176 | tf_op jit(solution)/shard_map/ppermute | solution.py:452
  66.9 15.9 %copy-start.8 = (bf16[1,1024,1024]{2,1,0:T(8,128)(2,1)S(1)}, bf16[1,1024,1024]{2,1,0:T(8,128)(2,1)}, u32[]{:S(2)}) copy-start(bf16[1,1024,1024]{2,1,0:T(8,128)(2,1)} %param.28) | copy-start | bytes 6291460
  75.3 15.0 %collective-permute-start.20 = (bf16[272,1024]{1,0:T(8,128)(2,1)S(1)}, bf16[272,1024]{1,0:T(8,128)(2,1)S(1)}, u32[]{:S(2)}, u32[]{:S(2)}) collective-permute-start(bf16[272,1024]{1,0:T(8,128)(2,1)S(1)} %encode.3.refs_1_), channel_id=1, source_target_pairs={{0,12},{1,13},{2,14},{3,15},{4,0},{5,1},{6,2},{7,3},{8,4},{9,5},{1... | collective-permute-start | bytes 1671176 | tf_op jit(solution)/shard_map/ppermute | solution.py:452
  78.4 21.7 %collective-permute-start.22 = (bf16[272,1024]{1,0:T(8,128)(2,1)S(1)}, bf16[272,1024]{1,0:T(8,128)(2,1)S(1)}, u32[]{:S(2)}, u32[]{:S(2)}) collective-permute-start(bf16[272,1024]{1,0:T(8,128)(2,1)S(1)} %encode.3.refs_1_), channel_id=1, source_target_pairs={{0,4},{1,5},{2,6},{3,7},{4,8},{5,9},{6,10},{7,11},{8,12},{9,13},{1... | collective-permute-start | bytes 1671176 | tf_op jit(solution)/shard_map/ppermute | solution.py:452
  78.4 4.4 %copy-start.6 = (bf16[1,1024,1024]{2,1,0:T(8,128)(2,1)S(1)}, bf16[1,1024,1024]{2,1,0:T(8,128)(2,1)}, u32[]{:S(2)}) copy-start(bf16[1,1024,1024]{2,1,0:T(8,128)(2,1)} %param.26) | copy-start | bytes 6291460
  78.4 4.4 %copy-start.7 = (bf16[1,1024,1024]{2,1,0:T(8,128)(2,1)S(1)}, bf16[1,1024,1024]{2,1,0:T(8,128)(2,1)}, u32[]{:S(2)}) copy-start(bf16[1,1024,1024]{2,1,0:T(8,128)(2,1)} %param.27) | copy-start | bytes 6291460
  90.3 16.1 %collective-permute-start.21 = (bf16[272,1024]{1,0:T(8,128)(2,1)S(1)}, bf16[272,1024]{1,0:T(8,128)(2,1)S(1)}, u32[]{:S(2)}, u32[]{:S(2)}) collective-permute-start(bf16[272,1024]{1,0:T(8,128)(2,1)S(1)} %collective-permute-done.20.refs_1_), channel_id=1, source_target_pairs={{0,12},{1,13},{2,14},{3,15},{4,0},{5,1},{6,2},{7,3},{8,4},{9,5},{1... | collective-permute-start | bytes 1671176 | tf_op jit(solution)/shard_map/ppermute | solution.py:452
  93.9 14.4 %collective-permute-start.17 = (bf16[272,1024]{1,0:T(8,128)(2,1)S(1)}, bf16[272,1024]{1,0:T(8,128)(2,1)S(1)}, u32[]{:S(2)}, u32[]{:S(2)}) collective-permute-start(bf16[272,1024]{1,0:T(8,128)(2,1)S(1)} %collective-permute-done.16.refs_0_), channel_id=1, source_target_pairs={{0,4},{1,5},{2,6},{3,7},{4,8},{5,9},{6,10},{7,11},{8,12},{9,13},{1... | collective-permute-start | bytes 1671176 | tf_op jit(solution)/shard_map/ppermute | solution.py:452
